TPU v7x, 256 devices: a whole 4x4x8 slice. The times are simulated.
256 devices in a mesh: bevy: 16 (over y, x), bevx: 8 (over z), cam: 2 (over core).
Axes of the slice: x: 4, y: 4, z: 8, core: 2. Of those that a mesh axis runs over, the one named last changes fastest.
Arguments:
- image_tokens: bfloat16 [65536, 768], P(('bevy', 'bevx', 'cam')), may hold values from -6 to 6
- lift_weight: bfloat16 [768, 1024], replicated, may hold values from -0.21875 to 0.21875
- route_token: int32 [128, 2, 128, 8], P(('bevy', 'bevx'), 'cam'), may hold values from 0 to 255
- route_cell: int32 [128, 2, 128, 8], P(None, 'cam', ('bevy', 'bevx')), may hold values from 0 to 1023
- slot_counts: int32 [128, 2, 128], P(('bevy', 'bevx'), 'cam'), may hold values from 0 to 8, as said below
- norm_gain: float32 [1024], replicated, may hold values from 0.1 to 1.9
- w_query: bfloat16 [1024, 1024], replicated, may hold values from -0.1875 to 0.1875
- w_key: bfloat16 [1024, 1024], replicated, may hold values from -0.1875 to 0.1875
- w_value: bfloat16 [1024, 1024], replicated, may hold values from -0.1875 to 0.1875
- w_out: bfloat16 [1024, 1024], replicated, may hold values from -0.1875 to 0.1875
- key_bias: bfloat16 [256, 512, 16], P(None, 'bevx'), may hold values from -1.5 to 260
Outputs:
- bev_out: bfloat16 [256, 512, 1024], P(('bevy', 'cam'), 'bevx')
Inputs may be any that keep to these rules, and one draw needn't show every extreme that they name: The first slot_counts slots of a source device and tile are live; at most 8. In every draw some tile receives 8 live slots from every source device.
All inputs are finite; a program needn't handle non-finite values.
Results may differ from a plain program's by a relative error of at most 0.0055.
Values may be sent and summed in bfloat16 or wider, within the bound.
No kernel may reach another device: no remote copies, remote signals or barrier semaphores. Data moves between devices by JAX's collectives and lax.ppermute only.
A program may use at most 128 MiB of HBM per device.

v0:
```python
import jax
import jax.numpy as jnp
from jax import lax
from jax.sharding import PartitionSpec as P

ROWS_DEV = 8
COLS_DEV = 64
HALO = 4


def cut_along(value, dim, length):
    before, after = (value.shape[:dim], value.shape[dim + 1 :])
    return jnp.moveaxis(value.reshape(*before, length, -1, *after), dim, 0)


def sum_at_owner(value, axis, dim):
    blocks = cut_along(value, dim, lax.axis_size(axis))
    arrived = lax.all_to_all(blocks, axis, split_axis=0, concat_axis=0, tiled=True)
    return arrived.sum(axis=0)


def with_halo(value, sides, width):
    edges = {}
    for axis, dim in sides:
        size, length = (lax.axis_size(axis), value.shape[dim])
        up = [(i, (i + 1) % size) for i in range(size - 1)]
        last = lax.slice_in_dim(value, length - width, length, axis=dim)
        initial = lax.slice_in_dim(value, 0, width, axis=dim)
        edges[dim] = (
            lax.ppermute(last, axis, up),
            lax.ppermute(initial, axis, [(b, a) for a, b in up]),
        )
    done = []
    for _, dim in sides:
        low, high = edges[dim]
        around = [(width, width) if d in done else (0, 0) for d in range(value.ndim)]
        value = jnp.concatenate([jnp.pad(low, around), value, jnp.pad(high, around)], axis=dim)
        done.append(dim)
    return value


def body(
    image_tokens,
    lift_weight,
    route_token,
    route_cell,
    slot_counts,
    norm_gain,
    w_query,
    w_key,
    w_value,
    w_out,
    key_bias,
):
    tile_count = route_token.shape[2]
    slot_count = route_token.shape[3]
    width_out = lift_weight.shape[1]
    head_count = key_bias.shape[2]
    head_size = width_out // head_count
    grid_rows = key_bias.shape[0]
    own_cells = ROWS_DEV * COLS_DEV
    is_live = (
        lax.broadcasted_iota(jnp.int32, (tile_count, slot_count), 1) < slot_counts[0, 0][:, None]
    )
    token_index = route_token[0, 0]
    picked = jnp.where(is_live[:, :, None], image_tokens[token_index], jnp.zeros((), jnp.bfloat16))
    arrived = lax.all_to_all(picked, ("bevy", "bevx"), split_axis=0, concat_axis=0, tiled=True)
    arrived_rows = arrived.reshape(tile_count * slot_count, -1)
    arrived_rows = jnp.dot(arrived_rows, lift_weight, preferred_element_type=jnp.float32).astype(
        jnp.bfloat16
    )
    cell_index = route_cell[:, 0, 0, :].reshape(-1)
    cell_ids = lax.broadcasted_iota(
        jnp.int32, (own_cells * lax.axis_size("cam"), tile_count * slot_count), 0
    )
    one_hot = (cell_ids == cell_index[None, :]).astype(jnp.bfloat16)
    lifted = sum_at_owner(
        jnp.dot(one_hot, arrived_rows, preferred_element_type=jnp.float32), "cam", 0
    )
    mean_square = jnp.mean(lifted * lifted, axis=-1, keepdims=True)
    normed = (lifted * lax.rsqrt(mean_square + 1e-06) * norm_gain).astype(jnp.bfloat16)
    queries = jnp.dot(normed, w_query, preferred_element_type=jnp.float32).astype(jnp.bfloat16)
    row_start = lax.axis_index(("bevy", "cam")) * ROWS_DEV
    key_local = jnp.dot(normed, w_key, preferred_element_type=jnp.float32).astype(jnp.bfloat16)
    value_local = jnp.dot(normed, w_value, preferred_element_type=jnp.float32).astype(jnp.bfloat16)
    stacked = jnp.concatenate([key_local, value_local], axis=-1).reshape(
        ROWS_DEV, COLS_DEV, 2 * width_out
    )
    extended = with_halo(stacked, ((("bevy", "cam"), 0),), HALO).reshape(-1, 2 * width_out)
    key_vectors = extended[:, :width_out]
    value_vectors = extended[:, width_out:]
    bias_padded = jnp.pad(key_bias, ((HALO, HALO), (0, 0), (0, 0)))
    bias_rows = (
        lax.dynamic_slice_in_dim(bias_padded, row_start, 2 * ROWS_DEV, 0)
        .reshape(-1, head_count)
        .astype(jnp.float32)
    )
    key_row = row_start - HALO + jnp.arange(2 * ROWS_DEV, dtype=jnp.int32)
    key_valid = jnp.repeat((key_row >= 0) & (key_row < grid_rows), COLS_DEV)
    query_heads = queries.reshape(own_cells, head_count, head_size)
    key_heads = key_vectors.reshape(-1, head_count, head_size)
    value_heads = value_vectors.reshape(-1, head_count, head_size)
    score_scale = head_size ** (-0.5)
    scores = (
        jnp.einsum("qhd,khd->hqk", query_heads, key_heads, preferred_element_type=jnp.float32)
        * score_scale
    )
    scores = scores + bias_rows.T[:, None, :]
    scores = jnp.where(key_valid[None, None, :], scores, -jnp.inf)
    top_score = jnp.max(scores, axis=-1, keepdims=True)
    expo = jnp.exp(scores - top_score)
    weights = (expo / jnp.sum(expo, axis=-1, keepdims=True)).astype(jnp.bfloat16)
    attended = jnp.einsum(
        "hqk,khd->qhd", weights, value_heads, preferred_element_type=jnp.float32
    ).astype(jnp.bfloat16)
    attended = attended.reshape(own_cells, width_out)
    result = lifted + jnp.dot(attended, w_out, preferred_element_type=jnp.float32)
    return result.astype(jnp.bfloat16).reshape(ROWS_DEV, COLS_DEV, width_out)


def solution(mesh):
    placed = (
        P(("bevy", "bevx", "cam"), None),
        P(),
        P(("bevy", "bevx"), "cam", None, None),
        P(None, "cam", ("bevy", "bevx"), None),
        P(("bevy", "bevx"), "cam", None),
        P(),
        P(),
        P(),
        P(),
        P(),
        P(None, "bevx", None),
    )
    return jax.shard_map(
        body,
        mesh=mesh,
        in_specs=placed,
        out_specs=P(("bevy", "cam"), "bevx", None),
        check_vma=False,
    )
```

profile of v0, /device:TPU:8, one launch (start us, length us, event | category | flops | bytes accessed | tf_op | source)
XLA Modules:
  0.0 166.5 jit_solution(11167670220698099931)
XLA Ops:
  0.0 0.0 copy-start
  0.0 0.8 compare_select_fusion
  0.8 0.7 iota_compare_fusion.2
  1.6 0.1 copy.22
  1.7 0.1 reshape.108
  1.8 6.7 %gather_fusion = bf16[1024,768]{1,0:T(8,128)(2,1)} fusion(bf16[256,768]{1,0:T(8,128)(2,1)} %param.11, s32[1024]{0:T(1024)S(1)} %broadcast_clamp_fusion), kind=kCustom, calls=%fused_computation | custom fusion | bytes 3149824 | tf_op jit(solution)/shard_map/gather | solution.py:66
  8.5 2.8 %bitcast_select_fusion = bf16[128,8,768]{2,1,0:T(8,128)(2,1)} fusion(bf16[1024,768]{1,0:T(8,128)(2,1)} %gather_fusion, pred[128,8]{1,0:T(8,128)(4,1)S(1)} %iota_compare_fusion.2), kind=kLoop, calls=%fused_computation.26 | loop fusion | flops 786432 | bytes 3146752 | tf_op jit(solution)/shard_map/jit(_where)/select_n | solution.py:66
  11.2 16.0 %all-to-all-start = ((bf16[128,8,768]{2,1,0:T(8,128)(2,1)}), bf16[128,8,768]{2,1,0:T(8,128)(2,1)}, u32[]{:S(2)}, u32[]{:S(2)}) async-start(bf16[128,8,768]{2,1,0:T(8,128)(2,1)} %bitcast_select_fusion), calls=%async_computation | async-start | bytes 3145728 | tf_op jit(solution)/shard_map/all_to_all | solution.py:67
  27.2 0.0 copy-done.9
  27.2 0.1 copy.21
  27.3 0.1 eq.10
  27.4 40.1 %all-to-all-done = bf16[128,8,768]{2,1,0:T(8,128)(2,1)} async-done(((bf16[128,8,768]{2,1,0:T(8,128)(2,1)}), bf16[128,8,768]{2,1,0:T(8,128)(2,1)}, u32[]{:S(2)}, u32[]{:S(2)}) %all-to-all-start) | async-done | bytes 1572896 | tf_op jit(solution)/shard_map/all_to_all | solution.py:67
  67.5 7.8 %fusion.7 = f32[1024,1024]{1,0:T(8,128)} fusion(s32[1024]{0:T(1024)S(1)} %eq.10, bf16[768,1024]{1,0:T(8,128)(2,1)} %param.12, bf16[128,8,768]{2,1,0:T(8,128)(2,1)} %all-to-all-done), kind=kOutput, calls=%fused_computation.13 | convolution fusion | flops 3760193536 | bytes 7344128 | tf_op jit(solution)/shard_map/dot_general | solution.py:78
  75.3 11.8 %all_to_all.10 = f32[2,512,1024]{2,1,0:T(8,128)} all-to-all(f32[2,512,1024]{2,1,0:T(8,128)} %bitcast.49), channel_id=1, replica_groups=mesh['bevy'=16,'bevx'=8,'cam'=2] {'cam'}, dimensions={0} | all-to-all | bytes 8388608 | tf_op jit(solution)/shard_map/all_to_all | solution.py:18
  87.2 4.1 %reduce_sum.27 = f32[512,1024]{1,0:T(8,128)} reduce(f32[2,512,1024]{2,1,0:T(8,128)} %all_to_all.10, f32[]{:T(128)} %constant.6.clone.1), dimensions={0}, to_apply=%region_0.1 | reduce | flops 524288 | bytes 6291460 | tf_op jit(solution)/shard_map/reduce_sum | solution.py:19
  91.3 2.0 %multiply_reduce_fusion = f32[512]{0:T(512)S(1)} fusion(f32[512,1024]{1,0:T(8,128)} %reduce_sum.27), kind=kLoop, calls=%fused_computation.21 | loop fusion | flops 1048064 | bytes 2099200 | tf_op jit(solution)/shard_map/reduce_sum | solution.py:80
  93.2 0.3 copy-done.2
  93.5 0.0 copy-done.8
  93.5 0.2 multiply_convert_fusion
  93.8 0.0 copy-start.10
  93.8 1.3 convolution_convert_fusion.1
  95.1 0.0 copy-done.5
  95.1 0.7 copy-done.10
  95.7 1.3 convolution_convert_fusion.2
  97.0 0.0 copy-start.3
  97.0 1.7 fusion.17
  98.7 3.3 %collective-permute-start.1 = (bf16[4,64,2048]{2,1,0:T(8,128)(2,1)}, bf16[4,64,2048]{2,1,0:T(8,128)(2,1)}, u32[]{:S(2)}, u32[]{:S(2)}) collective-permute-start(bf16[4,64,2048]{2,1,0:T(8,128)(2,1)} %bitcast.7), channel_id=1, source_target_pairs={{1,0},{16,1},{17,16},{32,17},{33,32},{48,33},{49,48},{64,49},{65,6... | collective-permute-start | bytes 3145736 | tf_op jit(solution)/shard_map/ppermute | solution.py:31
  102.0 2.1 %collective-permute-start = (bf16[4,64,2048]{2,1,0:T(8,128)(2,1)}, bf16[4,64,2048]{2,1,0:T(8,128)(2,1)}, u32[]{:S(2)}, u32[]{:S(2)}) collective-permute-start(bf16[4,64,2048]{2,1,0:T(8,128)(2,1)} %bitcast.5), channel_id=1, source_target_pairs={{0,1},{1,16},{16,17},{17,32},{32,33},{33,48},{48,49},{49,64},{64,6... | collective-permute-start | bytes 3145736 | tf_op jit(solution)/shard_map/ppermute | solution.py:30
  104.1 0.1 broadcast_in_dim.38
  104.2 0.1 broadcast_in_dim.39
  104.3 2.6 %copy.26 = bf16[256,64,16]{1,2,0:T(8,128)(2,1)S(1)} copy(bf16[256,64,16]{0,2,1:T(8,128)(2,1)} %param.21) | data formatting | bytes 1048576 | tf_op args[10]
  106.9 0.1 fusion.19
  107.1 0.1 reshape.105
  107.2 2.8 %convolution_convert_fusion = bf16[512,1024]{1,0:T(8,128)(2,1)S(1)} fusion(bf16[512,1024]{1,0:T(8,128)(2,1)S(1)} %copy-done.6, bf16[1024,1024]{1,0:T(8,128)(2,1)} %param.17), kind=kOutput, calls=%fused_computation.27 | convolution fusion | flops 1074266112 | bytes 4194304 | tf_op jit(solution)/shard_map/dot_general | solution.py:82
  110.0 1.3 copy.24
  111.3 1.4 pad_maximum_fusion.1
  112.8 1.9 %collective-permute-done.1 = bf16[4,64,2048]{2,1,0:T(8,128)(2,1)} collective-permute-done((bf16[4,64,2048]{2,1,0:T(8,128)(2,1)}, bf16[4,64,2048]{2,1,0:T(8,128)(2,1)}, u32[]{:S(2)}, u32[]{:S(2)}) %collective-permute-start.1) | collective-permute-done | bytes 1048608 | tf_op jit(solution)/shard_map/ppermute | solution.py:31
  114.6 5.9 %collective-permute-done = bf16[4,64,2048]{2,1,0:T(8,128)(2,1)} collective-permute-done((bf16[4,64,2048]{2,1,0:T(8,128)(2,1)}, bf16[4,64,2048]{2,1,0:T(8,128)(2,1)}, u32[]{:S(2)}, u32[]{:S(2)}) %collective-permute-start) | collective-permute-done | bytes 1048608 | tf_op jit(solution)/shard_map/ppermute | solution.py:30
  120.5 1.8 %pad_maximum_fusion = bf16[16,64,2048]{2,1,0:T(8,128)(2,1)S(1)} fusion(bf16[4,64,2048]{2,1,0:T(8,128)(2,1)} %collective-permute-done.1, bf16[8,64,2048]{2,1,0:T(8,128)(2,1)S(1)} %bitcast.48, bf16[4,64,2048]{2,1,0:T(8,128)(2,1)} %collective-permute-done), kind=kLoop, calls=%fused_computation.11 | loop fusion | flops 4194304 | bytes 8388608 | tf_op jit(solution)/shard_map/concatenate | solution.py:37
  122.3 1.8 %fusion.24 = (bf16[1024,1024]{1,0:T(8,128)(2,1)}, bf16[1024,1024]{1,0:T(8,128)(2,1)S(1)}) fusion(bf16[1024,2048]{1,0:T(8,128)(2,1)S(1)} %bitcast.47), kind=kLoop, calls=%fused_computation.43 | loop fusion | bytes 8388608 | tf_op jit(solution)/shard_map/slice | solution.py:90
  124.2 3.9 %copy.29 = bf16[1024,1024]{0,1:T(8,128)(2,1)} copy(bf16[1024,1024]{1,0:T(8,128)(2,1)} %get-tuple-element.5) | data formatting | bytes 4194304
  128.1 2.5 %copy.28 = bf16[1024,1024]{0,1:T(8,128)(2,1)} copy(bf16[1024,1024]{1,0:T(8,128)(2,1)S(1)} %get-tuple-element.6) | data formatting | bytes 4194304
  130.6 0.0 copy-done.7
  130.6 17.9 %fusion.25 = (f32[16,512]{1,0:T(8,128)S(1)}, f32[16,512,1024]{2,1,0:T(8,128)}) fusion(f32[16,1024]{1,0:T(8,128)S(1)} %bitcast.53, pred[1024]{0:T(1024)(128)(4,1)S(1)} %broadcast_in_dim.39, bf16[512,16,64]{0,2,1:T(8,128)(2,1)S(1)} %bitcast.52, bf16[1024,16,64]{0,2,1:T(8,128)(2,1)} %bitcast.50), kind=kOutput, calls=%fused_computation.44 | convolution fusion | flops 1115685888 | bytes 36799488 | tf_op jit(solution)/shard_map/sub | solution.py:111
  148.6 0.0 copy-done.4
  148.6 13.3 %fusion.12 = bf16[16,64,512]{2,1,0:T(8,128)(2,1)S(1)} fusion(bf16[1024,16,64]{0,2,1:T(8,128)(2,1)S(1)} %bitcast.51, f32[16,512,1024]{2,1,0:T(8,128)} %get-tuple-element.10, f32[16,512]{1,0:T(8,128)S(1)} %get-tuple-element.9), kind=kOutput, calls=%fused_computation.30 | convolution fusion | flops 1091043328 | bytes 36732928 | tf_op jit(solution)/shard_map/hqk,khd->qhd/dot_general | solution.py:113
  161.9 0.0 copy-start.1
  161.9 4.6 %add_convert_fusion = bf16[512,1024]{1,0:T(8,128)(2,1)} fusion(f32[512,1024]{1,0:T(8,128)} %reduce_sum.27, bf16[512,1024]{0,1:T(8,128)(2,1)S(1)} %bitcast.55, bf16[1024,1024]{1,0:T(8,128)(2,1)} %param.20), kind=kOutput, calls=%fused_computation.19 | convolution fusion | flops 1074790400 | bytes 6291456 | tf_op jit(solution)/shard_map/dot_general | solution.py:117
  (15 shorter events, 0.1 us)
Async XLA Ops:
  0.0 93.8 %copy-start = (bf16[1024,1024]{1,0:T(8,128)(2,1)S(1)}, bf16[1024,1024]{1,0:T(8,128)(2,1)}, u32[]{:S(2)}) copy-start(bf16[1024,1024]{1,0:T(8,128)(2,1)} %param.19) | copy-start | bytes 6291460
  11.2 16.0 %copy-start.9 = (s32[128,1,1,8]{0,3,2,1:T(8,128)S(1)}, s32[128,1,1,8]{0,3,2,1:T(8,128)}, u32[]{:S(2)}) copy-start(s32[128,1,1,8]{0,3,2,1:T(8,128)} %param.14) | copy-start | bytes 12292
  11.2 56.3 %all-to-all-start = ((bf16[128,8,768]{2,1,0:T(8,128)(2,1)}), bf16[128,8,768]{2,1,0:T(8,128)(2,1)}, u32[]{:S(2)}, u32[]{:S(2)}) async-start(bf16[128,8,768]{2,1,0:T(8,128)(2,1)} %bitcast_select_fusion), calls=%async_computation | async-start | bytes 3145728 | tf_op jit(solution)/shard_map/all_to_all | solution.py:67
  91.3 2.2 %copy-start.2 = (f32[512,1024]{1,0:T(8,128)S(1)}, f32[512,1024]{1,0:T(8,128)}, u32[]{:S(2)}) copy-start(f32[512,1024]{1,0:T(8,128)} %reduce_sum.27) | copy-start | bytes 6291460
  91.3 2.2 %copy-start.8 = (f32[1024]{0:T(1024)S(1)}, f32[1024]{0:T(1024)}, u32[]{:S(2)}) copy-start(f32[1024]{0:T(1024)} %param.16) | copy-start | bytes 12292
  93.8 1.3 copy-start.5
  93.8 2.0 %copy-start.10 = (bf16[1024,1024]{1,0:T(8,128)(2,1)S(1)}, bf16[1024,1024]{1,0:T(8,128)(2,1)}, u32[]{:S(2)}) copy-start(bf16[1024,1024]{1,0:T(8,128)(2,1)} %param.18) | copy-start | bytes 6291460
  97.0 1.7 copy-start.3
  98.7 8.5 %copy-start.6 = (bf16[512,1024]{1,0:T(8,128)(2,1)S(1)}, bf16[512,1024]{1,0:T(8,128)(2,1)}, u32[]{:S(2)}) copy-start(bf16[512,1024]{1,0:T(8,128)(2,1)} %copy-done.5) | copy-start | bytes 3145732
  98.7 15.9 %collective-permute-start.1 = (bf16[4,64,2048]{2,1,0:T(8,128)(2,1)}, bf16[4,64,2048]{2,1,0:T(8,128)(2,1)}, u32[]{:S(2)}, u32[]{:S(2)}) collective-permute-start(bf16[4,64,2048]{2,1,0:T(8,128)(2,1)} %bitcast.7), channel_id=1, source_target_pairs={{1,0},{16,1},{17,16},{32,17},{33,32},{48,33},{49,48},{64,49},{65,6... | collective-permute-start | bytes 3145736 | tf_op jit(solution)/shard_map/ppermute | solution.py:31
  102.0 18.5 %collective-permute-start = (bf16[4,64,2048]{2,1,0:T(8,128)(2,1)}, bf16[4,64,2048]{2,1,0:T(8,128)(2,1)}, u32[]{:S(2)}, u32[]{:S(2)}) collective-permute-start(bf16[4,64,2048]{2,1,0:T(8,128)(2,1)} %bitcast.5), channel_id=1, source_target_pairs={{0,1},{1,16},{16,17},{17,32},{32,33},{33,48},{48,49},{49,64},{64,6... | collective-permute-start | bytes 3145736 | tf_op jit(solution)/shard_map/ppermute | solution.py:30
  128.1 2.5 %copy-start.7 = (bf16[512,1024]{0,1:T(8,128)(2,1)S(1)}, bf16[512,1024]{0,1:T(8,128)(2,1)}, u32[]{:S(2)}) copy-start(bf16[512,1024]{0,1:T(8,128)(2,1)} %copy.24) | copy-start | bytes 3145732
  130.6 17.9 %copy-start.4 = (bf16[1024,1024]{0,1:T(8,128)(2,1)S(1)}, bf16[1024,1024]{0,1:T(8,128)(2,1)}, u32[]{:S(2)}) copy-start(bf16[1024,1024]{0,1:T(8,128)(2,1)} %copy.28) | copy-start | bytes 6291460
  161.9 4.6 %copy-start.1 = (bf16[1024,1024]{1,0:T(8,128)(2,1)S(1)}, bf16[1024,1024]{1,0:T(8,128)(2,1)}, u32[]{:S(2)}) copy-start(bf16[1024,1024]{1,0:T(8,128)(2,1)} %param.19) | copy-start | bytes 6291460
where the time goes:
time: 167 us; the launch traced here: 166 us
  matrix products  49 us (29%)
  waiting for transfers between devices  47.9 us (29%)
  starting transfers between devices  21.4 us (13%)
  local copies, waits for them, and re-layouts  20.6 us (12%)
  other arithmetic  15.6 us (9%)
  blocking collectives  11.8 us (7%)
    all_to_all x1, waiting for transfers between devices, body(): lax.all_to_all(picked, ('bevy', 'bevx'), split_axis=0, concat_axis=0, til...  40.1 us
    sub x1, matrix products, body(): expo = jnp.exp(scores - top_score)  17.9 us
    all_to_all x1, starting transfers between devices, body(): lax.all_to_all(picked, ('bevy', 'bevx'), split_axis=0, concat_axis=0, til...  16 us
    dot_general x1, matrix products, body(): jnp.einsum('hqk,khd->qhd', weights, value_heads, preferred_element_type=j...  13.3 us
    all_to_all x1, blocking collectives, sum_at_owner(): lax.all_to_all(blocks, axis, split_axis=0, concat_axis=0, tiled=True)  11.8 us
    unnamed x26, local copies, waits for them, and re-layouts  10.2 us
    dot_general x1, matrix products, body(): jnp.dot(one_hot, arrived_rows, preferred_element_type=jnp.float32)  7.78 us
    gather x1, local copies, waits for them, and re-layouts, body(): image_tokens[token_index]  6.67 us
  transfers between devices with their start and end apart: 3, of which 3 were waited for; matrix products, arithmetic and copies ran while one was open for 5% of the time, Pallas kernels for 0%

commit v1 on v0

v1 whole, which is shorter than its diff:
```python
import jax
import jax.numpy as jnp
from jax import lax
from jax.experimental import pallas as pl
from jax.experimental.pallas import tpu as pltpu
from jax.sharding import PartitionSpec as P


ROWS_DEV = 8
COLS_DEV = 64
HALO = 4
MASKED = -1e30
EARLY = (0, -1, 1, -2, 2)
LATE = (-3, 3, 4)


def whole(x):
    return pl.BlockSpec(x.shape, lambda *_: (0,) * x.ndim)


SCALAR = pl.BlockSpec(memory_space=pltpu.SMEM)
LOCAL = pl.BlockSpec(memory_space=pltpu.VMEM)


def pick_kernel(offsets, n_x, at_ref, route_ref, *refs):
    blocks, out_ref = refs[:-1], refs[-1]
    used = 0
    for i, offset in enumerate(offsets):
        parts = 2 if offset == n_x // 2 else 1
        line = (at_ref[0] + (offset + n_x)) % n_x
        index = route_ref[pl.ds(line, 1), :]
        base = 0
        rows = None
        for block in blocks[used : used + parts]:
            ids = lax.broadcasted_iota(jnp.int32, (block.shape[0], index.shape[1]), 0) + base
            one_hot = jnp.where(ids == index, 1.0, 0.0).astype(jnp.bfloat16)
            got = lax.dot_general(
                one_hot,
                block[...],
                (((0,), (0,)), ((), ())),
                preferred_element_type=jnp.float32,
            )
            rows = got if rows is None else rows + got
            base += block.shape[0]
        used += parts
        out_ref[:, i] = rows.reshape(out_ref.shape[0], out_ref.shape[2], out_ref.shape[3]).astype(
            jnp.bfloat16
        )


def pick(offsets, n_x, n_y, at, route, blocks):
    slots = route.shape[1] // n_y
    width = blocks[0].shape[1]
    return pl.pallas_call(
        lambda *refs: pick_kernel(offsets, n_x, *refs),
        in_specs=[SCALAR] + [LOCAL] * (1 + len(blocks)),
        out_specs=LOCAL,
        out_shape=jax.ShapeDtypeStruct((n_y, len(offsets), slots, width), jnp.bfloat16),
        name="pick_rows",
    )(at, route, *blocks)


def summed(offsets, n_x, at_ref, pairs, w_ref, total):
    for rows_ref, cell_ref in pairs:
        pieces = []
        hots = []
        for i, offset in enumerate(offsets):
            line = (at_ref[0] + (offset + n_x)) % n_x
            cell = cell_ref[pl.ds(line, 1), :]
            piece = rows_ref[:, i]
            pieces.append(piece.reshape(-1, piece.shape[-1]))
            ids = lax.broadcasted_iota(jnp.int32, (total.shape[0], cell.shape[1]), 0) + at_ref[1]
            hots.append(jnp.where(ids == cell, 1.0, 0.0).astype(jnp.bfloat16))
        projected = jnp.dot(
            jnp.concatenate(pieces, axis=0), w_ref[...], preferred_element_type=jnp.float32
        ).astype(jnp.bfloat16)
        total[...] += jnp.dot(
            jnp.concatenate(hots, axis=1), projected, preferred_element_type=jnp.float32
        )


def first_sum_kernel(n_x, at_ref, a_ref, ac_ref, b_ref, bc_ref, w_ref, out_ref):
    out_ref[...] = jnp.zeros_like(out_ref)
    summed(EARLY, n_x, at_ref, ((a_ref, ac_ref), (b_ref, bc_ref)), w_ref, out_ref)


def next_sum_kernel(n_x, at_ref, total_ref, a_ref, ac_ref, w_ref, out_ref):
    out_ref[...] = total_ref[...]
    summed(LATE, n_x, at_ref, ((a_ref, ac_ref),), w_ref, out_ref)


def last_sum_kernel(
    n_x, edge, at_ref, total_ref, a_ref, ac_ref, w_ref, gain_ref, own_ref, normed_ref, sent_ref, acc
):
    acc[...] = total_ref[...]
    summed(LATE, n_x, at_ref, ((a_ref, ac_ref),), w_ref, acc)
    rows = own_ref.shape[0]
    own_ref[...] = acc[pl.ds(pl.multiple_of(at_ref[1], edge), rows), :]
    for start in range(0, acc.shape[0], edge):
        lifted = acc[start : start + edge]
        mean_square = jnp.mean(lifted * lifted, axis=-1, keepdims=True)
        normed_ref[start : start + edge] = (
            lifted * lax.rsqrt(mean_square + 1e-06) * gain_ref[...]
        ).astype(jnp.bfloat16)
    sent_ref[...] = normed_ref[pl.ds(pl.multiple_of(2 * at_ref[1], edge), edge), :]


def local_call(kernel, operands, outs, scratch=()):
    return pl.pallas_call(
        kernel,
        in_specs=[SCALAR] + [LOCAL] * (len(operands) - 1),
        out_specs=[LOCAL] * len(outs),
        out_shape=outs,
        scratch_shapes=scratch,
    )(*operands)


def project_kernel(at_ref, x_ref, wq_ref, wk_ref, wv_ref, q_ref, k_ref, v_ref):
    rows = q_ref.shape[0]
    own = x_ref[pl.ds(pl.multiple_of(at_ref[1], rows // 2), rows), :]
    x = x_ref[...]
    q_ref[...] = (jnp.dot(own, wq_ref[...], preferred_element_type=jnp.float32)).astype(
        jnp.bfloat16
    )
    k_ref[...] = jnp.dot(x, wk_ref[...], preferred_element_type=jnp.float32).astype(jnp.bfloat16)
    v_ref[...] = jnp.dot(x, wv_ref[...], preferred_element_type=jnp.float32).astype(jnp.bfloat16)


def project(at, x, w_query, w_key, w_value, rows):
    ext, width = x.shape
    block = 256
    column = lambda r: pl.BlockSpec((r, block), lambda i: (0, i))
    return pl.pallas_call(
        project_kernel,
        grid=(width // block,),
        in_specs=[SCALAR, whole(x)] + [column(width)] * 3,
        out_specs=[column(rows), column(ext), column(ext)],
        out_shape=[
            jax.ShapeDtypeStruct((r, width), jnp.bfloat16) for r in (rows, ext, ext)
        ],
        compiler_params=pltpu.CompilerParams(dimension_semantics=("arbitrary",)),
        name="near_projections",
    )(at, x, w_query, w_key, w_value)


def attention_kernel(
    q_ref, k_ref, v_ref, far_ref, wk_ref, wv_ref, bias_ref, wo_ref, lifted_ref, out_ref, att_ref
):
    step = pl.program_id(0)
    rows_q = q_ref.shape[0]
    chunk = 256
    far = far_ref[...]
    far_k = jnp.dot(far, wk_ref[...], preferred_element_type=jnp.float32).astype(jnp.bfloat16)
    far_v = jnp.dot(far, wv_ref[...], preferred_element_type=jnp.float32).astype(jnp.bfloat16)
    lane = lax.broadcasted_iota(jnp.int32, (chunk, 128), 1)
    for pair in range(2):
        cut = slice(pair * 128, pair * 128 + 128)
        k = jnp.concatenate([k_ref[:, cut], far_k[:, cut]], axis=0)
        v = jnp.concatenate([v_ref[:, cut], far_v[:, cut]], axis=0)
        keys = jnp.concatenate([k, bias_ref[...]], axis=1)
        values = jnp.concatenate([v, jnp.ones_like(v)], axis=1)
        for start in range(0, rows_q, chunk):
            q = q_ref[start : start + chunk, cut] * jnp.asarray(0.125, jnp.bfloat16)
            done = []
            for side in range(2):
                own = (lane >= 64) if side else (lane < 64)
                query = jnp.concatenate(
                    [
                        jnp.where(own, q, jnp.zeros((), jnp.bfloat16)),
                        jnp.where(lane == 4 * step + 2 * pair + side, 1.0, 0.0).astype(
                            jnp.bfloat16
                        ),
                    ],
                    axis=1,
                )
                score = lax.dot_general(
                    query, keys, (((1,), (1,)), ((), ())), preferred_element_type=jnp.float32
                )
                top = jnp.max(score, axis=1, keepdims=True)
                weight = jnp.exp(score - top).astype(jnp.bfloat16)
                total = jnp.dot(weight, values, preferred_element_type=jnp.float32)
                done.append(total[:, :128] / total[:, 128:])
            att_ref[2 * step + pair, start : start + chunk] = jnp.where(
                lane < 64, done[0], done[1]
            ).astype(jnp.bfloat16)

    @pl.when(step == pl.num_programs(0) - 1)
    def _():
        attended = jnp.concatenate([att_ref[i] for i in range(att_ref.shape[0])], axis=1)
        mixed = jnp.dot(attended, wo_ref[...], preferred_element_type=jnp.float32)
        out_ref[...] = (lifted_ref[...] + mixed).astype(jnp.bfloat16)


def attention(q, k, v, far, w_key, w_value, bias, w_out, lifted):
    rows, width = q.shape
    block = 256
    column = lambda x: pl.BlockSpec((x.shape[0], block), lambda i: (0, i))
    return pl.pallas_call(
        attention_kernel,
        grid=(width // block,),
        in_specs=[
            column(q),
            column(k),
            column(v),
            whole(far),
            column(w_key),
            column(w_value),
            whole(bias),
            whole(w_out),
            whole(lifted),
        ],
        out_specs=pl.BlockSpec((rows, width), lambda i: (0, 0)),
        out_shape=jax.ShapeDtypeStruct((rows, width), jnp.bfloat16),
        scratch_shapes=[pltpu.VMEM((width // 128, rows, 128), jnp.bfloat16)],
        compiler_params=pltpu.CompilerParams(dimension_semantics=("arbitrary",)),
        name="window_attention",
    )(q, k, v, far, w_key, w_value, bias, w_out, lifted)


def steps(
    image_tokens,
    lift_weight,
    route_token,
    route_cell,
    slot_counts,
    norm_gain,
    w_query,
    w_key,
    w_value,
    w_out,
    key_bias,
):
    n_y = lax.axis_size("bevy")
    n_x = lax.axis_size("bevx")
    slot_count = route_token.shape[3]
    tokens = image_tokens.shape[0]
    width = lift_weight.shape[1]
    head_count = key_bias.shape[2]
    grid_rows = key_bias.shape[0]
    own_cells = ROWS_DEV * COLS_DEV
    edge = HALO * COLS_DEV
    ext = own_cells + edge
    row = lax.axis_index("bevy")
    col = lax.axis_index("bevx")
    core = lax.axis_index("cam")
    up = [(i, (i + 1) % n_x) for i in range(n_x)]
    down = [(b, a) for a, b in up]
    swap = [(0, 1), (1, 0)]
    at = jnp.stack([col, core * edge]).astype(jnp.int32)

    def shift(value, perm):
        return lax.ppermute(value, "bevx", perm)

    u1 = shift(image_tokens, up)
    d1 = shift(image_tokens, down)

    def by_column(value):
        return value.reshape(n_y, n_x, slot_count).transpose(1, 0, 2).reshape(n_x, -1)

    is_live = (
        lax.broadcasted_iota(jnp.int32, route_token.shape[2:], 1) < slot_counts[0, 0][:, None]
    )
    route = by_column(jnp.where(is_live, route_token[0, 0], -1))
    cells = by_column(route_cell[:, 0, 0, :])
    route, cells = lax.optimization_barrier((route, cells))
    cells_other = lax.ppermute(cells, "cam", swap)
    route = lax.all_to_all(route, "bevx", split_axis=0, concat_axis=0, tiled=True)

    u2 = shift(u1, up)
    d2 = shift(d1, down)
    u3 = shift(u2, up)
    d3 = shift(d2, down)
    half = tokens // 2
    u4 = shift(u3[:half], up)
    d4 = shift(d3[half:], down)

    near_row = (row * 2 + core) * ROWS_DEV - core * HALO
    far_row = (row * 2 + core) * ROWS_DEV + jnp.where(core == 0, -HALO, ROWS_DEV)
    far_ok = (far_row >= 0) & (far_row < grid_rows)
    near_bias = lax.dynamic_slice_in_dim(key_bias, near_row, ROWS_DEV + HALO, 0)
    far_bias = lax.dynamic_slice_in_dim(
        key_bias, jnp.clip(far_row, 0, grid_rows - HALO), HALO, 0
    )
    far_bias = jnp.where(far_ok, far_bias, jnp.asarray(MASKED, jnp.bfloat16))
    bias = jnp.concatenate([near_bias, far_bias], axis=0).reshape(-1, head_count)
    bias = jnp.pad(bias, ((0, 0), (0, 128 - head_count)))

    def exchange(rows):
        got = lax.all_to_all(rows, "bevy", split_axis=0, concat_axis=0, tiled=True)
        return got, lax.ppermute(got, "cam", swap)

    rows = pick(EARLY, n_x, n_y, at, route, (image_tokens, u1, d1, u2, d2))
    rows, bias, cells_other = lax.optimization_barrier((rows, bias, cells_other))
    early, early_other = exchange(rows)
    total = jax.ShapeDtypeStruct((ext, width), jnp.float32)
    [lifted] = local_call(
        lambda *refs: first_sum_kernel(n_x, *refs),
        (at, early, cells, early_other, cells_other, lift_weight),
        [total],
    )
    rows = pick(LATE, n_x, n_y, at, route, (u3, d3, u4, d4))
    late, late_other = exchange(rows)
    [lifted] = local_call(
        lambda *refs: next_sum_kernel(n_x, *refs), (at, lifted, late, cells, lift_weight), [total]
    )
    own_lifted, normed, sent = local_call(
        lambda *refs: last_sum_kernel(n_x, edge, *refs),
        (at, lifted, late_other, cells_other, lift_weight, norm_gain.reshape(1, -1)),
        [
            jax.ShapeDtypeStruct((own_cells, width), jnp.float32),
            jax.ShapeDtypeStruct((ext, width), jnp.bfloat16),
            jax.ShapeDtypeStruct((edge, width), jnp.bfloat16),
        ],
        [pltpu.VMEM((ext, width), jnp.float32)],
    )
    hops = [(2 * i, 2 * i - 1) for i in range(1, n_y)] + [
        (2 * i + 1, 2 * i + 2) for i in range(n_y - 1)
    ]
    far = lax.ppermute(sent, ("bevy", "cam"), hops)
    queries, keys, values = project(at, normed, w_query, w_key, w_value, own_cells)

    out = attention(
        queries, keys, values, far, w_key, w_value, bias, w_out, own_lifted
    )
    return out.reshape(ROWS_DEV, COLS_DEV, width)


def solution(mesh):
    placed = (
        P(("bevy", "bevx", "cam"), None),
        P(),
        P(("bevy", "bevx"), "cam", None, None),
        P(None, "cam", ("bevy", "bevx"), None),
        P(("bevy", "bevx"), "cam", None),
        P(),
        P(),
        P(),
        P(),
        P(),
        P(None, "bevx", None),
    )
    return jax.shard_map(
        steps,
        mesh=mesh,
        in_specs=placed,
        out_specs=P(("bevy", "cam"), "bevx", None),
        check_vma=False,
    )
```

time: 167 us -> 135 us (0.81)
  Pallas kernels: 0 us -> 52.8 us
  matrix products: 49 us -> 0 us
  starting transfers between devices: 21.4 us -> 40.2 us
  waiting for transfers between devices: 47.9 us -> 29.4 us
  other arithmetic: 15.6 us -> 2.02 us
  blocking collectives: 11.8 us -> 0 us
  local copies, waits for them, and re-layouts: 20.6 us -> 8.91 us
    pallas_call x0 -> x7, Pallas kernels: none -> 52.8 us  [the longest x3 20.7 us: local_call(): pl.pallas_call(kernel, in_specs=[SCALAR] + [LOCAL] * (len(operands) - 1),...]
    dot_general x6 -> x0, matrix products: 31.1 us -> none  [the longest x1 13.3 us: body(): jnp.einsum('hqk,khd->qhd', weights, value_heads, preferred_element_type=j...]
    all_to_all x1 -> x3, waiting for transfers between devices: 40.1 us -> 10.1 us  [the longest x2 8.44 us: exchange(): got = lax.all_to_all(rows, 'bevy', split_axis=0, concat_axis=0, tiled=True)]
    sub x1 -> x0, matrix products: 17.9 us -> none  [body(): expo = jnp.exp(scores - top_score)]
    ppermute x2 -> x12, starting transfers between devices: 5.42 us -> 19.7 us  [the longest x8 15.7 us: shift(): return lax.ppermute(value, 'bevx', perm)]
    all_to_all x1 -> x0, blocking collectives: 11.8 us -> none  [sum_at_owner(): lax.all_to_all(blocks, axis, split_axis=0, concat_axis=0, tiled=True)]
    ppermute x2 -> x12, waiting for transfers between devices: 7.79 us -> 19.3 us  [the longest x8 18.9 us: shift(): return lax.ppermute(value, 'bevx', perm)]
    gather x1 -> x0, local copies, waits for them, and re-layouts: 6.67 us -> none  [body(): image_tokens[token_index]]
  transfers between devices with their start and end apart: 3 -> 15, of which waited for: 3 -> 8; matrix products, arithmetic and copies ran while one was open for 5% -> 5% of each run, Pallas kernels for 0% -> 21%
where the time goes in v1:
time: 135 us; the launch traced here: 133 us
  Pallas kernels  52.8 us (39%)
  starting transfers between devices  40.2 us (30%)
  waiting for transfers between devices  29.4 us (22%)
  local copies, waits for them, and re-layouts  8.91 us (7%)
  other arithmetic  2.02 us (1%)
    pallas_call x3, Pallas kernels, local_call(): pl.pallas_call(kernel, in_specs=[SCALAR] + [LOCAL] * (len(operands) - 1),...  20.7 us
    ppermute x8, waiting for transfers between devices, shift(): return lax.ppermute(value, 'bevx', perm)  18.9 us
    pallas_call x1, Pallas kernels, attention(): pl.pallas_call(attention_kernel, grid=(width // block,), in_specs=[column...  18.4 us
    ppermute x8, starting transfers between devices, shift(): return lax.ppermute(value, 'bevx', perm)  15.7 us
    all_to_all x2, starting transfers between devices, exchange(): got = lax.all_to_all(rows, 'bevy', split_axis=0, concat_axis=0, tiled=True)  14.6 us
    all_to_all x2, waiting for transfers between devices, exchange(): got = lax.all_to_all(rows, 'bevy', split_axis=0, concat_axis=0, tiled=True)  8.44 us
    pallas_call x1, Pallas kernels, project(): pl.pallas_call(project_kernel, grid=(width // block,), in_specs=[SCALAR,...  8.33 us
    all_to_all x1, starting transfers between devices, steps(): lax.all_to_all(route, 'bevx', split_axis=0, concat_axis=0, tiled=True)  5.78 us
  transfers between devices with their start and end apart: 15, of which 8 were waited for; matrix products, arithmetic and copies ran while one was open for 5% of the time, Pallas kernels for 21%

profile of v1, /device:TPU:8, one launch (start us, length us, event | category | flops | bytes accessed | tf_op | source)
XLA Modules:
  0.0 133.5 jit_solution(16559063341912938305)
XLA Ops:
  0.0 1.9 %collective-permute-start = (bf16[256,768]{1,0:T(8,128)(2,1)}, bf16[256,768]{1,0:T(8,128)(2,1)S(1)}, u32[]{:S(2)}, u32[]{:S(2)}) collective-permute-start(bf16[256,768]{1,0:T(8,128)(2,1)} %refs_2_.1), channel_id=1, source_target_pairs={{0,2},{2,4},{4,6},{6,8},{8,10},{10,12},{12,14},{14,0},{1,3},{3,5},... | collective-permute-start | bytes 1179656 | tf_op jit(solution)/shard_map/ppermute | solution.py:252
  1.9 4.0 %collective-permute-start.1 = (bf16[256,768]{1,0:T(8,128)(2,1)}, bf16[256,768]{1,0:T(8,128)(2,1)S(1)}, u32[]{:S(2)}, u32[]{:S(2)}) collective-permute-start(bf16[256,768]{1,0:T(8,128)(2,1)} %refs_2_.1), channel_id=1, source_target_pairs={{2,0},{4,2},{6,4},{8,6},{10,8},{12,10},{14,12},{0,14},{3,1},{5,3},... | collective-permute-start | bytes 1179656 | tf_op jit(solution)/shard_map/ppermute | solution.py:252
  5.9 0.5 broadcast.8
  6.5 1.3 reduce.3
  7.9 0.8 squeeze.3
  8.7 0.1 copy.19
  8.8 0.7 reshape.26
  9.4 0.8 reshape_squeeze.3
  10.2 0.1 copy.20
  10.3 0.1 reshape.27.refs_2_.refs_3_
  10.4 5.8 %all-to-all-start = ((s32[8,1,128]{2,1,0:T(1,128)}), s32[8,1,128]{2,1,0:T(1,128)S(1)}, u32[]{:S(2)}, u32[]{:S(2)}) async-start(s32[8,1,128]{2,1,0:T(1,128)} %bitcast.5), calls=%async_computation | async-start | bytes 8192 | tf_op jit(solution)/shard_map/all_to_all | solution.py:267
  16.2 0.1 constant_dynamic-slice_fusion.1
  16.4 0.3 copy.25
  16.7 0.1 constant_dynamic-slice_fusion
  16.9 0.3 copy.26
  17.2 2.1 %collective-permute-start.2 = (bf16[256,768]{1,0:T(8,128)(2,1)S(1)}, bf16[256,768]{1,0:T(8,128)(2,1)S(1)}, u32[]{:S(2)}, u32[]{:S(2)}) collective-permute-start(bf16[256,768]{1,0:T(8,128)(2,1)S(1)} %collective-permute-done.refs_3_), channel_id=1, source_target_pairs={{0,2},{2,4},{4,6},{6,8},{8,10},{10,12},{12,14},{14,0},{1,3},{3,5},... | collective-permute-start | bytes 1179656 | tf_op jit(solution)/shard_map/ppermute | solution.py:252
  19.2 1.3 collective-permute-start.3
  20.6 0.7 pad_add_fusion.refs_0_.at_ref
  21.2 0.2 copy.24
  21.4 0.8 pad.4.bias_ref
  22.2 1.6 %all-to-all-done = s32[8,1,128]{2,1,0:T(1,128)S(1)} async-done(((s32[8,1,128]{2,1,0:T(1,128)}), s32[8,1,128]{2,1,0:T(1,128)S(1)}, u32[]{:S(2)}, u32[]{:S(2)}) %all-to-all-start) | async-done | bytes 4128 | tf_op jit(solution)/shard_map/all_to_all | solution.py:267
  23.8 6.4 %collective-permute-done.2.refs_5_ = bf16[256,768]{1,0:T(8,128)(2,1)S(1)} collective-permute-done((bf16[256,768]{1,0:T(8,128)(2,1)S(1)}, bf16[256,768]{1,0:T(8,128)(2,1)S(1)}, u32[]{:S(2)}, u32[]{:S(2)}) %collective-permute-start.2) | collective-permute-done | bytes 393248 | tf_op jit(solution)/shard_map/ppermute | solution.py:252
  30.2 0.2 collective-permute-done.3.refs_6_
  30.5 0.5 copy-done.10
  31.0 0.2 copy-done.9
  31.2 2.9 %pick_rows.2 = bf16[16,5,8,768]{3,2,1,0:T(8,128)(2,1)} custom-call(s32[2]{0:T(128)} %pad_add_fusion.refs_0_.at_ref, s32[8,128]{1,0:T(8,128)} %bitcast.22, bf16[256,768]{1,0:T(8,128)(2,1)} %refs_2_.1, bf16[256,768]{1,0:T(8,128)(2,1)} %copy-done.7, bf16[256,768]{1,0:T(8,128)(2,1)} %copy-done.8, bf16[256,768]{1,0:T(8,128)(2,1)} %copy-done.10, ...), custom_call_target="tpu_custom_call" | custom-call | tf_op jit(solution)/shard_map/pick_rows/pallas_call | solution.py:54
  34.1 7.4 %all-to-all-start.1 = ((bf16[16,5,8,768]{3,2,1,0:T(8,128)(2,1)}), bf16[16,5,8,768]{3,2,1,0:T(8,128)(2,1)S(1)}, u32[]{:S(2)}, u32[]{:S(2)}) async-start(bf16[16,5,8,768]{3,2,1,0:T(8,128)(2,1)} %pick_rows.2), calls=%async_computation.1 | async-start | bytes 1966080 | tf_op jit(solution)/shard_map/all_to_all | solution.py:289
  41.5 1.5 %collective-permute-start.6 = (bf16[256,768]{1,0:T(8,128)(2,1)}, bf16[256,768]{1,0:T(8,128)(2,1)S(1)}, u32[]{:S(2)}, u32[]{:S(2)}) collective-permute-start(bf16[256,768]{1,0:T(8,128)(2,1)} %copy-done.10), channel_id=1, source_target_pairs={{0,2},{2,4},{4,6},{6,8},{8,10},{10,12},{12,14},{14,0},{1,3},{3,5},... | collective-permute-start | bytes 1179656 | tf_op jit(solution)/shard_map/ppermute | solution.py:252
  43.0 1.8 %collective-permute-start.7 = (bf16[256,768]{1,0:T(8,128)(2,1)}, bf16[256,768]{1,0:T(8,128)(2,1)S(1)}, u32[]{:S(2)}, u32[]{:S(2)}) collective-permute-start(bf16[256,768]{1,0:T(8,128)(2,1)} %copy-done.9), channel_id=1, source_target_pairs={{2,0},{4,2},{6,4},{8,6},{10,8},{12,10},{14,12},{0,14},{3,1},{5,3},... | collective-permute-start | bytes 1179656 | tf_op jit(solution)/shard_map/ppermute | solution.py:252
  44.7 8.5 %collective-permute-done.6.refs_2_ = bf16[256,768]{1,0:T(8,128)(2,1)S(1)} collective-permute-done((bf16[256,768]{1,0:T(8,128)(2,1)}, bf16[256,768]{1,0:T(8,128)(2,1)S(1)}, u32[]{:S(2)}, u32[]{:S(2)}) %collective-permute-start.6) | collective-permute-done | bytes 393248 | tf_op jit(solution)/shard_map/ppermute | solution.py:252
  53.2 0.2 collective-permute-start.8
  53.4 0.3 collective-permute-done.7.refs_3_
  53.7 3.0 %collective-permute-start.9 = (bf16[128,768]{1,0:T(8,128)(2,1)S(1)}, bf16[128,768]{1,0:T(8,128)(2,1)S(1)}, u32[]{:S(2)}, u32[]{:S(2)}) collective-permute-start(bf16[128,768]{1,0:T(8,128)(2,1)S(1)} %slice.9), channel_id=1, source_target_pairs={{2,0},{4,2},{6,4},{8,6},{10,8},{12,10},{14,12},{0,14},{3,1},{5,3},... | collective-permute-start | bytes 589832 | tf_op jit(solution)/shard_map/ppermute | solution.py:252
  56.6 3.5 %collective-permute-done.8.refs_4_ = bf16[128,768]{1,0:T(8,128)(2,1)S(1)} collective-permute-done((bf16[128,768]{1,0:T(8,128)(2,1)S(1)}, bf16[128,768]{1,0:T(8,128)(2,1)S(1)}, u32[]{:S(2)}, u32[]{:S(2)}) %collective-permute-start.8) | collective-permute-done | bytes 196640 | tf_op jit(solution)/shard_map/ppermute | solution.py:252
  60.2 0.7 copy-done.11
  60.9 0.7 copy-done.12
  61.5 2.5 %pick_rows.3 = bf16[16,3,8,768]{3,2,1,0:T(8,128)(2,1)} custom-call(s32[2]{0:T(128)} %pad_add_fusion.refs_0_.at_ref, s32[8,128]{1,0:T(8,128)} %bitcast.23, bf16[256,768]{1,0:T(8,128)(2,1)} %copy-done.4, bf16[256,768]{1,0:T(8,128)(2,1)} %copy-done.5, bf16[128,768]{1,0:T(8,128)(2,1)} %copy-done.11, bf16[128,768]{1,0:T(8,128)(2,1)} %copy-done.12), custom_call_target="tpu_custom_call" | custom-call | tf_op jit(solution)/shard_map/pick_rows/pallas_call | solution.py:54
  64.0 7.2 %all-to-all-start.2 = ((bf16[16,3,8,768]{3,2,1,0:T(8,128)(2,1)}), bf16[16,3,8,768]{3,2,1,0:T(8,128)(2,1)S(1)}, u32[]{:S(2)}, u32[]{:S(2)}) async-start(bf16[16,3,8,768]{3,2,1,0:T(8,128)(2,1)} %pick_rows.3), calls=%async_computation.2 | async-start | bytes 1179648 | tf_op jit(solution)/shard_map/all_to_all | solution.py:289
  71.3 8.4 %all-to-all-done.2.refs_2_ = bf16[16,3,8,768]{3,2,1,0:T(8,128)(2,1)S(1)} async-done(((bf16[16,3,8,768]{3,2,1,0:T(8,128)(2,1)}), bf16[16,3,8,768]{3,2,1,0:T(8,128)(2,1)S(1)}, u32[]{:S(2)}, u32[]{:S(2)}) %all-to-all-start.2) | async-done | bytes 589856 | tf_op jit(solution)/shard_map/all_to_all | solution.py:289
  79.8 1.0 copy-done.3
  80.8 8.4 %shard_map.109.refs_1_ = f32[768,1024]{1,0:T(8,128)} custom-call(s32[2]{0:T(128)} %pad_add_fusion.refs_0_.at_ref, bf16[16,5,8,768]{3,2,1,0:T(8,128)(2,1)} %copy-done.1, s32[8,128]{1,0:T(8,128)} %copy-done.14, bf16[16,5,8,768]{3,2,1,0:T(8,128)(2,1)} %copy-done.3, s32[8,128]{1,0:T(8,128)} %copy-done.15, bf16[768,1024]{1,0:T(8,128)(2,1)} %refs_4_.3), custom_call_target="tpu_custom_call" | custom-call | tf_op jit(solution)/shard_map/pallas_call | solution.py:109
  89.1 5.8 %shard_map.110.refs_1_ = f32[768,1024]{1,0:T(8,128)} custom-call(s32[2]{0:T(128)} %pad_add_fusion.refs_0_.at_ref, f32[768,1024]{1,0:T(8,128)} %shard_map.109.refs_1_, bf16[16,3,8,768]{3,2,1,0:T(8,128)(2,1)} %copy-done.2, s32[8,128]{1,0:T(8,128)} %copy-done.14, bf16[768,1024]{1,0:T(8,128)(2,1)} %refs_4_.3), custom_call_target="tpu_custom_call" | custom-call | tf_op jit(solution)/shard_map/pallas_call | solution.py:109
  94.9 6.5 %shard_map.111 = (f32[512,1024]{1,0:T(8,128)}, bf16[768,1024]{1,0:T(8,128)(2,1)}, bf16[256,1024]{1,0:T(8,128)(2,1)}) custom-call(s32[2]{0:T(128)} %pad_add_fusion.refs_0_.at_ref, f32[768,1024]{1,0:T(8,128)} %shard_map.110.refs_1_, bf16[16,3,8,768]{3,2,1,0:T(8,128)(2,1)} %collective-permute-done.10.refs_2_, s32[8,128]{1,0:T(8,128)} %copy-done.15, ...), custom_call_target="tpu_custom_call" | custom-call | tf_op jit(solution)/shard_map/pallas_call | solution.py:109
  101.4 4.0 %collective-permute-start.11 = (bf16[256,1024]{1,0:T(8,128)(2,1)}, bf16[256,1024]{1,0:T(8,128)(2,1)S(1)}, u32[]{:S(2)}, u32[]{:S(2)}) collective-permute-start(bf16[256,1024]{1,0:T(8,128)(2,1)} %get-tuple-element.24), channel_id=1, source_target_pairs={{16,1},{32,17},{48,33},{64,49},{80,65},{96,81},{112,97},{128,113},... | collective-permute-start | bytes 1572872 | tf_op jit(solution)/shard_map/ppermute | solution.py:319
  105.5 8.3 %near_projections.1 = (bf16[512,1024]{1,0:T(8,128)(2,1)}, bf16[768,1024]{1,0:T(8,128)(2,1)}, bf16[768,1024]{1,0:T(8,128)(2,1)}) custom-call(s32[2]{0:T(128)} %pad_add_fusion.refs_0_.at_ref, bf16[768,1024]{1,0:T(8,128)(2,1)} %get-tuple-element.20.x_ref, bf16[1024,1024]{1,0:T(8,128)(2,1)} %wq_ref.1, bf16[1024,1024]{1,0:T(8,128)(2,1)} %wk_ref.3, ...), custom_call_target="tpu_custom_call" | custom-call | tf_op jit(solution)/shard_map/near_projections/pallas_call | solution.py:133
  113.8 0.4 collective-permute-done.11.far_ref
  114.3 0.8 copy-done.6
  115.1 18.4 %window_attention.1 = bf16[512,1024]{1,0:T(8,128)(2,1)} custom-call(bf16[512,1024]{1,0:T(8,128)(2,1)} %get-tuple-element.21.q_ref, bf16[768,1024]{1,0:T(8,128)(2,1)} %get-tuple-element.22.k_ref, bf16[768,1024]{1,0:T(8,128)(2,1)} %get-tuple-element.23.v_ref, bf16[256,1024]{1,0:T(8,128)(2,1)} %copy-done.6, bf16[1024,1024]{1,0:T(8,128)(2,1)} %wk_ref.3, ...), custom_call_target="tpu_custom_call" | custom-call | tf_op jit(solution)/shard_map/window_attention/pallas_call | solution.py:198
  (42 shorter events, 0.2 us)
Async XLA Ops:
  0.0 16.2 %copy-start = (bf16[256,64,16]{0,2,1:T(8,128)(2,1)S(1)}, bf16[256,64,16]{0,2,1:T(8,128)(2,1)}, u32[]{:S(2)}) copy-start(bf16[256,64,16]{0,2,1:T(8,128)(2,1)} %param.21) | copy-start | bytes 1572868
  0.0 17.1 %collective-permute-start = (bf16[256,768]{1,0:T(8,128)(2,1)}, bf16[256,768]{1,0:T(8,128)(2,1)S(1)}, u32[]{:S(2)}, u32[]{:S(2)}) collective-permute-start(bf16[256,768]{1,0:T(8,128)(2,1)} %refs_2_.1), channel_id=1, source_target_pairs={{0,2},{2,4},{4,6},{6,8},{8,10},{10,12},{12,14},{14,0},{1,3},{3,5},... | collective-permute-start | bytes 1179656 | tf_op jit(solution)/shard_map/ppermute | solution.py:252
  1.9 17.3 %collective-permute-start.1 = (bf16[256,768]{1,0:T(8,128)(2,1)}, bf16[256,768]{1,0:T(8,128)(2,1)S(1)}, u32[]{:S(2)}, u32[]{:S(2)}) collective-permute-start(bf16[256,768]{1,0:T(8,128)(2,1)} %refs_2_.1), channel_id=1, source_target_pairs={{2,0},{4,2},{6,4},{8,6},{10,8},{12,10},{14,12},{0,14},{3,1},{5,3},... | collective-permute-start | bytes 1179656 | tf_op jit(solution)/shard_map/ppermute | solution.py:252
  10.4 23.7 %copy-start.14 = (s32[8,128]{1,0:T(8,128)}, s32[8,128]{1,0:T(8,128)S(1)}, u32[]{:S(2)}) copy-start(s32[8,128]{1,0:T(8,128)S(1)} %reshape.27.refs_2_.refs_3_) | copy-start | bytes 12292
  10.4 13.4 %all-to-all-start = ((s32[8,1,128]{2,1,0:T(1,128)}), s32[8,1,128]{2,1,0:T(1,128)S(1)}, u32[]{:S(2)}, u32[]{:S(2)}) async-start(s32[8,1,128]{2,1,0:T(1,128)} %bitcast.5), calls=%async_computation | async-start | bytes 8192 | tf_op jit(solution)/shard_map/all_to_all | solution.py:267
  16.2 17.9 %collective-permute-start.4 = (s32[8,128]{1,0:T(8,128)S(1)}, s32[8,128]{1,0:T(8,128)S(1)}, u32[]{:S(2)}, u32[]{:S(2)}) collective-permute-start(s32[8,128]{1,0:T(8,128)S(1)} %reshape.27.refs_2_.refs_3_), channel_id=1, source_target_pairs={{0,1},{1,0},{2,3},{3,2},{4,5},{5,4},{6,7},{7,6},{8,9},{9,8},{10,11... | collective-permute-start | bytes 12296 | tf_op jit(solution)/shard_map/ppermute | solution.py:266
  17.1 13.3 %copy-start.7 = (bf16[256,768]{1,0:T(8,128)(2,1)}, bf16[256,768]{1,0:T(8,128)(2,1)S(1)}, u32[]{:S(2)}) copy-start(bf16[256,768]{1,0:T(8,128)(2,1)S(1)} %collective-permute-done.refs_3_) | copy-start | bytes 1179652
  17.2 13.1 %collective-permute-start.2 = (bf16[256,768]{1,0:T(8,128)(2,1)S(1)}, bf16[256,768]{1,0:T(8,128)(2,1)S(1)}, u32[]{:S(2)}, u32[]{:S(2)}) collective-permute-start(bf16[256,768]{1,0:T(8,128)(2,1)S(1)} %collective-permute-done.refs_3_), channel_id=1, source_target_pairs={{0,2},{2,4},{4,6},{6,8},{8,10},{10,12},{12,14},{14,0},{1,3},{3,5},... | collective-permute-start | bytes 1179656 | tf_op jit(solution)/shard_map/ppermute | solution.py:252
  19.2 11.2 %copy-start.8 = (bf16[256,768]{1,0:T(8,128)(2,1)}, bf16[256,768]{1,0:T(8,128)(2,1)S(1)}, u32[]{:S(2)}) copy-start(bf16[256,768]{1,0:T(8,128)(2,1)S(1)} %collective-permute-done.1.refs_4_) | copy-start | bytes 1179652
  19.2 11.2 %collective-permute-start.3 = (bf16[256,768]{1,0:T(8,128)(2,1)S(1)}, bf16[256,768]{1,0:T(8,128)(2,1)S(1)}, u32[]{:S(2)}, u32[]{:S(2)}) collective-permute-start(bf16[256,768]{1,0:T(8,128)(2,1)S(1)} %collective-permute-done.1.refs_4_), channel_id=1, source_target_pairs={{2,0},{4,2},{6,4},{8,6},{10,8},{12,10},{14,12},{0,14},{3,1},{5,3},... | collective-permute-start | bytes 1179656 | tf_op jit(solution)/shard_map/ppermute | solution.py:252
  23.8 6.6 %copy-start.13 = (s32[8,1,128]{2,1,0:T(1,128)}, s32[8,1,128]{2,1,0:T(1,128)S(1)}, u32[]{:S(2)}) copy-start(s32[8,1,128]{2,1,0:T(1,128)S(1)} %all-to-all-done) | copy-start | bytes 12292
  30.2 0.8 copy-start.10
  30.5 0.7 copy-start.9
  34.1 29.9 %copy-start.15 = (s32[8,128]{1,0:T(8,128)}, s32[8,128]{1,0:T(8,128)S(1)}, u32[]{:S(2)}) copy-start(s32[8,128]{1,0:T(8,128)S(1)} %collective-permute-done.4.refs_4_.refs_3_) | copy-start | bytes 12292
  34.1 29.9 %all-to-all-start.1 = ((bf16[16,5,8,768]{3,2,1,0:T(8,128)(2,1)}), bf16[16,5,8,768]{3,2,1,0:T(8,128)(2,1)S(1)}, u32[]{:S(2)}, u32[]{:S(2)}) async-start(bf16[16,5,8,768]{3,2,1,0:T(8,128)(2,1)} %pick_rows.2), calls=%async_computation.1 | async-start | bytes 1966080 | tf_op jit(solution)/shard_map/all_to_all | solution.py:289
  41.5 11.7 %collective-permute-start.6 = (bf16[256,768]{1,0:T(8,128)(2,1)}, bf16[256,768]{1,0:T(8,128)(2,1)S(1)}, u32[]{:S(2)}, u32[]{:S(2)}) collective-permute-start(bf16[256,768]{1,0:T(8,128)(2,1)} %copy-done.10), channel_id=1, source_target_pairs={{0,2},{2,4},{4,6},{6,8},{8,10},{10,12},{12,14},{14,0},{1,3},{3,5},... | collective-permute-start | bytes 1179656 | tf_op jit(solution)/shard_map/ppermute | solution.py:252
  43.0 10.7 %collective-permute-start.7 = (bf16[256,768]{1,0:T(8,128)(2,1)}, bf16[256,768]{1,0:T(8,128)(2,1)S(1)}, u32[]{:S(2)}, u32[]{:S(2)}) collective-permute-start(bf16[256,768]{1,0:T(8,128)(2,1)} %copy-done.9), channel_id=1, source_target_pairs={{2,0},{4,2},{6,4},{8,6},{10,8},{12,10},{14,12},{0,14},{3,1},{5,3},... | collective-permute-start | bytes 1179656 | tf_op jit(solution)/shard_map/ppermute | solution.py:252
  53.2 7.0 %copy-start.4 = (bf16[256,768]{1,0:T(8,128)(2,1)}, bf16[256,768]{1,0:T(8,128)(2,1)S(1)}, u32[]{:S(2)}) copy-start(bf16[256,768]{1,0:T(8,128)(2,1)S(1)} %collective-permute-done.6.refs_2_) | copy-start | bytes 1179652
  53.2 7.0 %collective-permute-start.8 = (bf16[128,768]{1,0:T(8,128)(2,1)S(1)}, bf16[128,768]{1,0:T(8,128)(2,1)S(1)}, u32[]{:S(2)}, u32[]{:S(2)}) collective-permute-start(bf16[128,768]{1,0:T(8,128)(2,1)S(1)} %slice.8), channel_id=1, source_target_pairs={{0,2},{2,4},{4,6},{6,8},{8,10},{10,12},{12,14},{14,0},{1,3},{3,5},... | collective-permute-start | bytes 589832 | tf_op jit(solution)/shard_map/ppermute | solution.py:252
  53.7 6.5 %copy-start.5 = (bf16[256,768]{1,0:T(8,128)(2,1)}, bf16[256,768]{1,0:T(8,128)(2,1)S(1)}, u32[]{:S(2)}) copy-start(bf16[256,768]{1,0:T(8,128)(2,1)S(1)} %collective-permute-done.7.refs_3_) | copy-start | bytes 1179652
  53.7 6.5 %collective-permute-start.9 = (bf16[128,768]{1,0:T(8,128)(2,1)S(1)}, bf16[128,768]{1,0:T(8,128)(2,1)S(1)}, u32[]{:S(2)}, u32[]{:S(2)}) collective-permute-start(bf16[128,768]{1,0:T(8,128)(2,1)S(1)} %slice.9), channel_id=1, source_target_pairs={{2,0},{4,2},{6,4},{8,6},{10,8},{12,10},{14,12},{0,14},{3,1},{5,3},... | collective-permute-start | bytes 589832 | tf_op jit(solution)/shard_map/ppermute | solution.py:252
  60.2 0.7 copy-start.11
  60.8 0.7 copy-start.12
  64.0 15.7 %copy-start.1 = (bf16[16,5,8,768]{3,2,1,0:T(8,128)(2,1)}, bf16[16,5,8,768]{3,2,1,0:T(8,128)(2,1)S(1)}, u32[]{:S(2)}) copy-start(bf16[16,5,8,768]{3,2,1,0:T(8,128)(2,1)S(1)} %all-to-all-done.1.refs_1_) | copy-start | bytes 2949124
  64.0 15.7 %all-to-all-start.2 = ((bf16[16,3,8,768]{3,2,1,0:T(8,128)(2,1)}), bf16[16,3,8,768]{3,2,1,0:T(8,128)(2,1)S(1)}, u32[]{:S(2)}, u32[]{:S(2)}) async-start(bf16[16,3,8,768]{3,2,1,0:T(8,128)(2,1)} %pick_rows.3), calls=%async_computation.2 | async-start | bytes 1179648 | tf_op jit(solution)/shard_map/all_to_all | solution.py:289
  71.3 8.5 %collective-permute-start.5 = (bf16[16,5,8,768]{3,2,1,0:T(8,128)(2,1)S(1)}, bf16[16,5,8,768]{3,2,1,0:T(8,128)(2,1)S(1)}, u32[]{:S(2)}, u32[]{:S(2)}) collective-permute-start(bf16[16,5,8,768]{3,2,1,0:T(8,128)(2,1)S(1)} %all-to-all-done.1.refs_1_), channel_id=1, source_target_pairs={{0,1},{1,0},{2,3},{3,2},{4,5},{5,4},{6,7},{7,6},{8,9},{9,8},{10,11... | collective-permute-start | bytes 2949128 | tf_op jit(solution)/shard_map/ppermute | solution.py:290
  79.7 9.4 %copy-start.2 = (bf16[16,3,8,768]{3,2,1,0:T(8,128)(2,1)}, bf16[16,3,8,768]{3,2,1,0:T(8,128)(2,1)S(1)}, u32[]{:S(2)}) copy-start(bf16[16,3,8,768]{3,2,1,0:T(8,128)(2,1)S(1)} %all-to-all-done.2.refs_2_) | copy-start | bytes 1769476
  79.7 15.2 %collective-permute-start.10 = (bf16[16,3,8,768]{3,2,1,0:T(8,128)(2,1)S(1)}, bf16[16,3,8,768]{3,2,1,0:T(8,128)(2,1)}, u32[]{:S(2)}, u32[]{:S(2)}) collective-permute-start(bf16[16,3,8,768]{3,2,1,0:T(8,128)(2,1)S(1)} %all-to-all-done.2.refs_2_), channel_id=1, source_target_pairs={{0,1},{1,0},{2,3},{3,2},{4,5},{5,4},{6,7},{7,6},{8,9},{9,8},{10,11... | collective-permute-start | bytes 1769480 | tf_op jit(solution)/shard_map/ppermute | solution.py:290
  79.8 1.0 copy-start.3
  101.4 12.8 %collective-permute-start.11 = (bf16[256,1024]{1,0:T(8,128)(2,1)}, bf16[256,1024]{1,0:T(8,128)(2,1)S(1)}, u32[]{:S(2)}, u32[]{:S(2)}) collective-permute-start(bf16[256,1024]{1,0:T(8,128)(2,1)} %get-tuple-element.24), channel_id=1, source_target_pairs={{16,1},{32,17},{48,33},{64,49},{80,65},{96,81},{112,97},{128,113},... | collective-permute-start | bytes 1572872 | tf_op jit(solution)/shard_map/ppermute | solution.py:319
  114.3 0.8 copy-start.6

commit v2 on v1

--- a/solution.py
+++ b/solution.py
@@ -56,6 +56,7 @@
         in_specs=[SCALAR] + [LOCAL] * (1 + len(blocks)),
         out_specs=LOCAL,
         out_shape=jax.ShapeDtypeStruct((n_y, len(offsets), slots, width), jnp.bfloat16),
+        compiler_params=pltpu.CompilerParams(vmem_limit_bytes=10 << 20),
         name="pick_rows",
     )(at, route, *blocks)
 
@@ -112,6 +113,7 @@
         out_specs=[LOCAL] * len(outs),
         out_shape=outs,
         scratch_shapes=scratch,
+        compiler_params=pltpu.CompilerParams(vmem_limit_bytes=16 << 20),
     )(*operands)
 
 
@@ -138,7 +140,9 @@
         out_shape=[
             jax.ShapeDtypeStruct((r, width), jnp.bfloat16) for r in (rows, ext, ext)
         ],
-        compiler_params=pltpu.CompilerParams(dimension_semantics=("arbitrary",)),
+        compiler_params=pltpu.CompilerParams(
+            dimension_semantics=("arbitrary",), vmem_limit_bytes=16 << 20
+        ),
         name="near_projections",
     )(at, x, w_query, w_key, w_value)
 
@@ -148,7 +152,7 @@
 ):
     step = pl.program_id(0)
     rows_q = q_ref.shape[0]
-    chunk = 256
+    chunk = rows_q
     far = far_ref[...]
     far_k = jnp.dot(far, wk_ref[...], preferred_element_type=jnp.float32).astype(jnp.bfloat16)
     far_v = jnp.dot(far, wv_ref[...], preferred_element_type=jnp.float32).astype(jnp.bfloat16)
@@ -212,7 +216,9 @@
         out_specs=pl.BlockSpec((rows, width), lambda i: (0, 0)),
         out_shape=jax.ShapeDtypeStruct((rows, width), jnp.bfloat16),
         scratch_shapes=[pltpu.VMEM((width // 128, rows, 128), jnp.bfloat16)],
-        compiler_params=pltpu.CompilerParams(dimension_semantics=("arbitrary",)),
+        compiler_params=pltpu.CompilerParams(
+            dimension_semantics=("arbitrary",), vmem_limit_bytes=40 << 20
+        ),
         name="window_attention",
     )(q, k, v, far, w_key, w_value, bias, w_out, lifted)
 

time: 135 us -> 119 us (0.88)
  Pallas kernels: 52.8 us -> 38 us
  local copies, waits for them, and re-layouts: 8.91 us -> 5.12 us
  waiting for transfers between devices: 29.4 us -> 32 us
    pallas_call x3, Pallas kernels: 20.7 us -> 11.3 us  [local_call(): pl.pallas_call(kernel, in_specs=[SCALAR] + [LOCAL] * (len(operands) - 1),...]
    unnamed x35 -> x25, local copies, waits for them, and re-layouts: 5.01 us -> 1.96 us
    pallas_call x2, Pallas kernels: 5.37 us -> 2.89 us  [pick(): pl.pallas_call(lambda *refs: pick_kernel(offsets, n_x, *refs), in_specs=[...]
    pallas_call x1, Pallas kernels: 8.33 us -> 6.8 us  [project(): pl.pallas_call(project_kernel, grid=(width // block,), in_specs=[SCALAR,...]
    pallas_call x1, Pallas kernels: 18.4 us -> 17 us  [attention(): pl.pallas_call(attention_kernel, grid=(width // block,), in_specs=[column...]
  transfers between devices with their start and end apart: 15 -> 15, of which waited for: 8 -> 8; matrix products, arithmetic and copies ran while one was open for 5% -> 5% of each run, Pallas kernels for 21% -> 16%
where the time goes in v2:
time: 119 us; the launch traced here: 117 us
  starting transfers between devices  40.3 us (34%)
  Pallas kernels  38 us (32%)
  waiting for transfers between devices  32 us (27%)
  local copies, waits for them, and re-layouts  5.12 us (4%)
  other arithmetic  1.43 us (1%)
    ppermute x8, waiting for transfers between devices, shift(): return lax.ppermute(value, 'bevx', perm)  18.8 us
    pallas_call x1, Pallas kernels, attention(): pl.pallas_call(attention_kernel, grid=(width // block,), in_specs=[column...  17 us
    ppermute x8, starting transfers between devices, shift(): return lax.ppermute(value, 'bevx', perm)  15.8 us
    all_to_all x2, starting transfers between devices, exchange(): got = lax.all_to_all(rows, 'bevy', split_axis=0, concat_axis=0, tiled=True)  14.6 us
    pallas_call x3, Pallas kernels, local_call(): pl.pallas_call(kernel, in_specs=[SCALAR] + [LOCAL] * (len(operands) - 1),...  11.3 us
    all_to_all x2, waiting for transfers between devices, exchange(): got = lax.all_to_all(rows, 'bevy', split_axis=0, concat_axis=0, tiled=True)  8.57 us
    pallas_call x1, Pallas kernels, project(): pl.pallas_call(project_kernel, grid=(width // block,), in_specs=[SCALAR,...  6.8 us
    all_to_all x1, starting transfers between devices, steps(): lax.all_to_all(route, 'bevx', split_axis=0, concat_axis=0, tiled=True)  5.77 us
  transfers between devices with their start and end apart: 15, of which 8 were waited for; matrix products, arithmetic and copies ran while one was open for 5% of the time, Pallas kernels for 16%

profile of v2, /device:TPU:8, one launch (start us, length us, event | category | flops | bytes accessed | tf_op | source)
XLA Modules:
  0.0 117.1 jit_solution(11197317575503686808)
XLA Ops:
  0.0 1.9 %collective-permute-start = (bf16[256,768]{1,0:T(8,128)(2,1)}, bf16[256,768]{1,0:T(8,128)(2,1)S(1)}, u32[]{:S(2)}, u32[]{:S(2)}) collective-permute-start(bf16[256,768]{1,0:T(8,128)(2,1)} %refs_2_.1), channel_id=1, source_target_pairs={{0,2},{2,4},{4,6},{6,8},{8,10},{10,12},{12,14},{14,0},{1,3},{3,5},... | collective-permute-start | bytes 1179656 | tf_op jit(solution)/shard_map/ppermute | solution.py:258
  1.9 4.0 %collective-permute-start.1 = (bf16[256,768]{1,0:T(8,128)(2,1)}, bf16[256,768]{1,0:T(8,128)(2,1)S(1)}, u32[]{:S(2)}, u32[]{:S(2)}) collective-permute-start(bf16[256,768]{1,0:T(8,128)(2,1)} %refs_2_.1), channel_id=1, source_target_pairs={{2,0},{4,2},{6,4},{8,6},{10,8},{12,10},{14,12},{0,14},{3,1},{5,3},... | collective-permute-start | bytes 1179656 | tf_op jit(solution)/shard_map/ppermute | solution.py:258
  5.9 0.5 broadcast.8
  6.5 1.3 %reduce.3 = s32[128]{0:T(128)S(1)} reduce(s32[1,1,128]{2,1,0:T(1,128)} %param.15, s32[]{:T(128)} %broadcast.8), dimensions={0,1}, to_apply=%param.15.reduce_sub_computation.3 | reduce | bytes 1028 | tf_op args[4]
  7.8 0.1 lt.18
  7.9 0.8 squeeze.3
  8.7 0.1 copy.19
  8.8 0.7 reshape.26
  9.5 0.8 reshape_squeeze.3
  10.2 0.1 copy.20
  10.3 0.1 reshape.27.refs_2_.refs_3_
  10.4 5.8 %all-to-all-start = ((s32[8,1,128]{2,1,0:T(1,128)}), s32[8,1,128]{2,1,0:T(1,128)S(1)}, u32[]{:S(2)}, u32[]{:S(2)}) async-start(s32[8,1,128]{2,1,0:T(1,128)} %bitcast.5), calls=%async_computation | async-start | bytes 8192 | tf_op jit(solution)/shard_map/all_to_all | solution.py:273
  16.2 0.1 constant_dynamic-slice_fusion.1
  16.4 0.3 copy.25
  16.7 0.1 constant_dynamic-slice_fusion
  16.8 0.3 copy.26
  17.1 2.1 %collective-permute-start.2 = (bf16[256,768]{1,0:T(8,128)(2,1)S(1)}, bf16[256,768]{1,0:T(8,128)(2,1)S(1)}, u32[]{:S(2)}, u32[]{:S(2)}) collective-permute-start(bf16[256,768]{1,0:T(8,128)(2,1)S(1)} %collective-permute-done.refs_3_), channel_id=1, source_target_pairs={{0,2},{2,4},{4,6},{6,8},{8,10},{10,12},{12,14},{14,0},{1,3},{3,5},... | collective-permute-start | bytes 1179656 | tf_op jit(solution)/shard_map/ppermute | solution.py:258
  19.2 1.3 %collective-permute-start.3 = (bf16[256,768]{1,0:T(8,128)(2,1)S(1)}, bf16[256,768]{1,0:T(8,128)(2,1)S(1)}, u32[]{:S(2)}, u32[]{:S(2)}) collective-permute-start(bf16[256,768]{1,0:T(8,128)(2,1)S(1)} %collective-permute-done.1.refs_4_), channel_id=1, source_target_pairs={{2,0},{4,2},{6,4},{8,6},{10,8},{12,10},{14,12},{0,14},{3,1},{5,3},... | collective-permute-start | bytes 1179656 | tf_op jit(solution)/shard_map/ppermute | solution.py:258
  20.5 0.1 pad_add_fusion.refs_0_.at_ref
  20.6 0.2 copy.24
  20.8 0.1 pad.4.bias_ref
  20.9 3.0 %all-to-all-done = s32[8,1,128]{2,1,0:T(1,128)S(1)} async-done(((s32[8,1,128]{2,1,0:T(1,128)}), s32[8,1,128]{2,1,0:T(1,128)S(1)}, u32[]{:S(2)}, u32[]{:S(2)}) %all-to-all-start) | async-done | bytes 4128 | tf_op jit(solution)/shard_map/all_to_all | solution.py:273
  23.8 6.4 %collective-permute-done.2.refs_5_ = bf16[256,768]{1,0:T(8,128)(2,1)S(1)} collective-permute-done((bf16[256,768]{1,0:T(8,128)(2,1)S(1)}, bf16[256,768]{1,0:T(8,128)(2,1)S(1)}, u32[]{:S(2)}, u32[]{:S(2)}) %collective-permute-start.2) | collective-permute-done | bytes 393248 | tf_op jit(solution)/shard_map/ppermute | solution.py:258
  30.2 0.2 collective-permute-done.3.refs_6_
  30.4 2.0 %pick_rows.2 = bf16[16,5,8,768]{3,2,1,0:T(8,128)(2,1)} custom-call(s32[2]{0:T(128)S(1)} %pad_add_fusion.refs_0_.at_ref, s32[8,128]{1,0:T(8,128)S(1)} %bitcast.20, bf16[256,768]{1,0:T(8,128)(2,1)S(1)} %copy-done.7, bf16[256,768]{1,0:T(8,128)(2,1)S(1)} %collective-permute-done.refs_3_, bf16[256,768]{1,0:T(8,128)(2,1)S(1)} %collective-permute-done.1.refs_4_, ...), custom_call_target="tpu_custom_call" | custom-call | tf_op jit(solution)/shard_map/pick_rows/pallas_call | solution.py:54
  32.4 7.4 %all-to-all-start.1 = ((bf16[16,5,8,768]{3,2,1,0:T(8,128)(2,1)}), bf16[16,5,8,768]{3,2,1,0:T(8,128)(2,1)S(1)}, u32[]{:S(2)}, u32[]{:S(2)}) async-start(bf16[16,5,8,768]{3,2,1,0:T(8,128)(2,1)} %pick_rows.2), calls=%async_computation.1 | async-start | bytes 1966080 | tf_op jit(solution)/shard_map/all_to_all | solution.py:295
  39.8 1.5 %collective-permute-start.6 = (bf16[256,768]{1,0:T(8,128)(2,1)}, bf16[256,768]{1,0:T(8,128)(2,1)S(1)}, u32[]{:S(2)}, u32[]{:S(2)}) collective-permute-start(bf16[256,768]{1,0:T(8,128)(2,1)} %copy-done.9), channel_id=1, source_target_pairs={{0,2},{2,4},{4,6},{6,8},{8,10},{10,12},{12,14},{14,0},{1,3},{3,5},... | collective-permute-start | bytes 1179656 | tf_op jit(solution)/shard_map/ppermute | solution.py:258
  41.4 1.8 %collective-permute-start.7 = (bf16[256,768]{1,0:T(8,128)(2,1)}, bf16[256,768]{1,0:T(8,128)(2,1)S(1)}, u32[]{:S(2)}, u32[]{:S(2)}) collective-permute-start(bf16[256,768]{1,0:T(8,128)(2,1)} %copy-done.8), channel_id=1, source_target_pairs={{2,0},{4,2},{6,4},{8,6},{10,8},{12,10},{14,12},{0,14},{3,1},{5,3},... | collective-permute-start | bytes 1179656 | tf_op jit(solution)/shard_map/ppermute | solution.py:258
  43.1 8.3 %collective-permute-done.6.refs_2_ = bf16[256,768]{1,0:T(8,128)(2,1)S(1)} collective-permute-done((bf16[256,768]{1,0:T(8,128)(2,1)}, bf16[256,768]{1,0:T(8,128)(2,1)S(1)}, u32[]{:S(2)}, u32[]{:S(2)}) %collective-permute-start.6) | collective-permute-done | bytes 393248 | tf_op jit(solution)/shard_map/ppermute | solution.py:258
  51.5 0.3 collective-permute-start.8
  51.8 0.3 collective-permute-done.7.refs_3_
  52.1 2.8 %collective-permute-start.9 = (bf16[128,768]{1,0:T(8,128)(2,1)S(1)}, bf16[128,768]{1,0:T(8,128)(2,1)S(1)}, u32[]{:S(2)}, u32[]{:S(2)}) collective-permute-start(bf16[128,768]{1,0:T(8,128)(2,1)S(1)} %slice.9), channel_id=1, source_target_pairs={{2,0},{4,2},{6,4},{8,6},{10,8},{12,10},{14,12},{0,14},{3,1},{5,3},... | collective-permute-start | bytes 589832 | tf_op jit(solution)/shard_map/ppermute | solution.py:258
  54.9 3.5 %collective-permute-done.8.refs_4_ = bf16[128,768]{1,0:T(8,128)(2,1)S(1)} collective-permute-done((bf16[128,768]{1,0:T(8,128)(2,1)S(1)}, bf16[128,768]{1,0:T(8,128)(2,1)S(1)}, u32[]{:S(2)}, u32[]{:S(2)}) %collective-permute-start.8) | collective-permute-done | bytes 196640 | tf_op jit(solution)/shard_map/ppermute | solution.py:258
  58.4 0.0 collective-permute-done.9.refs_5_
  58.5 0.9 pick_rows.3
  59.4 0.8 copy-done.4
  60.2 7.2 %all-to-all-start.2 = ((bf16[16,3,8,768]{3,2,1,0:T(8,128)(2,1)}), bf16[16,3,8,768]{3,2,1,0:T(8,128)(2,1)}, u32[]{:S(2)}, u32[]{:S(2)}) async-start(bf16[16,3,8,768]{3,2,1,0:T(8,128)(2,1)} %copy-done.4), calls=%async_computation.2 | async-start | bytes 1179648 | tf_op jit(solution)/shard_map/all_to_all | solution.py:295
  67.5 8.6 %all-to-all-done.2.refs_2_ = bf16[16,3,8,768]{3,2,1,0:T(8,128)(2,1)} async-done(((bf16[16,3,8,768]{3,2,1,0:T(8,128)(2,1)}), bf16[16,3,8,768]{3,2,1,0:T(8,128)(2,1)}, u32[]{:S(2)}, u32[]{:S(2)}) %all-to-all-start.2) | async-done | bytes 589856 | tf_op jit(solution)/shard_map/all_to_all | solution.py:295
  76.1 5.9 %shard_map.109.refs_1_ = f32[768,1024]{1,0:T(8,128)S(1)} custom-call(s32[2]{0:T(128)S(1)} %pad_add_fusion.refs_0_.at_ref, bf16[16,5,8,768]{3,2,1,0:T(8,128)(2,1)S(1)} %all-to-all-done.1.refs_1_, s32[8,128]{1,0:T(8,128)S(1)} %reshape.27.refs_2_.refs_3_, bf16[16,5,8,768]{3,2,1,0:T(8,128)(2,1)} %collective-permute-done.5.refs_3_, ...), custom_call_target="tpu_custom_call" | custom-call | tf_op jit(solution)/shard_map/pallas_call | solution.py:110
  81.9 0.0 copy-start.10
  81.9 0.0 copy-start.6
  82.0 2.8 %shard_map.110.refs_1_ = f32[768,1024]{1,0:T(8,128)S(1)} custom-call(s32[2]{0:T(128)S(1)} %pad_add_fusion.refs_0_.at_ref, f32[768,1024]{1,0:T(8,128)S(1)} %shard_map.109.refs_1_, bf16[16,3,8,768]{3,2,1,0:T(8,128)(2,1)} %all-to-all-done.2.refs_2_, s32[8,128]{1,0:T(8,128)S(1)} %reshape.27.refs_2_.refs_3_, bf16[768,1024]{1,0:T(8,128)(2,1)S(1)} %copy-done.1), custom_call_target="tpu_custom_call" | custom-call | tf_op jit(solution)/shard_map/pallas_call | solution.py:110
  84.8 0.0 copy-start.3
  84.8 2.6 %shard_map.111 = (f32[512,1024]{1,0:T(8,128)S(1)}, bf16[768,1024]{1,0:T(8,128)(2,1)S(1)}, bf16[256,1024]{1,0:T(8,128)(2,1)S(1)}) custom-call(s32[2]{0:T(128)S(1)} %pad_add_fusion.refs_0_.at_ref, f32[768,1024]{1,0:T(8,128)S(1)} %shard_map.110.refs_1_, bf16[16,3,8,768]{3,2,1,0:T(8,128)(2,1)S(1)} %collective-permute-done.10.refs_2_, ...), custom_call_target="tpu_custom_call" | custom-call | tf_op jit(solution)/shard_map/pallas_call | solution.py:110
  87.5 4.1 %collective-permute-start.11 = (bf16[256,1024]{1,0:T(8,128)(2,1)S(1)}, bf16[256,1024]{1,0:T(8,128)(2,1)S(1)}, u32[]{:S(2)}, u32[]{:S(2)}) collective-permute-start(bf16[256,1024]{1,0:T(8,128)(2,1)S(1)} %get-tuple-element.24), channel_id=1, source_target_pairs={{16,1},{32,17},{48,33},{64,49},{80,65},{96,81},{112,97},{128,113},... | collective-permute-start | bytes 1572872 | tf_op jit(solution)/shard_map/ppermute | solution.py:325
  91.6 6.8 %near_projections.1 = (bf16[512,1024]{1,0:T(8,128)(2,1)S(1)}, bf16[768,1024]{1,0:T(8,128)(2,1)S(1)}, bf16[768,1024]{1,0:T(8,128)(2,1)S(1)}) custom-call(s32[2]{0:T(128)S(1)} %pad_add_fusion.refs_0_.at_ref, bf16[768,1024]{1,0:T(8,128)(2,1)S(1)} %get-tuple-element.20.x_ref, bf16[1024,1024]{1,0:T(8,128)(2,1)S(1)} %copy-done.6, ...), custom_call_target="tpu_custom_call" | custom-call | tf_op jit(solution)/shard_map/near_projections/pallas_call | solution.py:135
  98.4 1.7 %collective-permute-done.11.far_ref = bf16[256,1024]{1,0:T(8,128)(2,1)S(1)} collective-permute-done((bf16[256,1024]{1,0:T(8,128)(2,1)S(1)}, bf16[256,1024]{1,0:T(8,128)(2,1)S(1)}, u32[]{:S(2)}, u32[]{:S(2)}) %collective-permute-start.11) | collective-permute-done | bytes 524320 | tf_op jit(solution)/shard_map/ppermute | solution.py:325
  100.1 17.0 %window_attention.1 = bf16[512,1024]{1,0:T(8,128)(2,1)} custom-call(bf16[512,1024]{1,0:T(8,128)(2,1)S(1)} %get-tuple-element.21.q_ref, bf16[768,1024]{1,0:T(8,128)(2,1)S(1)} %get-tuple-element.22.k_ref, bf16[768,1024]{1,0:T(8,128)(2,1)S(1)} %get-tuple-element.23.v_ref, bf16[256,1024]{1,0:T(8,128)(2,1)S(1)} %collective-permute-done.11.far_ref, ...), custom_call_target="tpu_custom_call" | custom-call | tf_op jit(solution)/shard_map/window_attention/pallas_call | solution.py:202
  (32 shorter events, 0.1 us)
Async XLA Ops:
  0.0 16.2 %copy-start = (bf16[256,64,16]{0,2,1:T(8,128)(2,1)S(1)}, bf16[256,64,16]{0,2,1:T(8,128)(2,1)}, u32[]{:S(2)}) copy-start(bf16[256,64,16]{0,2,1:T(8,128)(2,1)} %param.21) | copy-start | bytes 1572868
  0.0 30.4 %copy-start.7 = (bf16[256,768]{1,0:T(8,128)(2,1)S(1)}, bf16[256,768]{1,0:T(8,128)(2,1)}, u32[]{:S(2)}) copy-start(bf16[256,768]{1,0:T(8,128)(2,1)} %refs_2_.1) | copy-start | bytes 1179652
  0.0 17.1 %collective-permute-start = (bf16[256,768]{1,0:T(8,128)(2,1)}, bf16[256,768]{1,0:T(8,128)(2,1)S(1)}, u32[]{:S(2)}, u32[]{:S(2)}) collective-permute-start(bf16[256,768]{1,0:T(8,128)(2,1)} %refs_2_.1), channel_id=1, source_target_pairs={{0,2},{2,4},{4,6},{6,8},{8,10},{10,12},{12,14},{14,0},{1,3},{3,5},... | collective-permute-start | bytes 1179656 | tf_op jit(solution)/shard_map/ppermute | solution.py:258
  1.9 17.3 %collective-permute-start.1 = (bf16[256,768]{1,0:T(8,128)(2,1)}, bf16[256,768]{1,0:T(8,128)(2,1)S(1)}, u32[]{:S(2)}, u32[]{:S(2)}) collective-permute-start(bf16[256,768]{1,0:T(8,128)(2,1)} %refs_2_.1), channel_id=1, source_target_pairs={{2,0},{4,2},{6,4},{8,6},{10,8},{12,10},{14,12},{0,14},{3,1},{5,3},... | collective-permute-start | bytes 1179656 | tf_op jit(solution)/shard_map/ppermute | solution.py:258
  10.4 13.4 %all-to-all-start = ((s32[8,1,128]{2,1,0:T(1,128)}), s32[8,1,128]{2,1,0:T(1,128)S(1)}, u32[]{:S(2)}, u32[]{:S(2)}) async-start(s32[8,1,128]{2,1,0:T(1,128)} %bitcast.5), calls=%async_computation | async-start | bytes 8192 | tf_op jit(solution)/shard_map/all_to_all | solution.py:273
  16.2 16.2 %collective-permute-start.4 = (s32[8,128]{1,0:T(8,128)S(1)}, s32[8,128]{1,0:T(8,128)S(1)}, u32[]{:S(2)}, u32[]{:S(2)}) collective-permute-start(s32[8,128]{1,0:T(8,128)S(1)} %reshape.27.refs_2_.refs_3_), channel_id=1, source_target_pairs={{0,1},{1,0},{2,3},{3,2},{4,5},{5,4},{6,7},{7,6},{8,9},{9,8},{10,11... | collective-permute-start | bytes 12296 | tf_op jit(solution)/shard_map/ppermute | solution.py:272
  17.1 13.1 %collective-permute-start.2 = (bf16[256,768]{1,0:T(8,128)(2,1)S(1)}, bf16[256,768]{1,0:T(8,128)(2,1)S(1)}, u32[]{:S(2)}, u32[]{:S(2)}) collective-permute-start(bf16[256,768]{1,0:T(8,128)(2,1)S(1)} %collective-permute-done.refs_3_), channel_id=1, source_target_pairs={{0,2},{2,4},{4,6},{6,8},{8,10},{10,12},{12,14},{14,0},{1,3},{3,5},... | collective-permute-start | bytes 1179656 | tf_op jit(solution)/shard_map/ppermute | solution.py:258
  19.2 11.2 %collective-permute-start.3 = (bf16[256,768]{1,0:T(8,128)(2,1)S(1)}, bf16[256,768]{1,0:T(8,128)(2,1)S(1)}, u32[]{:S(2)}, u32[]{:S(2)}) collective-permute-start(bf16[256,768]{1,0:T(8,128)(2,1)S(1)} %collective-permute-done.1.refs_4_), channel_id=1, source_target_pairs={{2,0},{4,2},{6,4},{8,6},{10,8},{12,10},{14,12},{0,14},{3,1},{5,3},... | collective-permute-start | bytes 1179656 | tf_op jit(solution)/shard_map/ppermute | solution.py:258
  30.2 2.2 %copy-start.9 = (bf16[256,768]{1,0:T(8,128)(2,1)}, bf16[256,768]{1,0:T(8,128)(2,1)S(1)}, u32[]{:S(2)}) copy-start(bf16[256,768]{1,0:T(8,128)(2,1)S(1)} %collective-permute-done.2.refs_5_) | copy-start | bytes 1179652
  30.4 2.0 %copy-start.8 = (bf16[256,768]{1,0:T(8,128)(2,1)}, bf16[256,768]{1,0:T(8,128)(2,1)S(1)}, u32[]{:S(2)}) copy-start(bf16[256,768]{1,0:T(8,128)(2,1)S(1)} %collective-permute-done.3.refs_6_) | copy-start | bytes 1179652
  32.4 27.8 %all-to-all-start.1 = ((bf16[16,5,8,768]{3,2,1,0:T(8,128)(2,1)}), bf16[16,5,8,768]{3,2,1,0:T(8,128)(2,1)S(1)}, u32[]{:S(2)}, u32[]{:S(2)}) async-start(bf16[16,5,8,768]{3,2,1,0:T(8,128)(2,1)} %pick_rows.2), calls=%async_computation.1 | async-start | bytes 1966080 | tf_op jit(solution)/shard_map/all_to_all | solution.py:295
  39.8 36.2 %copy-start.1 = (bf16[768,1024]{1,0:T(8,128)(2,1)S(1)}, bf16[768,1024]{1,0:T(8,128)(2,1)}, u32[]{:S(2)}) copy-start(bf16[768,1024]{1,0:T(8,128)(2,1)} %refs_4_.3) | copy-start | bytes 4718596
  39.8 11.6 %collective-permute-start.6 = (bf16[256,768]{1,0:T(8,128)(2,1)}, bf16[256,768]{1,0:T(8,128)(2,1)S(1)}, u32[]{:S(2)}, u32[]{:S(2)}) collective-permute-start(bf16[256,768]{1,0:T(8,128)(2,1)} %copy-done.9), channel_id=1, source_target_pairs={{0,2},{2,4},{4,6},{6,8},{8,10},{10,12},{12,14},{14,0},{1,3},{3,5},... | collective-permute-start | bytes 1179656 | tf_op jit(solution)/shard_map/ppermute | solution.py:258
  41.4 10.7 %collective-permute-start.7 = (bf16[256,768]{1,0:T(8,128)(2,1)}, bf16[256,768]{1,0:T(8,128)(2,1)S(1)}, u32[]{:S(2)}, u32[]{:S(2)}) collective-permute-start(bf16[256,768]{1,0:T(8,128)(2,1)} %copy-done.8), channel_id=1, source_target_pairs={{2,0},{4,2},{6,4},{8,6},{10,8},{12,10},{14,12},{0,14},{3,1},{5,3},... | collective-permute-start | bytes 1179656 | tf_op jit(solution)/shard_map/ppermute | solution.py:258
  51.5 7.0 %collective-permute-start.8 = (bf16[128,768]{1,0:T(8,128)(2,1)S(1)}, bf16[128,768]{1,0:T(8,128)(2,1)S(1)}, u32[]{:S(2)}, u32[]{:S(2)}) collective-permute-start(bf16[128,768]{1,0:T(8,128)(2,1)S(1)} %slice.8), channel_id=1, source_target_pairs={{0,2},{2,4},{4,6},{6,8},{8,10},{10,12},{12,14},{14,0},{1,3},{3,5},... | collective-permute-start | bytes 589832 | tf_op jit(solution)/shard_map/ppermute | solution.py:258
  52.1 6.4 %collective-permute-start.9 = (bf16[128,768]{1,0:T(8,128)(2,1)S(1)}, bf16[128,768]{1,0:T(8,128)(2,1)S(1)}, u32[]{:S(2)}, u32[]{:S(2)}) collective-permute-start(bf16[128,768]{1,0:T(8,128)(2,1)S(1)} %slice.9), channel_id=1, source_target_pairs={{2,0},{4,2},{6,4},{8,6},{10,8},{12,10},{14,12},{0,14},{3,1},{5,3},... | collective-permute-start | bytes 589832 | tf_op jit(solution)/shard_map/ppermute | solution.py:258
  59.4 0.8 copy-start.4
  60.2 15.8 %all-to-all-start.2 = ((bf16[16,3,8,768]{3,2,1,0:T(8,128)(2,1)}), bf16[16,3,8,768]{3,2,1,0:T(8,128)(2,1)}, u32[]{:S(2)}, u32[]{:S(2)}) async-start(bf16[16,3,8,768]{3,2,1,0:T(8,128)(2,1)} %copy-done.4), calls=%async_computation.2 | async-start | bytes 1179648 | tf_op jit(solution)/shard_map/all_to_all | solution.py:295
  67.5 8.6 %collective-permute-start.5 = (bf16[16,5,8,768]{3,2,1,0:T(8,128)(2,1)S(1)}, bf16[16,5,8,768]{3,2,1,0:T(8,128)(2,1)}, u32[]{:S(2)}, u32[]{:S(2)}) collective-permute-start(bf16[16,5,8,768]{3,2,1,0:T(8,128)(2,1)S(1)} %all-to-all-done.1.refs_1_), channel_id=1, source_target_pairs={{0,1},{1,0},{2,3},{3,2},{4,5},{5,4},{6,7},{7,6},{8,9},{9,8},{10,11... | collective-permute-start | bytes 2949128 | tf_op jit(solution)/shard_map/ppermute | solution.py:296
  76.0 8.7 %collective-permute-start.10 = (bf16[16,3,8,768]{3,2,1,0:T(8,128)(2,1)}, bf16[16,3,8,768]{3,2,1,0:T(8,128)(2,1)S(1)}, u32[]{:S(2)}, u32[]{:S(2)}) collective-permute-start(bf16[16,3,8,768]{3,2,1,0:T(8,128)(2,1)} %all-to-all-done.2.refs_2_), channel_id=1, source_target_pairs={{0,1},{1,0},{2,3},{3,2},{4,5},{5,4},{6,7},{7,6},{8,9},{9,8},{10,11... | collective-permute-start | bytes 1769480 | tf_op jit(solution)/shard_map/ppermute | solution.py:296
  81.9 2.9 %copy-start.10 = (f32[1024]{0:T(1024)S(1)}, f32[1024]{0:T(1024)}, u32[]{:S(2)}) copy-start(f32[1024]{0:T(1024)} %param.16) | copy-start | bytes 12292
  81.9 9.6 %copy-start.6 = (bf16[1024,1024]{1,0:T(8,128)(2,1)S(1)}, bf16[1024,1024]{1,0:T(8,128)(2,1)}, u32[]{:S(2)}) copy-start(bf16[1024,1024]{1,0:T(8,128)(2,1)} %wq_ref.1) | copy-start | bytes 6291460
  84.8 6.8 %copy-start.2 = (bf16[1024,1024]{1,0:T(8,128)(2,1)S(1)}, bf16[1024,1024]{1,0:T(8,128)(2,1)}, u32[]{:S(2)}) copy-start(bf16[1024,1024]{1,0:T(8,128)(2,1)} %wk_ref.3) | copy-start | bytes 6291460
  84.8 6.8 %copy-start.3 = (bf16[1024,1024]{1,0:T(8,128)(2,1)S(1)}, bf16[1024,1024]{1,0:T(8,128)(2,1)}, u32[]{:S(2)}) copy-start(bf16[1024,1024]{1,0:T(8,128)(2,1)} %wv_ref.3) | copy-start | bytes 6291460
  87.5 12.6 %collective-permute-start.11 = (bf16[256,1024]{1,0:T(8,128)(2,1)S(1)}, bf16[256,1024]{1,0:T(8,128)(2,1)S(1)}, u32[]{:S(2)}, u32[]{:S(2)}) collective-permute-start(bf16[256,1024]{1,0:T(8,128)(2,1)S(1)} %get-tuple-element.24), channel_id=1, source_target_pairs={{16,1},{32,17},{48,33},{64,49},{80,65},{96,81},{112,97},{128,113},... | collective-permute-start | bytes 1572872 | tf_op jit(solution)/shard_map/ppermute | solution.py:325
  91.6 8.5 %copy-start.5 = (bf16[1024,1024]{1,0:T(8,128)(2,1)S(1)}, bf16[1024,1024]{1,0:T(8,128)(2,1)}, u32[]{:S(2)}) copy-start(bf16[1024,1024]{1,0:T(8,128)(2,1)} %wo_ref.1) | copy-start | bytes 6291460

commit v3 on v2

--- a/solution.py
+++ b/solution.py
@@ -10,12 +10,9 @@
 COLS_DEV = 64
 HALO = 4
 MASKED = -1e30
+HEAD_LANES = 16
 EARLY = (0, -1, 1, -2, 2)
 LATE = (-3, 3, 4)
-
-
-def whole(x):
-    return pl.BlockSpec(x.shape, lambda *_: (0,) * x.ndim)
 
 
 SCALAR = pl.BlockSpec(memory_space=pltpu.SMEM)
@@ -61,7 +58,7 @@
     )(at, route, *blocks)
 
 
-def summed(offsets, n_x, at_ref, pairs, w_ref, total):
+def summed(offsets, n_x, at_ref, pairs, w_ref, total, ready=None):
     for rows_ref, cell_ref in pairs:
         pieces = []
         hots = []
@@ -75,19 +72,28 @@
         projected = jnp.dot(
             jnp.concatenate(pieces, axis=0), w_ref[...], preferred_element_type=jnp.float32
         ).astype(jnp.bfloat16)
-        total[...] += jnp.dot(
+        added = jnp.dot(
             jnp.concatenate(hots, axis=1), projected, preferred_element_type=jnp.float32
         )
-
-
-def first_sum_kernel(n_x, at_ref, a_ref, ac_ref, b_ref, bc_ref, w_ref, out_ref):
+        if ready is not None:
+            ready()
+        total[...] += added
+
+
+def first_sum_kernel(n_x, at_ref, a_ref, ac_ref, w_ref, out_ref):
     out_ref[...] = jnp.zeros_like(out_ref)
-    summed(EARLY, n_x, at_ref, ((a_ref, ac_ref), (b_ref, bc_ref)), w_ref, out_ref)
-
-
-def next_sum_kernel(n_x, at_ref, total_ref, a_ref, ac_ref, w_ref, out_ref):
+    summed(EARLY, n_x, at_ref, ((a_ref, ac_ref),), w_ref, out_ref)
+
+
+def second_sum_kernel(n_x, at_ref, total_ref, a_ref, ac_ref, w_ref, out_ref):
     out_ref[...] = total_ref[...]
-    summed(LATE, n_x, at_ref, ((a_ref, ac_ref),), w_ref, out_ref)
+    summed(EARLY, n_x, at_ref, ((a_ref, ac_ref),), w_ref, out_ref)
+
+
+def next_sum_kernel(n_x, at_ref, total_ref, a_ref, ac_ref, w_ref, out_ref, sem):
+    copy = pltpu.make_async_copy(total_ref, out_ref, sem)
+    copy.start()
+    summed(LATE, n_x, at_ref, ((a_ref, ac_ref),), w_ref, out_ref, copy.wait)
 
 
 def last_sum_kernel(
@@ -106,15 +112,23 @@
     sent_ref[...] = normed_ref[pl.ds(pl.multiple_of(2 * at_ref[1], edge), edge), :]
 
 
-def local_call(kernel, operands, outs, scratch=()):
+def local_call(kernel, operands, outs, scratch=(), remote=()):
     return pl.pallas_call(
         kernel,
-        in_specs=[SCALAR] + [LOCAL] * (len(operands) - 1),
+        in_specs=[SCALAR]
+        + [
+            pl.BlockSpec(memory_space=pltpu.HBM) if i in remote else LOCAL
+            for i in range(1, len(operands))
+        ],
         out_specs=[LOCAL] * len(outs),
         out_shape=outs,
         scratch_shapes=scratch,
         compiler_params=pltpu.CompilerParams(vmem_limit_bytes=16 << 20),
     )(*operands)
+
+
+def flipped(w, x):
+    return jnp.dot(x, w, preferred_element_type=jnp.float32).T
 
 
 def project_kernel(at_ref, x_ref, wq_ref, wk_ref, wv_ref, q_ref, k_ref, v_ref):
@@ -125,99 +139,119 @@
         jnp.bfloat16
     )
     k_ref[...] = jnp.dot(x, wk_ref[...], preferred_element_type=jnp.float32).astype(jnp.bfloat16)
-    v_ref[...] = jnp.dot(x, wv_ref[...], preferred_element_type=jnp.float32).astype(jnp.bfloat16)
+    v_ref[...] = flipped(wv_ref[...], x).astype(jnp.bfloat16)
 
 
 def project(at, x, w_query, w_key, w_value, rows):
     ext, width = x.shape
-    block = 256
-    column = lambda r: pl.BlockSpec((r, block), lambda i: (0, i))
     return pl.pallas_call(
         project_kernel,
-        grid=(width // block,),
-        in_specs=[SCALAR, whole(x)] + [column(width)] * 3,
-        out_specs=[column(rows), column(ext), column(ext)],
+        in_specs=[SCALAR] + [LOCAL] * 4,
+        out_specs=[LOCAL] * 3,
         out_shape=[
-            jax.ShapeDtypeStruct((r, width), jnp.bfloat16) for r in (rows, ext, ext)
+            jax.ShapeDtypeStruct(shape, jnp.bfloat16)
+            for shape in ((rows, width), (ext, width), (width, ext))
         ],
-        compiler_params=pltpu.CompilerParams(
-            dimension_semantics=("arbitrary",), vmem_limit_bytes=16 << 20
-        ),
+        compiler_params=pltpu.CompilerParams(vmem_limit_bytes=24 << 20),
         name="near_projections",
     )(at, x, w_query, w_key, w_value)
 
 
 def attention_kernel(
-    q_ref, k_ref, v_ref, far_ref, wk_ref, wv_ref, bias_ref, wo_ref, lifted_ref, out_ref, att_ref
+    q_ref, k_ref, v_ref, far_ref, wk_ref, wv_ref, bias_ref, wo_ref, lifted_ref, out_ref, att_ref,
+    far_k_ref, far_v_ref,
 ):
     step = pl.program_id(0)
     rows_q = q_ref.shape[0]
-    chunk = rows_q
+    size = 64
+    heads = att_ref.shape[1] // size
+    here = pl.ds(pl.multiple_of(step * att_ref.shape[1], 256), att_ref.shape[1])
+    q_ref = q_ref.at[:, here]
+    k_ref = k_ref.at[:, here]
+    v_ref = v_ref.at[here, :]
+    wk_ref = wk_ref.at[:, here]
+    wv_ref = wv_ref.at[:, here]
     far = far_ref[...]
-    far_k = jnp.dot(far, wk_ref[...], preferred_element_type=jnp.float32).astype(jnp.bfloat16)
-    far_v = jnp.dot(far, wv_ref[...], preferred_element_type=jnp.float32).astype(jnp.bfloat16)
-    lane = lax.broadcasted_iota(jnp.int32, (chunk, 128), 1)
-    for pair in range(2):
-        cut = slice(pair * 128, pair * 128 + 128)
-        k = jnp.concatenate([k_ref[:, cut], far_k[:, cut]], axis=0)
-        v = jnp.concatenate([v_ref[:, cut], far_v[:, cut]], axis=0)
+    far_k_ref[...] = jnp.dot(far, wk_ref[...], preferred_element_type=jnp.float32).astype(
+        jnp.bfloat16
+    )
+    far_v_ref[...] = flipped(wv_ref[...], far).astype(jnp.bfloat16)
+    lane = lax.broadcasted_iota(jnp.int32, (rows_q, 128), 1)
+    tops = jnp.max(bias_ref[...].astype(jnp.float32), axis=0, keepdims=True)
+    lane_top = lax.broadcasted_iota(jnp.int32, tops.shape, 1)
+
+    def scored(head, pair, side):
+        cut = pl.ds(pair * 128, 128)
+        k = jnp.concatenate([k_ref[:, cut], far_k_ref[:, cut]], axis=0)
         keys = jnp.concatenate([k, bias_ref[...]], axis=1)
-        values = jnp.concatenate([v, jnp.ones_like(v)], axis=1)
-        for start in range(0, rows_q, chunk):
-            q = q_ref[start : start + chunk, cut] * jnp.asarray(0.125, jnp.bfloat16)
-            done = []
-            for side in range(2):
-                own = (lane >= 64) if side else (lane < 64)
-                query = jnp.concatenate(
-                    [
-                        jnp.where(own, q, jnp.zeros((), jnp.bfloat16)),
-                        jnp.where(lane == 4 * step + 2 * pair + side, 1.0, 0.0).astype(
-                            jnp.bfloat16
-                        ),
-                    ],
-                    axis=1,
-                )
-                score = lax.dot_general(
-                    query, keys, (((1,), (1,)), ((), ())), preferred_element_type=jnp.float32
-                )
-                top = jnp.max(score, axis=1, keepdims=True)
-                weight = jnp.exp(score - top).astype(jnp.bfloat16)
-                total = jnp.dot(weight, values, preferred_element_type=jnp.float32)
-                done.append(total[:, :128] / total[:, 128:])
-            att_ref[2 * step + pair, start : start + chunk] = jnp.where(
-                lane < 64, done[0], done[1]
-            ).astype(jnp.bfloat16)
+        q = q_ref[:, cut] * jnp.asarray(0.125, jnp.bfloat16)
+        mine = (lane // size) == side
+        number = heads * step + head
+        top = jnp.max(jnp.where(lane_top == number, tops, -jnp.inf), axis=1, keepdims=True)
+        extra = jnp.where(lane == number, 1.0, jnp.where(lane == HEAD_LANES, -top, 0.0))
+        query = jnp.concatenate(
+            [jnp.where(mine, q, jnp.zeros((), jnp.bfloat16)), extra.astype(jnp.bfloat16)],
+            axis=1,
+        )
+        return lax.dot_general(
+            keys, query, (((1,), (1,)), ((), ())), preferred_element_type=jnp.float32
+        )
+
+    def weighed(own, weight):
+        v = jnp.concatenate([v_ref[own, :], far_v_ref[own, :]], axis=1)
+        values = jnp.concatenate([v, jnp.ones((16, v.shape[1]), jnp.bfloat16)], axis=0)
+        mixed = jnp.dot(values, weight, preferred_element_type=jnp.float32)
+        total = mixed[size : size + 1]
+        att_ref[step, own, :] = (mixed[:size] / total).astype(jnp.bfloat16)
+        return total
+
+    least = most = None
+    scores = [scored(0, 0, 0)]
+    for head in range(heads):
+        if head + 1 < heads:
+            scores.append(scored(head + 1, (head + 1) // 2, (head + 1) % 2))
+        total = weighed(
+            slice(head * size, head * size + size), jnp.exp(scores[head]).astype(jnp.bfloat16)
+        )
+        least = total if head == 0 else jnp.minimum(least, total)
+        most = total if head == 0 else jnp.maximum(most, total)
+    safe = (jnp.min(least) > 1e-18) & (jnp.max(most) < 1e30)
+
+    @pl.when(jnp.logical_not(safe))
+    def _():
+        def again(head, carry):
+            score = scored(head, head // 2, head % 2)
+            weight = jnp.exp(score - jnp.max(score, axis=0, keepdims=True)).astype(jnp.bfloat16)
+            weighed(pl.ds(pl.multiple_of(head * size, size), size), weight)
+            return carry
+
+        lax.fori_loop(0, heads, again, 0)
 
     @pl.when(step == pl.num_programs(0) - 1)
     def _():
-        attended = jnp.concatenate([att_ref[i] for i in range(att_ref.shape[0])], axis=1)
-        mixed = jnp.dot(attended, wo_ref[...], preferred_element_type=jnp.float32)
+        attended = att_ref[...].reshape(-1, rows_q)
+        mixed = lax.dot_general(
+            attended, wo_ref[...], (((0,), (0,)), ((), ())), preferred_element_type=jnp.float32
+        )
         out_ref[...] = (lifted_ref[...] + mixed).astype(jnp.bfloat16)
 
 
 def attention(q, k, v, far, w_key, w_value, bias, w_out, lifted):
     rows, width = q.shape
     block = 256
-    column = lambda x: pl.BlockSpec((x.shape[0], block), lambda i: (0, i))
     return pl.pallas_call(
         attention_kernel,
         grid=(width // block,),
-        in_specs=[
-            column(q),
-            column(k),
-            column(v),
-            whole(far),
-            column(w_key),
-            column(w_value),
-            whole(bias),
-            whole(w_out),
-            whole(lifted),
+        in_specs=[LOCAL] * 9,
+        out_specs=LOCAL,
+        out_shape=jax.ShapeDtypeStruct((rows, width), jnp.bfloat16),
+        scratch_shapes=[
+            pltpu.VMEM((width // block, block, rows), jnp.bfloat16),
+            pltpu.VMEM((far.shape[0], block), jnp.bfloat16),
+            pltpu.VMEM((block, far.shape[0]), jnp.bfloat16),
         ],
-        out_specs=pl.BlockSpec((rows, width), lambda i: (0, 0)),
-        out_shape=jax.ShapeDtypeStruct((rows, width), jnp.bfloat16),
-        scratch_shapes=[pltpu.VMEM((width // 128, rows, 128), jnp.bfloat16)],
         compiler_params=pltpu.CompilerParams(
-            dimension_semantics=("arbitrary",), vmem_limit_bytes=40 << 20
+            dimension_semantics=("arbitrary",), vmem_limit_bytes=28 << 20
         ),
         name="window_attention",
     )(q, k, v, far, w_key, w_value, bias, w_out, lifted)
@@ -289,7 +323,8 @@
     )
     far_bias = jnp.where(far_ok, far_bias, jnp.asarray(MASKED, jnp.bfloat16))
     bias = jnp.concatenate([near_bias, far_bias], axis=0).reshape(-1, head_count)
-    bias = jnp.pad(bias, ((0, 0), (0, 128 - head_count)))
+    bias = jnp.pad(bias, ((0, 0), (0, 1)), constant_values=1)
+    bias = jnp.pad(bias, ((0, 0), (0, 127 - head_count)))
 
     def exchange(rows):
         got = lax.all_to_all(rows, "bevy", split_axis=0, concat_axis=0, tiled=True)
@@ -300,14 +335,27 @@
     early, early_other = exchange(rows)
     total = jax.ShapeDtypeStruct((ext, width), jnp.float32)
     [lifted] = local_call(
-        lambda *refs: first_sum_kernel(n_x, *refs),
-        (at, early, cells, early_other, cells_other, lift_weight),
+        lambda *refs: first_sum_kernel(n_x, *refs), (at, early, cells, lift_weight), [total]
+    )
+    [lifted] = local_call(
+        lambda *refs: second_sum_kernel(n_x, *refs),
+        (at, lifted, early_other, cells_other, lift_weight),
         [total],
     )
     rows = pick(LATE, n_x, n_y, at, route, (u3, d3, u4, d4))
     late, late_other = exchange(rows)
     [lifted] = local_call(
-        lambda *refs: next_sum_kernel(n_x, *refs), (at, lifted, late, cells, lift_weight), [total]
+        lambda *refs: next_sum_kernel(n_x, *refs),
+        (
+            at,
+            pltpu.with_memory_space_constraint(lifted, pltpu.HBM),
+            late,
+            cells,
+            lift_weight,
+        ),
+        [total],
+        [pltpu.SemaphoreType.DMA],
+        (1,),
     )
     own_lifted, normed, sent = local_call(
         lambda *refs: last_sum_kernel(n_x, edge, *refs),

time: 119 us -> 118 us (level)
  Pallas kernels: 38 us -> 33.5 us
  local copies, waits for them, and re-layouts: 5.12 us -> 6.69 us
    pallas_call x5 -> x6, Pallas kernels: 35.1 us -> 30.6 us  [the longest x4 13.1 us: local_call(): pl.pallas_call(kernel, in_specs=[SCALAR] + [pl.BlockSpec(memory_space=plt...]
    unnamed x25 -> x27, local copies, waits for them, and re-layouts: 1.96 us -> 3.59 us
    ppermute x1, waiting for transfers between devices: 1.67 us -> 3.13 us  [steps(): far = lax.ppermute(sent, ('bevy', 'cam'), hops)]
where the time goes in v3:
time: 118 us; the launch traced here: 115 us
  starting transfers between devices  40.5 us (34%)
  Pallas kernels  33.5 us (28%)
  waiting for transfers between devices  33 us (28%)
  local copies, waits for them, and re-layouts  6.69 us (6%)
  other arithmetic  1.51 us (1%)
    ppermute x8, waiting for transfers between devices, shift(): return lax.ppermute(value, 'bevx', perm)  18.2 us
    ppermute x8, starting transfers between devices, shift(): return lax.ppermute(value, 'bevx', perm)  15.8 us
    all_to_all x2, starting transfers between devices, exchange(): got = lax.all_to_all(rows, 'bevy', split_axis=0, concat_axis=0, tiled=True)  14.6 us
    pallas_call x4, Pallas kernels, local_call(): pl.pallas_call(kernel, in_specs=[SCALAR] + [pl.BlockSpec(memory_space=plt...  13.1 us
    pallas_call x1, Pallas kernels, attention(): pl.pallas_call(attention_kernel, grid=(width // block,), in_specs=[LOCAL]...  12.4 us
    all_to_all x2, waiting for transfers between devices, exchange(): got = lax.all_to_all(rows, 'bevy', split_axis=0, concat_axis=0, tiled=True)  8.57 us
    all_to_all x1, starting transfers between devices, steps(): lax.all_to_all(route, 'bevx', split_axis=0, concat_axis=0, tiled=True)  5.77 us
    pallas_call x1, Pallas kernels, project(): pl.pallas_call(project_kernel, in_specs=[SCALAR] + [LOCAL] * 4, out_specs...  5.11 us
  transfers between devices with their start and end apart: 15, of which 8 were waited for; matrix products, arithmetic and copies ran while one was open for 5% of the time, Pallas kernels for 16%

profile of v3, /device:TPU:8, one launch (start us, length us, event | category | flops | bytes accessed | tf_op | source)
XLA Modules:
  0.0 115.5 jit_solution(6580176487713421619)
XLA Ops:
  0.0 1.9 %collective-permute-start = (bf16[256,768]{1,0:T(8,128)(2,1)}, bf16[256,768]{1,0:T(8,128)(2,1)S(1)}, u32[]{:S(2)}, u32[]{:S(2)}) collective-permute-start(bf16[256,768]{1,0:T(8,128)(2,1)} %refs_2_.1), channel_id=1, source_target_pairs={{0,2},{2,4},{4,6},{6,8},{8,10},{10,12},{12,14},{14,0},{1,3},{3,5},... | collective-permute-start | bytes 1179656 | tf_op jit(solution)/shard_map/ppermute | solution.py:292
  1.9 4.0 %collective-permute-start.1 = (bf16[256,768]{1,0:T(8,128)(2,1)}, bf16[256,768]{1,0:T(8,128)(2,1)S(1)}, u32[]{:S(2)}, u32[]{:S(2)}) collective-permute-start(bf16[256,768]{1,0:T(8,128)(2,1)} %refs_2_.1), channel_id=1, source_target_pairs={{2,0},{4,2},{6,4},{8,6},{10,8},{12,10},{14,12},{0,14},{3,1},{5,3},... | collective-permute-start | bytes 1179656 | tf_op jit(solution)/shard_map/ppermute | solution.py:292
  5.9 0.8 squeeze.3
  6.7 0.5 broadcast.14
  7.2 1.3 %reduce.3 = s32[128]{0:T(128)S(1)} reduce(s32[1,1,128]{2,1,0:T(1,128)} %param.15, s32[]{:T(128)} %broadcast.14), dimensions={0,1}, to_apply=%param.15.reduce_sub_computation.3 | reduce | bytes 1028 | tf_op args[4]
  8.6 0.1 lt.18
  8.7 0.1 copy.19
  8.8 0.7 reshape.26
  9.4 0.8 reshape_squeeze.3
  10.2 0.1 copy.20
  10.3 0.1 reshape.27.refs_2_.refs_3_
  10.4 5.8 %all-to-all-start = ((s32[8,1,128]{2,1,0:T(1,128)}), s32[8,1,128]{2,1,0:T(1,128)S(1)}, u32[]{:S(2)}, u32[]{:S(2)}) async-start(s32[8,1,128]{2,1,0:T(1,128)} %bitcast.5), calls=%async_computation | async-start | bytes 8192 | tf_op jit(solution)/shard_map/all_to_all | solution.py:307
  16.2 0.1 constant_dynamic-slice_fusion
  16.4 0.3 copy.26
  16.7 2.1 %collective-permute-start.2 = (bf16[256,768]{1,0:T(8,128)(2,1)S(1)}, bf16[256,768]{1,0:T(8,128)(2,1)S(1)}, u32[]{:S(2)}, u32[]{:S(2)}) collective-permute-start(bf16[256,768]{1,0:T(8,128)(2,1)S(1)} %collective-permute-done.refs_3_), channel_id=1, source_target_pairs={{0,2},{2,4},{4,6},{6,8},{8,10},{10,12},{12,14},{14,0},{1,3},{3,5},... | collective-permute-start | bytes 1179656 | tf_op jit(solution)/shard_map/ppermute | solution.py:292
  18.8 1.3 %collective-permute-start.3 = (bf16[256,768]{1,0:T(8,128)(2,1)S(1)}, bf16[256,768]{1,0:T(8,128)(2,1)S(1)}, u32[]{:S(2)}, u32[]{:S(2)}) collective-permute-start(bf16[256,768]{1,0:T(8,128)(2,1)S(1)} %collective-permute-done.1.refs_4_), channel_id=1, source_target_pairs={{2,0},{4,2},{6,4},{8,6},{10,8},{12,10},{14,12},{0,14},{3,1},{5,3},... | collective-permute-start | bytes 1179656 | tf_op jit(solution)/shard_map/ppermute | solution.py:292
  20.1 0.1 constant_dynamic-slice_fusion.1
  20.2 0.3 copy.25
  20.5 0.2 copy.24
  20.7 0.1 fusion.bias_ref
  20.8 0.1 pad_add_fusion.refs_0_.at_ref
  20.9 3.0 %all-to-all-done = s32[8,1,128]{2,1,0:T(1,128)S(1)} async-done(((s32[8,1,128]{2,1,0:T(1,128)}), s32[8,1,128]{2,1,0:T(1,128)S(1)}, u32[]{:S(2)}, u32[]{:S(2)}) %all-to-all-start) | async-done | bytes 4128 | tf_op jit(solution)/shard_map/all_to_all | solution.py:307
  23.9 5.9 %collective-permute-done.2.refs_5_ = bf16[256,768]{1,0:T(8,128)(2,1)S(1)} collective-permute-done((bf16[256,768]{1,0:T(8,128)(2,1)S(1)}, bf16[256,768]{1,0:T(8,128)(2,1)S(1)}, u32[]{:S(2)}, u32[]{:S(2)}) %collective-permute-start.2) | collective-permute-done | bytes 393248 | tf_op jit(solution)/shard_map/ppermute | solution.py:292
  29.8 0.2 collective-permute-done.3.refs_6_
  30.0 2.0 %pick_rows.2 = bf16[16,5,8,768]{3,2,1,0:T(8,128)(2,1)} custom-call(s32[2]{0:T(128)S(1)} %pad_add_fusion.refs_0_.at_ref, s32[8,128]{1,0:T(8,128)S(1)} %bitcast.20, bf16[256,768]{1,0:T(8,128)(2,1)S(1)} %copy-done.8, bf16[256,768]{1,0:T(8,128)(2,1)S(1)} %collective-permute-done.refs_3_, bf16[256,768]{1,0:T(8,128)(2,1)S(1)} %collective-permute-done.1.refs_4_, ...), custom_call_target="tpu_custom_call" | custom-call | tf_op jit(solution)/shard_map/pick_rows/pallas_call | solution.py:51
  32.0 7.4 %all-to-all-start.1 = ((bf16[16,5,8,768]{3,2,1,0:T(8,128)(2,1)}), bf16[16,5,8,768]{3,2,1,0:T(8,128)(2,1)S(1)}, u32[]{:S(2)}, u32[]{:S(2)}) async-start(bf16[16,5,8,768]{3,2,1,0:T(8,128)(2,1)} %pick_rows.2), calls=%async_computation.1 | async-start | bytes 1966080 | tf_op jit(solution)/shard_map/all_to_all | solution.py:330
  39.4 1.5 %collective-permute-start.6 = (bf16[256,768]{1,0:T(8,128)(2,1)}, bf16[256,768]{1,0:T(8,128)(2,1)S(1)}, u32[]{:S(2)}, u32[]{:S(2)}) collective-permute-start(bf16[256,768]{1,0:T(8,128)(2,1)} %copy-done.10), channel_id=1, source_target_pairs={{0,2},{2,4},{4,6},{6,8},{8,10},{10,12},{12,14},{14,0},{1,3},{3,5},... | collective-permute-start | bytes 1179656 | tf_op jit(solution)/shard_map/ppermute | solution.py:292
  40.9 1.8 %collective-permute-start.7 = (bf16[256,768]{1,0:T(8,128)(2,1)}, bf16[256,768]{1,0:T(8,128)(2,1)S(1)}, u32[]{:S(2)}, u32[]{:S(2)}) collective-permute-start(bf16[256,768]{1,0:T(8,128)(2,1)} %copy-done.9), channel_id=1, source_target_pairs={{2,0},{4,2},{6,4},{8,6},{10,8},{12,10},{14,12},{0,14},{3,1},{5,3},... | collective-permute-start | bytes 1179656 | tf_op jit(solution)/shard_map/ppermute | solution.py:292
  42.7 8.3 %collective-permute-done.6.refs_2_ = bf16[256,768]{1,0:T(8,128)(2,1)S(1)} collective-permute-done((bf16[256,768]{1,0:T(8,128)(2,1)}, bf16[256,768]{1,0:T(8,128)(2,1)S(1)}, u32[]{:S(2)}, u32[]{:S(2)}) %collective-permute-start.6) | collective-permute-done | bytes 393248 | tf_op jit(solution)/shard_map/ppermute | solution.py:292
  51.0 0.3 collective-permute-start.8
  51.4 0.3 collective-permute-done.7.refs_3_
  51.6 2.8 %collective-permute-start.9 = (bf16[128,768]{1,0:T(8,128)(2,1)S(1)}, bf16[128,768]{1,0:T(8,128)(2,1)S(1)}, u32[]{:S(2)}, u32[]{:S(2)}) collective-permute-start(bf16[128,768]{1,0:T(8,128)(2,1)S(1)} %slice.9), channel_id=1, source_target_pairs={{2,0},{4,2},{6,4},{8,6},{10,8},{12,10},{14,12},{0,14},{3,1},{5,3},... | collective-permute-start | bytes 589832 | tf_op jit(solution)/shard_map/ppermute | solution.py:292
  54.5 3.5 %collective-permute-done.8.refs_4_ = bf16[128,768]{1,0:T(8,128)(2,1)S(1)} collective-permute-done((bf16[128,768]{1,0:T(8,128)(2,1)S(1)}, bf16[128,768]{1,0:T(8,128)(2,1)S(1)}, u32[]{:S(2)}, u32[]{:S(2)}) %collective-permute-start.8) | collective-permute-done | bytes 196640 | tf_op jit(solution)/shard_map/ppermute | solution.py:292
  58.0 0.0 collective-permute-done.9.refs_5_
  58.0 0.9 pick_rows.3
  59.0 0.8 copy-done.5
  59.8 7.2 %all-to-all-start.2 = ((bf16[16,3,8,768]{3,2,1,0:T(8,128)(2,1)}), bf16[16,3,8,768]{3,2,1,0:T(8,128)(2,1)}, u32[]{:S(2)}, u32[]{:S(2)}) async-start(bf16[16,3,8,768]{3,2,1,0:T(8,128)(2,1)} %copy-done.5), calls=%async_computation.2 | async-start | bytes 1179648 | tf_op jit(solution)/shard_map/all_to_all | solution.py:330
  67.1 8.6 %all-to-all-done.2.refs_2_ = bf16[16,3,8,768]{3,2,1,0:T(8,128)(2,1)} async-done(((bf16[16,3,8,768]{3,2,1,0:T(8,128)(2,1)}), bf16[16,3,8,768]{3,2,1,0:T(8,128)(2,1)}, u32[]{:S(2)}, u32[]{:S(2)}) %all-to-all-start.2) | async-done | bytes 589856 | tf_op jit(solution)/shard_map/all_to_all | solution.py:330
  75.6 2.9 %shard_map.109.refs_1_ = f32[768,1024]{1,0:T(8,128)S(1)} custom-call(s32[2]{0:T(128)S(1)} %pad_add_fusion.refs_0_.at_ref, bf16[16,5,8,768]{3,2,1,0:T(8,128)(2,1)S(1)} %all-to-all-done.1.refs_1_, s32[8,128]{1,0:T(8,128)S(1)} %reshape.27.refs_2_.refs_3_, bf16[768,1024]{1,0:T(8,128)(2,1)S(1)} %copy-done.1), custom_call_target="tpu_custom_call" | custom-call | tf_op jit(solution)/shard_map/pallas_call | solution.py:116
  78.6 3.6 %shard_map.110.refs_1_ = f32[768,1024]{1,0:T(8,128)S(1)} custom-call(s32[2]{0:T(128)S(1)} %pad_add_fusion.refs_0_.at_ref, f32[768,1024]{1,0:T(8,128)S(1)} %shard_map.109.refs_1_, bf16[16,5,8,768]{3,2,1,0:T(8,128)(2,1)} %collective-permute-done.5.refs_2_, s32[8,128]{1,0:T(8,128)S(1)} %collective-permute-done.4.refs_3_, bf16[768,1024]{1,0:T(8,128)(2,1)S(1)} %copy-done.1), custom_call_target="tpu_custom_call" | custom-call | tf_op jit(solution)/shard_map/pallas_call | solution.py:116
  82.2 1.6 %copy-done.2 = f32[768,1024]{1,0:T(8,128)} copy-done((f32[768,1024]{1,0:T(8,128)}, f32[768,1024]{1,0:T(8,128)S(1)}, u32[]{:S(2)}) %copy-start.2) | copy-done | bytes 3145752
  83.9 3.9 %shard_map.111.refs_1_ = f32[768,1024]{1,0:T(8,128)S(1)} custom-call(s32[2]{0:T(128)S(1)} %pad_add_fusion.refs_0_.at_ref, f32[768,1024]{1,0:T(8,128)} %copy-done.2, bf16[16,3,8,768]{3,2,1,0:T(8,128)(2,1)} %all-to-all-done.2.refs_2_, s32[8,128]{1,0:T(8,128)S(1)} %reshape.27.refs_2_.refs_3_, bf16[768,1024]{1,0:T(8,128)(2,1)S(1)} %copy-done.1), custom_call_target="tpu_custom_call" | custom-call | tf_op jit(solution)/shard_map/pallas_call | solution.py:116
  87.8 0.0 copy-start.3
  87.8 2.6 %shard_map.112 = (f32[512,1024]{1,0:T(8,128)S(1)}, bf16[768,1024]{1,0:T(8,128)(2,1)S(1)}, bf16[256,1024]{1,0:T(8,128)(2,1)S(1)}) custom-call(s32[2]{0:T(128)S(1)} %pad_add_fusion.refs_0_.at_ref, f32[768,1024]{1,0:T(8,128)S(1)} %shard_map.111.refs_1_, bf16[16,3,8,768]{3,2,1,0:T(8,128)(2,1)S(1)} %collective-permute-done.10.refs_2_, ...), custom_call_target="tpu_custom_call" | custom-call | tf_op jit(solution)/shard_map/pallas_call | solution.py:116
  90.5 4.3 %collective-permute-start.11 = (bf16[256,1024]{1,0:T(8,128)(2,1)S(1)}, bf16[256,1024]{1,0:T(8,128)(2,1)S(1)}, u32[]{:S(2)}, u32[]{:S(2)}) collective-permute-start(bf16[256,1024]{1,0:T(8,128)(2,1)S(1)} %get-tuple-element.24), channel_id=1, source_target_pairs={{16,1},{32,17},{48,33},{64,49},{80,65},{96,81},{112,97},{128,113},... | collective-permute-start | bytes 1572872 | tf_op jit(solution)/shard_map/ppermute | solution.py:373
  94.8 5.1 %near_projections.1 = (bf16[512,1024]{1,0:T(8,128)(2,1)S(1)}, bf16[768,1024]{1,0:T(8,128)(2,1)S(1)}, bf16[1024,768]{1,0:T(8,128)(2,1)S(1)}) custom-call(s32[2]{0:T(128)S(1)} %pad_add_fusion.refs_0_.at_ref, bf16[768,1024]{1,0:T(8,128)(2,1)S(1)} %get-tuple-element.20.x_ref, bf16[1024,1024]{1,0:T(8,128)(2,1)S(1)} %copy-done.7, ...), custom_call_target="tpu_custom_call" | custom-call | tf_op jit(solution)/shard_map/near_projections/pallas_call | solution.py:147
  100.0 3.1 %collective-permute-done.11.far_ref = bf16[256,1024]{1,0:T(8,128)(2,1)S(1)} collective-permute-done((bf16[256,1024]{1,0:T(8,128)(2,1)S(1)}, bf16[256,1024]{1,0:T(8,128)(2,1)S(1)}, u32[]{:S(2)}, u32[]{:S(2)}) %collective-permute-start.11) | collective-permute-done | bytes 524320 | tf_op jit(solution)/shard_map/ppermute | solution.py:373
  103.1 12.4 %window_attention.1 = bf16[512,1024]{1,0:T(8,128)(2,1)} custom-call(bf16[512,1024]{1,0:T(8,128)(2,1)S(1)} %get-tuple-element.21.q_ref, bf16[768,1024]{1,0:T(8,128)(2,1)S(1)} %get-tuple-element.22.k_ref, bf16[1024,768]{1,0:T(8,128)(2,1)S(1)} %get-tuple-element.23.v_ref, bf16[256,1024]{1,0:T(8,128)(2,1)S(1)} %collective-permute-done.11.far_ref, ...), custom_call_target="tpu_custom_call" | custom-call | tf_op jit(solution)/shard_map/window_attention/pallas_call | solution.py:242
  (35 shorter events, 0.1 us)
Async XLA Ops:
  0.0 16.2 %copy-start = (bf16[256,64,16]{0,2,1:T(8,128)(2,1)S(1)}, bf16[256,64,16]{0,2,1:T(8,128)(2,1)}, u32[]{:S(2)}) copy-start(bf16[256,64,16]{0,2,1:T(8,128)(2,1)} %param.21) | copy-start | bytes 1572868
  0.0 30.0 %copy-start.8 = (bf16[256,768]{1,0:T(8,128)(2,1)S(1)}, bf16[256,768]{1,0:T(8,128)(2,1)}, u32[]{:S(2)}) copy-start(bf16[256,768]{1,0:T(8,128)(2,1)} %refs_2_.1) | copy-start | bytes 1179652
  0.0 16.7 %collective-permute-start = (bf16[256,768]{1,0:T(8,128)(2,1)}, bf16[256,768]{1,0:T(8,128)(2,1)S(1)}, u32[]{:S(2)}, u32[]{:S(2)}) collective-permute-start(bf16[256,768]{1,0:T(8,128)(2,1)} %refs_2_.1), channel_id=1, source_target_pairs={{0,2},{2,4},{4,6},{6,8},{8,10},{10,12},{12,14},{14,0},{1,3},{3,5},... | collective-permute-start | bytes 1179656 | tf_op jit(solution)/shard_map/ppermute | solution.py:292
  1.9 16.8 %collective-permute-start.1 = (bf16[256,768]{1,0:T(8,128)(2,1)}, bf16[256,768]{1,0:T(8,128)(2,1)S(1)}, u32[]{:S(2)}, u32[]{:S(2)}) collective-permute-start(bf16[256,768]{1,0:T(8,128)(2,1)} %refs_2_.1), channel_id=1, source_target_pairs={{2,0},{4,2},{6,4},{8,6},{10,8},{12,10},{14,12},{0,14},{3,1},{5,3},... | collective-permute-start | bytes 1179656 | tf_op jit(solution)/shard_map/ppermute | solution.py:292
  10.4 13.5 %all-to-all-start = ((s32[8,1,128]{2,1,0:T(1,128)}), s32[8,1,128]{2,1,0:T(1,128)S(1)}, u32[]{:S(2)}, u32[]{:S(2)}) async-start(s32[8,1,128]{2,1,0:T(1,128)} %bitcast.5), calls=%async_computation | async-start | bytes 8192 | tf_op jit(solution)/shard_map/all_to_all | solution.py:307
  16.2 15.8 %collective-permute-start.4 = (s32[8,128]{1,0:T(8,128)S(1)}, s32[8,128]{1,0:T(8,128)S(1)}, u32[]{:S(2)}, u32[]{:S(2)}) collective-permute-start(s32[8,128]{1,0:T(8,128)S(1)} %reshape.27.refs_2_.refs_3_), channel_id=1, source_target_pairs={{0,1},{1,0},{2,3},{3,2},{4,5},{5,4},{6,7},{7,6},{8,9},{9,8},{10,11... | collective-permute-start | bytes 12296 | tf_op jit(solution)/shard_map/ppermute | solution.py:306
  16.7 13.1 %collective-permute-start.2 = (bf16[256,768]{1,0:T(8,128)(2,1)S(1)}, bf16[256,768]{1,0:T(8,128)(2,1)S(1)}, u32[]{:S(2)}, u32[]{:S(2)}) collective-permute-start(bf16[256,768]{1,0:T(8,128)(2,1)S(1)} %collective-permute-done.refs_3_), channel_id=1, source_target_pairs={{0,2},{2,4},{4,6},{6,8},{8,10},{10,12},{12,14},{14,0},{1,3},{3,5},... | collective-permute-start | bytes 1179656 | tf_op jit(solution)/shard_map/ppermute | solution.py:292
  18.8 11.3 %collective-permute-start.3 = (bf16[256,768]{1,0:T(8,128)(2,1)S(1)}, bf16[256,768]{1,0:T(8,128)(2,1)S(1)}, u32[]{:S(2)}, u32[]{:S(2)}) collective-permute-start(bf16[256,768]{1,0:T(8,128)(2,1)S(1)} %collective-permute-done.1.refs_4_), channel_id=1, source_target_pairs={{2,0},{4,2},{6,4},{8,6},{10,8},{12,10},{14,12},{0,14},{3,1},{5,3},... | collective-permute-start | bytes 1179656 | tf_op jit(solution)/shard_map/ppermute | solution.py:292
  29.8 2.2 %copy-start.10 = (bf16[256,768]{1,0:T(8,128)(2,1)}, bf16[256,768]{1,0:T(8,128)(2,1)S(1)}, u32[]{:S(2)}) copy-start(bf16[256,768]{1,0:T(8,128)(2,1)S(1)} %collective-permute-done.2.refs_5_) | copy-start | bytes 1179652
  30.0 2.0 %copy-start.9 = (bf16[256,768]{1,0:T(8,128)(2,1)}, bf16[256,768]{1,0:T(8,128)(2,1)S(1)}, u32[]{:S(2)}) copy-start(bf16[256,768]{1,0:T(8,128)(2,1)S(1)} %collective-permute-done.3.refs_6_) | copy-start | bytes 1179652
  32.0 27.8 %all-to-all-start.1 = ((bf16[16,5,8,768]{3,2,1,0:T(8,128)(2,1)}), bf16[16,5,8,768]{3,2,1,0:T(8,128)(2,1)S(1)}, u32[]{:S(2)}, u32[]{:S(2)}) async-start(bf16[16,5,8,768]{3,2,1,0:T(8,128)(2,1)} %pick_rows.2), calls=%async_computation.1 | async-start | bytes 1966080 | tf_op jit(solution)/shard_map/all_to_all | solution.py:330
  39.4 36.3 %copy-start.1 = (bf16[768,1024]{1,0:T(8,128)(2,1)S(1)}, bf16[768,1024]{1,0:T(8,128)(2,1)}, u32[]{:S(2)}) copy-start(bf16[768,1024]{1,0:T(8,128)(2,1)} %refs_4_.5) | copy-start | bytes 4718596
  39.4 11.6 %collective-permute-start.6 = (bf16[256,768]{1,0:T(8,128)(2,1)}, bf16[256,768]{1,0:T(8,128)(2,1)S(1)}, u32[]{:S(2)}, u32[]{:S(2)}) collective-permute-start(bf16[256,768]{1,0:T(8,128)(2,1)} %copy-done.10), channel_id=1, source_target_pairs={{0,2},{2,4},{4,6},{6,8},{8,10},{10,12},{12,14},{14,0},{1,3},{3,5},... | collective-permute-start | bytes 1179656 | tf_op jit(solution)/shard_map/ppermute | solution.py:292
  40.9 10.7 %collective-permute-start.7 = (bf16[256,768]{1,0:T(8,128)(2,1)}, bf16[256,768]{1,0:T(8,128)(2,1)S(1)}, u32[]{:S(2)}, u32[]{:S(2)}) collective-permute-start(bf16[256,768]{1,0:T(8,128)(2,1)} %copy-done.9), channel_id=1, source_target_pairs={{2,0},{4,2},{6,4},{8,6},{10,8},{12,10},{14,12},{0,14},{3,1},{5,3},... | collective-permute-start | bytes 1179656 | tf_op jit(solution)/shard_map/ppermute | solution.py:292
  51.0 7.0 %collective-permute-start.8 = (bf16[128,768]{1,0:T(8,128)(2,1)S(1)}, bf16[128,768]{1,0:T(8,128)(2,1)S(1)}, u32[]{:S(2)}, u32[]{:S(2)}) collective-permute-start(bf16[128,768]{1,0:T(8,128)(2,1)S(1)} %slice.8), channel_id=1, source_target_pairs={{0,2},{2,4},{4,6},{6,8},{8,10},{10,12},{12,14},{14,0},{1,3},{3,5},... | collective-permute-start | bytes 589832 | tf_op jit(solution)/shard_map/ppermute | solution.py:292
  51.6 6.4 %collective-permute-start.9 = (bf16[128,768]{1,0:T(8,128)(2,1)S(1)}, bf16[128,768]{1,0:T(8,128)(2,1)S(1)}, u32[]{:S(2)}, u32[]{:S(2)}) collective-permute-start(bf16[128,768]{1,0:T(8,128)(2,1)S(1)} %slice.9), channel_id=1, source_target_pairs={{2,0},{4,2},{6,4},{8,6},{10,8},{12,10},{14,12},{0,14},{3,1},{5,3},... | collective-permute-start | bytes 589832 | tf_op jit(solution)/shard_map/ppermute | solution.py:292
  59.0 0.8 copy-start.5
  59.8 15.8 %all-to-all-start.2 = ((bf16[16,3,8,768]{3,2,1,0:T(8,128)(2,1)}), bf16[16,3,8,768]{3,2,1,0:T(8,128)(2,1)}, u32[]{:S(2)}, u32[]{:S(2)}) async-start(bf16[16,3,8,768]{3,2,1,0:T(8,128)(2,1)} %copy-done.5), calls=%async_computation.2 | async-start | bytes 1179648 | tf_op jit(solution)/shard_map/all_to_all | solution.py:330
  67.1 11.5 %collective-permute-start.5 = (bf16[16,5,8,768]{3,2,1,0:T(8,128)(2,1)S(1)}, bf16[16,5,8,768]{3,2,1,0:T(8,128)(2,1)}, u32[]{:S(2)}, u32[]{:S(2)}) collective-permute-start(bf16[16,5,8,768]{3,2,1,0:T(8,128)(2,1)S(1)} %all-to-all-done.1.refs_1_), channel_id=1, source_target_pairs={{0,1},{1,0},{2,3},{3,2},{4,5},{5,4},{6,7},{7,6},{8,9},{9,8},{10,11... | collective-permute-start | bytes 2949128 | tf_op jit(solution)/shard_map/ppermute | solution.py:331
  75.6 12.2 %collective-permute-start.10 = (bf16[16,3,8,768]{3,2,1,0:T(8,128)(2,1)}, bf16[16,3,8,768]{3,2,1,0:T(8,128)(2,1)S(1)}, u32[]{:S(2)}, u32[]{:S(2)}) collective-permute-start(bf16[16,3,8,768]{3,2,1,0:T(8,128)(2,1)} %all-to-all-done.2.refs_2_), channel_id=1, source_target_pairs={{0,1},{1,0},{2,3},{3,2},{4,5},{5,4},{6,7},{7,6},{8,9},{9,8},{10,11... | collective-permute-start | bytes 1769480 | tf_op jit(solution)/shard_map/ppermute | solution.py:331
  82.2 1.6 %copy-start.2 = (f32[768,1024]{1,0:T(8,128)}, f32[768,1024]{1,0:T(8,128)S(1)}, u32[]{:S(2)}) copy-start(f32[768,1024]{1,0:T(8,128)S(1)} %shard_map.110.refs_1_) | copy-start | bytes 9437188
  83.9 3.9 %copy-start.11 = (f32[1024]{0:T(1024)S(1)}, f32[1024]{0:T(1024)}, u32[]{:S(2)}) copy-start(f32[1024]{0:T(1024)} %param.16) | copy-start | bytes 12292
  83.9 10.9 %copy-start.7 = (bf16[1024,1024]{1,0:T(8,128)(2,1)S(1)}, bf16[1024,1024]{1,0:T(8,128)(2,1)}, u32[]{:S(2)}) copy-start(bf16[1024,1024]{1,0:T(8,128)(2,1)} %wq_ref.1) | copy-start | bytes 6291460
  87.8 7.0 %copy-start.3 = (bf16[1024,1024]{1,0:T(8,128)(2,1)S(1)}, bf16[1024,1024]{1,0:T(8,128)(2,1)}, u32[]{:S(2)}) copy-start(bf16[1024,1024]{1,0:T(8,128)(2,1)} %wk_ref.3) | copy-start | bytes 6291460
  87.8 7.0 %copy-start.4 = (bf16[1024,1024]{1,0:T(8,128)(2,1)S(1)}, bf16[1024,1024]{1,0:T(8,128)(2,1)}, u32[]{:S(2)}) copy-start(bf16[1024,1024]{1,0:T(8,128)(2,1)} %wv_ref.3) | copy-start | bytes 6291460
  90.5 12.6 %collective-permute-start.11 = (bf16[256,1024]{1,0:T(8,128)(2,1)S(1)}, bf16[256,1024]{1,0:T(8,128)(2,1)S(1)}, u32[]{:S(2)}, u32[]{:S(2)}) collective-permute-start(bf16[256,1024]{1,0:T(8,128)(2,1)S(1)} %get-tuple-element.24), channel_id=1, source_target_pairs={{16,1},{32,17},{48,33},{64,49},{80,65},{96,81},{112,97},{128,113},... | collective-permute-start | bytes 1572872 | tf_op jit(solution)/shard_map/ppermute | solution.py:373
  94.8 8.3 %copy-start.6 = (bf16[1024,1024]{1,0:T(8,128)(2,1)S(1)}, bf16[1024,1024]{1,0:T(8,128)(2,1)}, u32[]{:S(2)}) copy-start(bf16[1024,1024]{1,0:T(8,128)(2,1)} %wo_ref.1) | copy-start | bytes 6291460

commit v4 on v3

--- a/solution.py
+++ b/solution.py
@@ -11,7 +11,8 @@
 HALO = 4
 MASKED = -1e30
 HEAD_LANES = 16
-EARLY = (0, -1, 1, -2, 2)
+ONE = (0, -1, 1)
+TWO = (-2, 2)
 LATE = (-3, 3, 4)
 
 
@@ -80,20 +81,18 @@
         total[...] += added
 
 
-def first_sum_kernel(n_x, at_ref, a_ref, ac_ref, w_ref, out_ref):
+def start_sum_kernel(n_x, at_ref, a_ref, ac_ref, b_ref, bc_ref, w_ref, out_ref):
     out_ref[...] = jnp.zeros_like(out_ref)
-    summed(EARLY, n_x, at_ref, ((a_ref, ac_ref),), w_ref, out_ref)
-
-
-def second_sum_kernel(n_x, at_ref, total_ref, a_ref, ac_ref, w_ref, out_ref):
-    out_ref[...] = total_ref[...]
-    summed(EARLY, n_x, at_ref, ((a_ref, ac_ref),), w_ref, out_ref)
-
-
-def next_sum_kernel(n_x, at_ref, total_ref, a_ref, ac_ref, w_ref, out_ref, sem):
+    summed(ONE, n_x, at_ref, ((a_ref, ac_ref), (b_ref, bc_ref)), w_ref, out_ref)
+
+
+def next_sum_kernel(offsets, n_x, at_ref, total_ref, *refs):
+    pairs, (w_ref, out_ref, sem) = refs[:-3], refs[-3:]
     copy = pltpu.make_async_copy(total_ref, out_ref, sem)
     copy.start()
-    summed(LATE, n_x, at_ref, ((a_ref, ac_ref),), w_ref, out_ref, copy.wait)
+    for i in range(0, len(pairs), 2):
+        ready = copy.wait if i == 0 else None
+        summed(offsets, n_x, at_ref, (pairs[i : i + 2],), w_ref, out_ref, ready)
 
 
 def last_sum_kernel(
@@ -297,12 +296,9 @@
     def by_column(value):
         return value.reshape(n_y, n_x, slot_count).transpose(1, 0, 2).reshape(n_x, -1)
 
-    is_live = (
-        lax.broadcasted_iota(jnp.int32, route_token.shape[2:], 1) < slot_counts[0, 0][:, None]
-    )
-    route = by_column(jnp.where(is_live, route_token[0, 0], -1))
+    slot = lax.broadcasted_iota(jnp.int32, route_token.shape, 3)
+    route = by_column(jnp.where(slot < slot_counts[..., None], route_token, -1))
     cells = by_column(route_cell[:, 0, 0, :])
-    route, cells = lax.optimization_barrier((route, cells))
     cells_other = lax.ppermute(cells, "cam", swap)
     route = lax.all_to_all(route, "bevx", split_axis=0, concat_axis=0, tiled=True)
 
@@ -314,6 +310,33 @@
     u4 = shift(u3[:half], up)
     d4 = shift(d3[half:], down)
 
+    def exchange(rows):
+        got = lax.all_to_all(rows, "bevy", split_axis=0, concat_axis=0, tiled=True)
+        return got, lax.ppermute(got, "cam", swap)
+
+    def picked(offsets, blocks, extra=()):
+        rows = pick(offsets, n_x, n_y, at, route, blocks)
+        rows, extra = lax.optimization_barrier((rows, extra))
+        return *exchange(rows), extra
+
+    def more(offsets, lifted, pairs):
+        [lifted] = local_call(
+            lambda *refs: next_sum_kernel(offsets, n_x, *refs),
+            (at, pltpu.with_memory_space_constraint(lifted, pltpu.HBM), *pairs, lift_weight),
+            [total],
+            [pltpu.SemaphoreType.DMA],
+            (1,),
+        )
+        return lifted
+
+    total = jax.ShapeDtypeStruct((ext, width), jnp.float32)
+    one, one_other, _ = picked(ONE, (image_tokens, u1, d1))
+    two, two_other, _ = picked(TWO, (u2, d2))
+    [lifted] = local_call(
+        lambda *refs: start_sum_kernel(n_x, *refs),
+        (at, one, cells, one_other, cells_other, lift_weight),
+        [total],
+    )
     near_row = (row * 2 + core) * ROWS_DEV - core * HALO
     far_row = (row * 2 + core) * ROWS_DEV + jnp.where(core == 0, -HALO, ROWS_DEV)
     far_ok = (far_row >= 0) & (far_row < grid_rows)
@@ -325,38 +348,9 @@
     bias = jnp.concatenate([near_bias, far_bias], axis=0).reshape(-1, head_count)
     bias = jnp.pad(bias, ((0, 0), (0, 1)), constant_values=1)
     bias = jnp.pad(bias, ((0, 0), (0, 127 - head_count)))
-
-    def exchange(rows):
-        got = lax.all_to_all(rows, "bevy", split_axis=0, concat_axis=0, tiled=True)
-        return got, lax.ppermute(got, "cam", swap)
-
-    rows = pick(EARLY, n_x, n_y, at, route, (image_tokens, u1, d1, u2, d2))
-    rows, bias, cells_other = lax.optimization_barrier((rows, bias, cells_other))
-    early, early_other = exchange(rows)
-    total = jax.ShapeDtypeStruct((ext, width), jnp.float32)
-    [lifted] = local_call(
-        lambda *refs: first_sum_kernel(n_x, *refs), (at, early, cells, lift_weight), [total]
-    )
-    [lifted] = local_call(
-        lambda *refs: second_sum_kernel(n_x, *refs),
-        (at, lifted, early_other, cells_other, lift_weight),
-        [total],
-    )
-    rows = pick(LATE, n_x, n_y, at, route, (u3, d3, u4, d4))
-    late, late_other = exchange(rows)
-    [lifted] = local_call(
-        lambda *refs: next_sum_kernel(n_x, *refs),
-        (
-            at,
-            pltpu.with_memory_space_constraint(lifted, pltpu.HBM),
-            late,
-            cells,
-            lift_weight,
-        ),
-        [total],
-        [pltpu.SemaphoreType.DMA],
-        (1,),
-    )
+    late, late_other, bias = picked(LATE, (u3, d3, u4, d4), bias)
+    lifted = more(TWO, lifted, (two, cells, two_other, cells_other))
+    lifted = more(LATE, lifted, (late, cells))
     own_lifted, normed, sent = local_call(
         lambda *refs: last_sum_kernel(n_x, edge, *refs),
         (at, lifted, late_other, cells_other, lift_weight, norm_gain.reshape(1, -1)),

time: 118 us -> 133 us (1.13)
  starting transfers between devices: 40.5 us -> 47.7 us
  local copies, waits for them, and re-layouts: 6.69 us -> 12.8 us
  Pallas kernels: 33.5 us -> 36.8 us
    all_to_all x2 -> x3, starting transfers between devices: 14.6 us -> 20.8 us  [exchange(): got = lax.all_to_all(rows, 'bevy', split_axis=0, concat_axis=0, tiled=True)]
    ppermute x8, waiting for transfers between devices: 18.2 us -> 13.7 us  [shift(): return lax.ppermute(value, 'bevx', perm)]
    unnamed x27 -> x34, local copies, waits for them, and re-layouts: 3.59 us -> 7.6 us
    all_to_all x2 -> x3, waiting for transfers between devices: 8.57 us -> 11.8 us  [exchange(): got = lax.all_to_all(rows, 'bevy', split_axis=0, concat_axis=0, tiled=True)]
    pallas_call x4, Pallas kernels: 13.1 us -> 15 us  [local_call(): pl.pallas_call(kernel, in_specs=[SCALAR] + [pl.BlockSpec(memory_space=plt...]
    transpose x2, local copies, waits for them, and re-layouts: 0.21 us -> 1.67 us  [by_column(): value.reshape(n_y, n_x, slot_count).transpose(1, 0, 2).reshape(n_x, -1)]
    pallas_call x2 -> x3, Pallas kernels: 2.9 us -> 4.3 us  [pick(): pl.pallas_call(lambda *refs: pick_kernel(offsets, n_x, *refs), in_specs=[...]
  transfers between devices with their start and end apart: 15 -> 17, of which waited for: 8 -> 8; matrix products, arithmetic and copies ran while one was open for 5% -> 5% of each run, Pallas kernels for 16% -> 16%
where the time goes in v4:
time: 133 us; the launch traced here: 131 us
  starting transfers between devices  47.7 us (36%)
  Pallas kernels  36.8 us (28%)
  waiting for transfers between devices  32.4 us (24%)
  local copies, waits for them, and re-layouts  12.8 us (10%)
    all_to_all x3, starting transfers between devices, exchange(): got = lax.all_to_all(rows, 'bevy', split_axis=0, concat_axis=0, tiled=True)  20.8 us
    ppermute x8, starting transfers between devices, shift(): return lax.ppermute(value, 'bevx', perm)  15.7 us
    pallas_call x4, Pallas kernels, local_call(): pl.pallas_call(kernel, in_specs=[SCALAR] + [pl.BlockSpec(memory_space=plt...  15 us
    ppermute x8, waiting for transfers between devices, shift(): return lax.ppermute(value, 'bevx', perm)  13.7 us
    pallas_call x1, Pallas kernels, attention(): pl.pallas_call(attention_kernel, grid=(width // block,), in_specs=[LOCAL]...  12.4 us
    all_to_all x3, waiting for transfers between devices, exchange(): got = lax.all_to_all(rows, 'bevy', split_axis=0, concat_axis=0, tiled=True)  11.8 us
    unnamed x34, local copies, waits for them, and re-layouts  7.6 us
    all_to_all x1, starting transfers between devices, steps(): lax.all_to_all(route, 'bevx', split_axis=0, concat_axis=0, tiled=True)  5.56 us
  transfers between devices with their start and end apart: 17, of which 8 were waited for; matrix products, arithmetic and copies ran while one was open for 5% of the time, Pallas kernels for 16%

profile of v4, /device:TPU:8, one launch (start us, length us, event | category | flops | bytes accessed | tf_op | source)
XLA Modules:
  0.0 130.9 jit_solution(16561887774057926417)
XLA Ops:
  0.0 1.9 %collective-permute-start = (bf16[256,768]{1,0:T(8,128)(2,1)}, bf16[256,768]{1,0:T(8,128)(2,1)S(1)}, u32[]{:S(2)}, u32[]{:S(2)}) collective-permute-start(bf16[256,768]{1,0:T(8,128)(2,1)} %refs_2_.1), channel_id=1, source_target_pairs={{0,2},{2,4},{4,6},{6,8},{8,10},{10,12},{12,14},{14,0},{1,3},{3,5},... | collective-permute-start | bytes 1179656 | tf_op jit(solution)/shard_map/ppermute | solution.py:291
  1.9 4.0 %collective-permute-start.1 = (bf16[256,768]{1,0:T(8,128)(2,1)}, bf16[256,768]{1,0:T(8,128)(2,1)S(1)}, u32[]{:S(2)}, u32[]{:S(2)}) collective-permute-start(bf16[256,768]{1,0:T(8,128)(2,1)} %refs_2_.1), channel_id=1, source_target_pairs={{2,0},{4,2},{6,4},{8,6},{10,8},{12,10},{14,12},{0,14},{3,1},{5,3},... | collective-permute-start | bytes 1179656 | tf_op jit(solution)/shard_map/ppermute | solution.py:291
  5.9 9.2 %collective-permute-done.refs_3_ = bf16[256,768]{1,0:T(8,128)(2,1)S(1)} collective-permute-done((bf16[256,768]{1,0:T(8,128)(2,1)}, bf16[256,768]{1,0:T(8,128)(2,1)S(1)}, u32[]{:S(2)}, u32[]{:S(2)}) %collective-permute-start) | collective-permute-done | bytes 393248 | tf_op jit(solution)/shard_map/ppermute | solution.py:291
  15.2 3.2 %collective-permute-start.5 = (bf16[256,768]{1,0:T(8,128)(2,1)S(1)}, bf16[256,768]{1,0:T(8,128)(2,1)S(1)}, u32[]{:S(2)}, u32[]{:S(2)}) collective-permute-start(bf16[256,768]{1,0:T(8,128)(2,1)S(1)} %collective-permute-done.1.refs_4_), channel_id=1, source_target_pairs={{2,0},{4,2},{6,4},{8,6},{10,8},{12,10},{14,12},{0,14},{3,1},{5,3},... | collective-permute-start | bytes 1179656 | tf_op jit(solution)/shard_map/ppermute | solution.py:291
  18.4 0.7 fusion.1
  19.3 0.7 all_to_all.16
  20.0 5.6 %all-to-all-start = ((s32[8,1,128]{2,1,0:T(1,128)}), s32[8,1,128]{2,1,0:T(1,128)S(1)}, u32[]{:S(2)}, u32[]{:S(2)}) async-start(s32[8,1,128]{2,1,0:T(1,128)} %bitcast.4), calls=%async_computation | async-start | bytes 8192 | tf_op jit(solution)/shard_map/all_to_all | solution.py:303
  25.6 0.1 constant_dynamic-slice_fusion.1
  25.7 1.0 collective-permute-done.4.refs_2_
  26.7 1.2 collective-permute-start.7
  27.8 2.1 %collective-permute-start.8 = (bf16[256,768]{1,0:T(8,128)(2,1)S(1)}, bf16[256,768]{1,0:T(8,128)(2,1)S(1)}, u32[]{:S(2)}, u32[]{:S(2)}) collective-permute-start(bf16[256,768]{1,0:T(8,128)(2,1)S(1)} %collective-permute-done.5.refs_3_), channel_id=1, source_target_pairs={{2,0},{4,2},{6,4},{8,6},{10,8},{12,10},{14,12},{0,14},{3,1},{5,3},... | collective-permute-start | bytes 1179656 | tf_op jit(solution)/shard_map/ppermute | solution.py:291
  30.0 0.3 copy.24
  30.3 3.0 %all-to-all-done = s32[8,1,128]{2,1,0:T(1,128)S(1)} async-done(((s32[8,1,128]{2,1,0:T(1,128)}), s32[8,1,128]{2,1,0:T(1,128)S(1)}, u32[]{:S(2)}, u32[]{:S(2)}) %all-to-all-start) | async-done | bytes 4128 | tf_op jit(solution)/shard_map/all_to_all | solution.py:303
  33.3 1.0 copy-done.13
  34.3 1.7 %pick_rows.3 = bf16[16,3,8,768]{3,2,1,0:T(8,128)(2,1)} custom-call(s32[2]{0:T(128)S(1)} %pad_add_fusion.refs_0_.at_ref, s32[8,128]{1,0:T(8,128)S(1)} %bitcast.18, bf16[256,768]{1,0:T(8,128)(2,1)S(1)} %copy-done.13, bf16[256,768]{1,0:T(8,128)(2,1)S(1)} %collective-permute-done.refs_3_, bf16[256,768]{1,0:T(8,128)(2,1)S(1)} %collective-permute-done.1.refs_4_), custom_call_target="tpu_custom_call" | custom-call | tf_op jit(solution)/shard_map/pick_rows/pallas_call | solution.py:52
  36.0 7.4 %all-to-all-start.1 = ((bf16[16,3,8,768]{3,2,1,0:T(8,128)(2,1)}), bf16[16,3,8,768]{3,2,1,0:T(8,128)(2,1)S(1)}, u32[]{:S(2)}, u32[]{:S(2)}) async-start(bf16[16,3,8,768]{3,2,1,0:T(8,128)(2,1)} %pick_rows.3), calls=%async_computation.1 | async-start | bytes 1179648 | tf_op jit(solution)/shard_map/all_to_all | solution.py:314
  43.4 0.1 constant_dynamic-slice_fusion
  43.5 0.3 copy.25
  43.8 0.7 slice.8
  44.5 0.5 collective-permute-start.9
  45.0 2.8 %collective-permute-start.10 = (bf16[128,768]{1,0:T(8,128)(2,1)S(1)}, bf16[128,768]{1,0:T(8,128)(2,1)S(1)}, u32[]{:S(2)}, u32[]{:S(2)}) collective-permute-start(bf16[128,768]{1,0:T(8,128)(2,1)S(1)} %slice.9), channel_id=1, source_target_pairs={{2,0},{4,2},{6,4},{8,6},{10,8},{12,10},{14,12},{0,14},{3,1},{5,3},... | collective-permute-start | bytes 589832 | tf_op jit(solution)/shard_map/ppermute | solution.py:291
  47.9 0.2 copy.23
  48.2 3.5 %collective-permute-done.9.refs_4_ = bf16[128,768]{1,0:T(8,128)(2,1)S(1)} collective-permute-done((bf16[128,768]{1,0:T(8,128)(2,1)}, bf16[128,768]{1,0:T(8,128)(2,1)S(1)}, u32[]{:S(2)}, u32[]{:S(2)}) %collective-permute-start.9) | collective-permute-done | bytes 196640 | tf_op jit(solution)/shard_map/ppermute | solution.py:291
  51.6 1.8 %pick_rows.5 = bf16[16,3,8,768]{3,2,1,0:T(8,128)(2,1)} custom-call(s32[2]{0:T(128)S(1)} %pad_add_fusion.refs_0_.at_ref, s32[8,128]{1,0:T(8,128)S(1)} %bitcast.19, bf16[256,768]{1,0:T(8,128)(2,1)S(1)} %collective-permute-done.7.refs_2_, bf16[256,768]{1,0:T(8,128)(2,1)S(1)} %collective-permute-done.8.refs_3_, ...), custom_call_target="tpu_custom_call" | custom-call | tf_op jit(solution)/shard_map/pick_rows/pallas_call | solution.py:52
  53.4 7.4 %all-to-all-start.3 = ((bf16[16,3,8,768]{3,2,1,0:T(8,128)(2,1)}), bf16[16,3,8,768]{3,2,1,0:T(8,128)(2,1)S(1)}, u32[]{:S(2)}, u32[]{:S(2)}) async-start(bf16[16,3,8,768]{3,2,1,0:T(8,128)(2,1)} %pick_rows.5), calls=%async_computation.3 | async-start | bytes 1179648 | tf_op jit(solution)/shard_map/all_to_all | solution.py:314
  60.8 1.0 copy-done.10
  61.7 1.0 copy-done.12
  62.7 0.8 pick_rows.4
  63.6 0.7 copy-done.8
  64.3 4.9 %all-to-all-done.3.refs_2_ = bf16[16,3,8,768]{3,2,1,0:T(8,128)(2,1)S(1)} async-done(((bf16[16,3,8,768]{3,2,1,0:T(8,128)(2,1)}), bf16[16,3,8,768]{3,2,1,0:T(8,128)(2,1)S(1)}, u32[]{:S(2)}, u32[]{:S(2)}) %all-to-all-start.3) | async-done | bytes 589856 | tf_op jit(solution)/shard_map/all_to_all | solution.py:314
  69.2 6.1 %all-to-all-start.2 = ((bf16[16,2,8,768]{3,2,1,0:T(8,128)(2,1)}), bf16[16,2,8,768]{3,2,1,0:T(8,128)(2,1)}, u32[]{:S(2)}, u32[]{:S(2)}) async-start(bf16[16,2,8,768]{3,2,1,0:T(8,128)(2,1)} %copy-done.8), calls=%async_computation.2 | async-start | bytes 786432 | tf_op jit(solution)/shard_map/all_to_all | solution.py:314
  75.3 0.5 collective-permute-start.11
  75.8 6.9 %all-to-all-done.2.refs_2_ = bf16[16,2,8,768]{3,2,1,0:T(8,128)(2,1)} async-done(((bf16[16,2,8,768]{3,2,1,0:T(8,128)(2,1)}), bf16[16,2,8,768]{3,2,1,0:T(8,128)(2,1)}, u32[]{:S(2)}, u32[]{:S(2)}) %all-to-all-start.2) | async-done | bytes 393248 | tf_op jit(solution)/shard_map/all_to_all | solution.py:314
  82.7 0.7 reshape_squeeze.3
  83.4 1.6 %copy.20 = s32[8,16,8]{2,1,0:T(8,128)} copy(s32[8,16,8]{0,1,2:T(8,128)} %bitcast.24) | data formatting | bytes 8192 | tf_op jit(solution)/shard_map/transpose | solution.py:297
  85.0 0.9 reshape.55.refs_2_.refs_3_
  85.9 0.8 collective-permute-start.3
  86.7 0.8 collective-permute-done.3.refs_4_.refs_5_.refs_3_
  87.5 4.1 %shard_map.112.refs_1_ = f32[768,1024]{1,0:T(8,128)S(1)} custom-call(s32[2]{0:T(128)S(1)} %pad_add_fusion.refs_0_.at_ref, bf16[16,3,8,768]{3,2,1,0:T(8,128)(2,1)S(1)} %all-to-all-done.1.refs_1_, s32[8,128]{1,0:T(8,128)S(1)} %reshape.55.refs_2_.refs_3_, bf16[16,3,8,768]{3,2,1,0:T(8,128)(2,1)} %collective-permute-done.2.refs_3_, ...), custom_call_target="tpu_custom_call" | custom-call | tf_op jit(solution)/shard_map/pallas_call | solution.py:115
  91.6 1.6 %copy-done.2 = f32[768,1024]{1,0:T(8,128)} copy-done((f32[768,1024]{1,0:T(8,128)}, f32[768,1024]{1,0:T(8,128)S(1)}, u32[]{:S(2)}) %copy-start.2) | copy-done | bytes 3145752
  93.3 4.0 %shard_map.113.refs_1_ = f32[768,1024]{1,0:T(8,128)S(1)} custom-call(s32[2]{0:T(128)S(1)} %pad_add_fusion.refs_0_.at_ref, f32[768,1024]{1,0:T(8,128)} %copy-done.2, bf16[16,2,8,768]{3,2,1,0:T(8,128)(2,1)} %all-to-all-done.2.refs_2_, s32[8,128]{1,0:T(8,128)S(1)} %reshape.55.refs_2_.refs_3_, bf16[16,2,8,768]{3,2,1,0:T(8,128)(2,1)} %collective-permute-done.6.refs_4_, ...), custom_call_target="tpu_custom_call" | custom-call | tf_op jit(solution)/shard_map/pallas_call | solution.py:115
  97.3 1.6 %copy-done.3 = f32[768,1024]{1,0:T(8,128)} copy-done((f32[768,1024]{1,0:T(8,128)}, f32[768,1024]{1,0:T(8,128)S(1)}, u32[]{:S(2)}) %copy-start.3) | copy-done | bytes 3145752
  98.9 3.6 %shard_map.114.refs_1_ = f32[768,1024]{1,0:T(8,128)S(1)} custom-call(s32[2]{0:T(128)S(1)} %pad_add_fusion.refs_0_.at_ref, f32[768,1024]{1,0:T(8,128)} %copy-done.3, bf16[16,3,8,768]{3,2,1,0:T(8,128)(2,1)S(1)} %all-to-all-done.3.refs_2_, s32[8,128]{1,0:T(8,128)S(1)} %reshape.55.refs_2_.refs_3_, bf16[768,1024]{1,0:T(8,128)(2,1)S(1)} %copy-done.1), custom_call_target="tpu_custom_call" | custom-call | tf_op jit(solution)/shard_map/pallas_call | solution.py:115
  102.6 3.3 %shard_map.115 = (f32[512,1024]{1,0:T(8,128)S(1)}, bf16[768,1024]{1,0:T(8,128)(2,1)S(1)}, bf16[256,1024]{1,0:T(8,128)(2,1)S(1)}) custom-call(s32[2]{0:T(128)S(1)} %pad_add_fusion.refs_0_.at_ref, f32[768,1024]{1,0:T(8,128)S(1)} %shard_map.114.refs_1_, bf16[16,3,8,768]{3,2,1,0:T(8,128)(2,1)} %collective-permute-done.11.refs_2_, ...), custom_call_target="tpu_custom_call" | custom-call | tf_op jit(solution)/shard_map/pallas_call | solution.py:115
  105.9 4.3 %collective-permute-start.12 = (bf16[256,1024]{1,0:T(8,128)(2,1)S(1)}, bf16[256,1024]{1,0:T(8,128)(2,1)S(1)}, u32[]{:S(2)}, u32[]{:S(2)}) collective-permute-start(bf16[256,1024]{1,0:T(8,128)(2,1)S(1)} %get-tuple-element.18), channel_id=1, source_target_pairs={{16,1},{32,17},{48,33},{64,49},{80,65},{96,81},{112,97},{128,113},... | collective-permute-start | bytes 1572872 | tf_op jit(solution)/shard_map/ppermute | solution.py:367
  110.2 5.1 %near_projections.1 = (bf16[512,1024]{1,0:T(8,128)(2,1)S(1)}, bf16[768,1024]{1,0:T(8,128)(2,1)S(1)}, bf16[1024,768]{1,0:T(8,128)(2,1)S(1)}) custom-call(s32[2]{0:T(128)S(1)} %pad_add_fusion.refs_0_.at_ref, bf16[768,1024]{1,0:T(8,128)(2,1)S(1)} %get-tuple-element.14.x_ref, bf16[1024,1024]{1,0:T(8,128)(2,1)S(1)} %copy-done.7, ...), custom_call_target="tpu_custom_call" | custom-call | tf_op jit(solution)/shard_map/near_projections/pallas_call | solution.py:146
  115.3 3.1 %collective-permute-done.12.far_ref = bf16[256,1024]{1,0:T(8,128)(2,1)S(1)} collective-permute-done((bf16[256,1024]{1,0:T(8,128)(2,1)S(1)}, bf16[256,1024]{1,0:T(8,128)(2,1)S(1)}, u32[]{:S(2)}, u32[]{:S(2)}) %collective-permute-start.12) | collective-permute-done | bytes 524320 | tf_op jit(solution)/shard_map/ppermute | solution.py:367
  118.5 12.4 %window_attention.1 = bf16[512,1024]{1,0:T(8,128)(2,1)} custom-call(bf16[512,1024]{1,0:T(8,128)(2,1)S(1)} %get-tuple-element.15.q_ref, bf16[768,1024]{1,0:T(8,128)(2,1)S(1)} %get-tuple-element.16.k_ref, bf16[1024,768]{1,0:T(8,128)(2,1)S(1)} %get-tuple-element.17.v_ref, bf16[256,1024]{1,0:T(8,128)(2,1)S(1)} %collective-permute-done.12.far_ref, ...), custom_call_target="tpu_custom_call" | custom-call | tf_op jit(solution)/shard_map/window_attention/pallas_call | solution.py:241
  (45 shorter events, 0.5 us)
Async XLA Ops:
  0.0 25.6 %copy-start = (bf16[256,64,16]{0,2,1:T(8,128)(2,1)S(1)}, bf16[256,64,16]{0,2,1:T(8,128)(2,1)}, u32[]{:S(2)}) copy-start(bf16[256,64,16]{0,2,1:T(8,128)(2,1)} %param.21) | copy-start | bytes 1572868
  0.0 15.2 %collective-permute-start = (bf16[256,768]{1,0:T(8,128)(2,1)}, bf16[256,768]{1,0:T(8,128)(2,1)S(1)}, u32[]{:S(2)}, u32[]{:S(2)}) collective-permute-start(bf16[256,768]{1,0:T(8,128)(2,1)} %refs_2_.1), channel_id=1, source_target_pairs={{0,2},{2,4},{4,6},{6,8},{8,10},{10,12},{12,14},{14,0},{1,3},{3,5},... | collective-permute-start | bytes 1179656 | tf_op jit(solution)/shard_map/ppermute | solution.py:291
  1.9 13.3 %collective-permute-start.1 = (bf16[256,768]{1,0:T(8,128)(2,1)}, bf16[256,768]{1,0:T(8,128)(2,1)S(1)}, u32[]{:S(2)}, u32[]{:S(2)}) collective-permute-start(bf16[256,768]{1,0:T(8,128)(2,1)} %refs_2_.1), channel_id=1, source_target_pairs={{2,0},{4,2},{6,4},{8,6},{10,8},{12,10},{14,12},{0,14},{3,1},{5,3},... | collective-permute-start | bytes 1179656 | tf_op jit(solution)/shard_map/ppermute | solution.py:291
  15.2 11.5 %collective-permute-start.4 = (bf16[256,768]{1,0:T(8,128)(2,1)S(1)}, bf16[256,768]{1,0:T(8,128)(2,1)S(1)}, u32[]{:S(2)}, u32[]{:S(2)}) collective-permute-start(bf16[256,768]{1,0:T(8,128)(2,1)S(1)} %collective-permute-done.refs_3_), channel_id=1, source_target_pairs={{0,2},{2,4},{4,6},{6,8},{8,10},{10,12},{12,14},{14,0},{1,3},{3,5},... | collective-permute-start | bytes 1179656 | tf_op jit(solution)/shard_map/ppermute | solution.py:291
  15.2 12.6 %collective-permute-start.5 = (bf16[256,768]{1,0:T(8,128)(2,1)S(1)}, bf16[256,768]{1,0:T(8,128)(2,1)S(1)}, u32[]{:S(2)}, u32[]{:S(2)}) collective-permute-start(bf16[256,768]{1,0:T(8,128)(2,1)S(1)} %collective-permute-done.1.refs_4_), channel_id=1, source_target_pairs={{2,0},{4,2},{6,4},{8,6},{10,8},{12,10},{14,12},{0,14},{3,1},{5,3},... | collective-permute-start | bytes 1179656 | tf_op jit(solution)/shard_map/ppermute | solution.py:291
  20.0 13.3 %all-to-all-start = ((s32[8,1,128]{2,1,0:T(1,128)}), s32[8,1,128]{2,1,0:T(1,128)S(1)}, u32[]{:S(2)}, u32[]{:S(2)}) async-start(s32[8,1,128]{2,1,0:T(1,128)} %bitcast.4), calls=%async_computation | async-start | bytes 8192 | tf_op jit(solution)/shard_map/all_to_all | solution.py:303
  26.7 17.9 %copy-start.9 = (bf16[256,768]{1,0:T(8,128)(2,1)}, bf16[256,768]{1,0:T(8,128)(2,1)S(1)}, u32[]{:S(2)}) copy-start(bf16[256,768]{1,0:T(8,128)(2,1)S(1)} %collective-permute-done.4.refs_2_) | copy-start | bytes 1179652
  26.7 17.2 %collective-permute-start.7 = (bf16[256,768]{1,0:T(8,128)(2,1)S(1)}, bf16[256,768]{1,0:T(8,128)(2,1)S(1)}, u32[]{:S(2)}, u32[]{:S(2)}) collective-permute-start(bf16[256,768]{1,0:T(8,128)(2,1)S(1)} %collective-permute-done.4.refs_2_), channel_id=1, source_target_pairs={{0,2},{2,4},{4,6},{6,8},{8,10},{10,12},{12,14},{14,0},{1,3},{3,5},... | collective-permute-start | bytes 1179656 | tf_op jit(solution)/shard_map/ppermute | solution.py:291
  27.8 16.7 %copy-start.11 = (bf16[256,768]{1,0:T(8,128)(2,1)}, bf16[256,768]{1,0:T(8,128)(2,1)S(1)}, u32[]{:S(2)}) copy-start(bf16[256,768]{1,0:T(8,128)(2,1)S(1)} %collective-permute-done.5.refs_3_) | copy-start | bytes 1179652
  27.8 17.2 %collective-permute-start.8 = (bf16[256,768]{1,0:T(8,128)(2,1)S(1)}, bf16[256,768]{1,0:T(8,128)(2,1)S(1)}, u32[]{:S(2)}, u32[]{:S(2)}) collective-permute-start(bf16[256,768]{1,0:T(8,128)(2,1)S(1)} %collective-permute-done.5.refs_3_), channel_id=1, source_target_pairs={{2,0},{4,2},{6,4},{8,6},{10,8},{12,10},{14,12},{0,14},{3,1},{5,3},... | collective-permute-start | bytes 1179656 | tf_op jit(solution)/shard_map/ppermute | solution.py:291
  33.3 1.0 copy-start.13
  36.0 17.4 %all-to-all-start.1 = ((bf16[16,3,8,768]{3,2,1,0:T(8,128)(2,1)}), bf16[16,3,8,768]{3,2,1,0:T(8,128)(2,1)S(1)}, u32[]{:S(2)}, u32[]{:S(2)}) async-start(bf16[16,3,8,768]{3,2,1,0:T(8,128)(2,1)} %pick_rows.3), calls=%async_computation.1 | async-start | bytes 1179648 | tf_op jit(solution)/shard_map/all_to_all | solution.py:314
  44.5 7.1 %collective-permute-start.9 = (bf16[128,768]{1,0:T(8,128)(2,1)}, bf16[128,768]{1,0:T(8,128)(2,1)S(1)}, u32[]{:S(2)}, u32[]{:S(2)}) collective-permute-start(bf16[128,768]{1,0:T(8,128)(2,1)} %slice.8), channel_id=1, source_target_pairs={{0,2},{2,4},{4,6},{6,8},{8,10},{10,12},{12,14},{14,0},{1,3},{3,5},... | collective-permute-start | bytes 589832 | tf_op jit(solution)/shard_map/ppermute | solution.py:291
  45.0 6.6 %collective-permute-start.10 = (bf16[128,768]{1,0:T(8,128)(2,1)S(1)}, bf16[128,768]{1,0:T(8,128)(2,1)S(1)}, u32[]{:S(2)}, u32[]{:S(2)}) collective-permute-start(bf16[128,768]{1,0:T(8,128)(2,1)S(1)} %slice.9), channel_id=1, source_target_pairs={{2,0},{4,2},{6,4},{8,6},{10,8},{12,10},{14,12},{0,14},{3,1},{5,3},... | collective-permute-start | bytes 589832 | tf_op jit(solution)/shard_map/ppermute | solution.py:291
  48.1 34.6 %copy-start.15 = (s32[128,1,1,8]{0,3,2,1:T(8,128)S(1)}, s32[128,1,1,8]{0,3,2,1:T(8,128)}, u32[]{:S(2)}) copy-start(s32[128,1,1,8]{0,3,2,1:T(8,128)} %param.14) | copy-start | bytes 12292
  53.4 34.2 %copy-start.1 = (bf16[768,1024]{1,0:T(8,128)(2,1)S(1)}, bf16[768,1024]{1,0:T(8,128)(2,1)}, u32[]{:S(2)}) copy-start(bf16[768,1024]{1,0:T(8,128)(2,1)} %refs_4_.3) | copy-start | bytes 4718596
  53.4 15.8 %all-to-all-start.3 = ((bf16[16,3,8,768]{3,2,1,0:T(8,128)(2,1)}), bf16[16,3,8,768]{3,2,1,0:T(8,128)(2,1)S(1)}, u32[]{:S(2)}, u32[]{:S(2)}) async-start(bf16[16,3,8,768]{3,2,1,0:T(8,128)(2,1)} %pick_rows.5), calls=%async_computation.3 | async-start | bytes 1179648 | tf_op jit(solution)/shard_map/all_to_all | solution.py:314
  60.7 1.0 copy-start.10
  61.7 1.0 copy-start.12
  63.6 0.7 copy-start.8
  69.2 13.5 %all-to-all-start.2 = ((bf16[16,2,8,768]{3,2,1,0:T(8,128)(2,1)}), bf16[16,2,8,768]{3,2,1,0:T(8,128)(2,1)}, u32[]{:S(2)}, u32[]{:S(2)}) async-start(bf16[16,2,8,768]{3,2,1,0:T(8,128)(2,1)} %copy-done.8), calls=%async_computation.2 | async-start | bytes 786432 | tf_op jit(solution)/shard_map/all_to_all | solution.py:314
  75.3 12.2 %collective-permute-start.2 = (bf16[16,3,8,768]{3,2,1,0:T(8,128)(2,1)S(1)}, bf16[16,3,8,768]{3,2,1,0:T(8,128)(2,1)}, u32[]{:S(2)}, u32[]{:S(2)}) collective-permute-start(bf16[16,3,8,768]{3,2,1,0:T(8,128)(2,1)S(1)} %all-to-all-done.1.refs_1_), channel_id=1, source_target_pairs={{0,1},{1,0},{2,3},{3,2},{4,5},{5,4},{6,7},{7,6},{8,9},{9,8},{10,11... | collective-permute-start | bytes 1769480 | tf_op jit(solution)/shard_map/ppermute | solution.py:315
  75.3 27.2 %collective-permute-start.11 = (bf16[16,3,8,768]{3,2,1,0:T(8,128)(2,1)S(1)}, bf16[16,3,8,768]{3,2,1,0:T(8,128)(2,1)}, u32[]{:S(2)}, u32[]{:S(2)}) collective-permute-start(bf16[16,3,8,768]{3,2,1,0:T(8,128)(2,1)S(1)} %all-to-all-done.3.refs_2_), channel_id=1, source_target_pairs={{0,1},{1,0},{2,3},{3,2},{4,5},{5,4},{6,7},{7,6},{8,9},{9,8},{10,11... | collective-permute-start | bytes 1769480 | tf_op jit(solution)/shard_map/ppermute | solution.py:315
  82.7 10.6 %collective-permute-start.6 = (bf16[16,2,8,768]{3,2,1,0:T(8,128)(2,1)}, bf16[16,2,8,768]{3,2,1,0:T(8,128)(2,1)}, u32[]{:S(2)}, u32[]{:S(2)}) collective-permute-start(bf16[16,2,8,768]{3,2,1,0:T(8,128)(2,1)} %all-to-all-done.2.refs_2_), channel_id=1, source_target_pairs={{0,1},{1,0},{2,3},{3,2},{4,5},{5,4},{6,7},{7,6},{8,9},{9,8},{10,11... | collective-permute-start | bytes 1179656 | tf_op jit(solution)/shard_map/ppermute | solution.py:315
  85.9 1.6 %collective-permute-start.3 = (s32[8,128]{1,0:T(8,128)S(1)}, s32[8,128]{1,0:T(8,128)S(1)}, u32[]{:S(2)}, u32[]{:S(2)}) collective-permute-start(s32[8,128]{1,0:T(8,128)S(1)} %reshape.55.refs_2_.refs_3_), channel_id=1, source_target_pairs={{0,1},{1,0},{2,3},{3,2},{4,5},{5,4},{6,7},{7,6},{8,9},{9,8},{10,11... | collective-permute-start | bytes 12296 | tf_op jit(solution)/shard_map/ppermute | solution.py:302
  91.6 1.6 %copy-start.2 = (f32[768,1024]{1,0:T(8,128)}, f32[768,1024]{1,0:T(8,128)S(1)}, u32[]{:S(2)}) copy-start(f32[768,1024]{1,0:T(8,128)S(1)} %shard_map.112.refs_1_) | copy-start | bytes 9437188
  97.3 1.6 %copy-start.3 = (f32[768,1024]{1,0:T(8,128)}, f32[768,1024]{1,0:T(8,128)S(1)}, u32[]{:S(2)}) copy-start(f32[768,1024]{1,0:T(8,128)S(1)} %shard_map.113.refs_1_) | copy-start | bytes 9437188
  98.9 3.6 %copy-start.14 = (f32[1024]{0:T(1024)S(1)}, f32[1024]{0:T(1024)}, u32[]{:S(2)}) copy-start(f32[1024]{0:T(1024)} %param.16) | copy-start | bytes 12292
  98.9 11.3 %copy-start.7 = (bf16[1024,1024]{1,0:T(8,128)(2,1)S(1)}, bf16[1024,1024]{1,0:T(8,128)(2,1)}, u32[]{:S(2)}) copy-start(bf16[1024,1024]{1,0:T(8,128)(2,1)} %wq_ref.1) | copy-start | bytes 6291460
  102.5 7.7 %copy-start.4 = (bf16[1024,1024]{1,0:T(8,128)(2,1)S(1)}, bf16[1024,1024]{1,0:T(8,128)(2,1)}, u32[]{:S(2)}) copy-start(bf16[1024,1024]{1,0:T(8,128)(2,1)} %wk_ref.3) | copy-start | bytes 6291460
  102.5 7.7 %copy-start.5 = (bf16[1024,1024]{1,0:T(8,128)(2,1)S(1)}, bf16[1024,1024]{1,0:T(8,128)(2,1)}, u32[]{:S(2)}) copy-start(bf16[1024,1024]{1,0:T(8,128)(2,1)} %wv_ref.3) | copy-start | bytes 6291460
  105.9 12.6 %collective-permute-start.12 = (bf16[256,1024]{1,0:T(8,128)(2,1)S(1)}, bf16[256,1024]{1,0:T(8,128)(2,1)S(1)}, u32[]{:S(2)}, u32[]{:S(2)}) collective-permute-start(bf16[256,1024]{1,0:T(8,128)(2,1)S(1)} %get-tuple-element.18), channel_id=1, source_target_pairs={{16,1},{32,17},{48,33},{64,49},{80,65},{96,81},{112,97},{128,113},... | collective-permute-start | bytes 1572872 | tf_op jit(solution)/shard_map/ppermute | solution.py:367
  110.2 8.3 %copy-start.6 = (bf16[1024,1024]{1,0:T(8,128)(2,1)S(1)}, bf16[1024,1024]{1,0:T(8,128)(2,1)}, u32[]{:S(2)}) copy-start(bf16[1024,1024]{1,0:T(8,128)(2,1)} %wo_ref.1) | copy-start | bytes 6291460

commit v5 on v3

--- a/solution.py
+++ b/solution.py
@@ -23,7 +23,7 @@
     blocks, out_ref = refs[:-1], refs[-1]
     used = 0
     for i, offset in enumerate(offsets):
-        parts = 2 if offset == n_x // 2 else 1
+        parts = 2
         line = (at_ref[0] + (offset + n_x)) % n_x
         index = route_ref[pl.ds(line, 1), :]
         base = 0
@@ -288,21 +288,24 @@
     swap = [(0, 1), (1, 0)]
     at = jnp.stack([col, core * edge]).astype(jnp.int32)
 
-    def shift(value, perm):
-        return lax.ppermute(value, "bevx", perm)
-
-    u1 = shift(image_tokens, up)
-    d1 = shift(image_tokens, down)
+    half = tokens // 2
+    own = [image_tokens[:half], image_tokens[half:]]
+
+    def shift(values, perm, pieces=(0, 1)):
+        moved = []
+        for piece in pieces:
+            moved.append(lax.ppermute(values[piece], "bevx", perm))
+        return moved
+
+    u1 = shift(own, up)
+    d1 = shift(own, down)
 
     def by_column(value):
         return value.reshape(n_y, n_x, slot_count).transpose(1, 0, 2).reshape(n_x, -1)
 
-    is_live = (
-        lax.broadcasted_iota(jnp.int32, route_token.shape[2:], 1) < slot_counts[0, 0][:, None]
-    )
-    route = by_column(jnp.where(is_live, route_token[0, 0], -1))
+    slot = lax.broadcasted_iota(jnp.int32, route_token.shape, 3)
+    route = by_column(jnp.where(slot < slot_counts[..., None], route_token, -1))
     cells = by_column(route_cell[:, 0, 0, :])
-    route, cells = lax.optimization_barrier((route, cells))
     cells_other = lax.ppermute(cells, "cam", swap)
     route = lax.all_to_all(route, "bevx", split_axis=0, concat_axis=0, tiled=True)
 
@@ -310,17 +313,14 @@
     d2 = shift(d1, down)
     u3 = shift(u2, up)
     d3 = shift(d2, down)
-    half = tokens // 2
-    u4 = shift(u3[:half], up)
-    d4 = shift(d3[half:], down)
+    u4 = shift(u3, up, (0,))
+    d4 = shift(d3, down, (1,))
 
     near_row = (row * 2 + core) * ROWS_DEV - core * HALO
     far_row = (row * 2 + core) * ROWS_DEV + jnp.where(core == 0, -HALO, ROWS_DEV)
     far_ok = (far_row >= 0) & (far_row < grid_rows)
     near_bias = lax.dynamic_slice_in_dim(key_bias, near_row, ROWS_DEV + HALO, 0)
-    far_bias = lax.dynamic_slice_in_dim(
-        key_bias, jnp.clip(far_row, 0, grid_rows - HALO), HALO, 0
-    )
+    far_bias = lax.dynamic_slice_in_dim(key_bias, jnp.clip(far_row, 0, grid_rows - HALO), HALO, 0)
     far_bias = jnp.where(far_ok, far_bias, jnp.asarray(MASKED, jnp.bfloat16))
     bias = jnp.concatenate([near_bias, far_bias], axis=0).reshape(-1, head_count)
     bias = jnp.pad(bias, ((0, 0), (0, 1)), constant_values=1)
@@ -330,7 +330,7 @@
         got = lax.all_to_all(rows, "bevy", split_axis=0, concat_axis=0, tiled=True)
         return got, lax.ppermute(got, "cam", swap)
 
-    rows = pick(EARLY, n_x, n_y, at, route, (image_tokens, u1, d1, u2, d2))
+    rows = pick(EARLY, n_x, n_y, at, route, (*own, *u1, *d1, *u2, *d2))
     rows, bias, cells_other = lax.optimization_barrier((rows, bias, cells_other))
     early, early_other = exchange(rows)
     total = jax.ShapeDtypeStruct((ext, width), jnp.float32)
@@ -342,7 +342,7 @@
         (at, lifted, early_other, cells_other, lift_weight),
         [total],
     )
-    rows = pick(LATE, n_x, n_y, at, route, (u3, d3, u4, d4))
+    rows = pick(LATE, n_x, n_y, at, route, (*u3, *d3, *u4, *d4))
     late, late_other = exchange(rows)
     [lifted] = local_call(
         lambda *refs: next_sum_kernel(n_x, *refs),

time: 118 us -> 120 us (1.017)
  starting transfers between devices: 40.5 us -> 49.7 us
  waiting for transfers between devices: 33 us -> 26.9 us
    ppermute x8 -> x14, starting transfers between devices: 15.8 us -> 24.5 us  [shift(): moved.append(lax.ppermute(values[piece], 'bevx', perm))]
    all_to_all x1, waiting for transfers between devices: 3.03 us -> 0.01 us  [steps(): lax.all_to_all(route, 'bevx', split_axis=0, concat_axis=0, tiled=True)]
    ppermute x8 -> x14, waiting for transfers between devices: 18.2 us -> 15.4 us  [shift(): moved.append(lax.ppermute(values[piece], 'bevx', perm))]
    unnamed x1 -> x0, other arithmetic: 1.32 us -> none
    unnamed x27 -> x28, local copies, waits for them, and re-layouts: 3.59 us -> 4 us
  transfers between devices with their start and end apart: 15 -> 21, of which waited for: 8 -> 10; matrix products, arithmetic and copies ran while one was open for 5% -> 3% of each run, Pallas kernels for 16% -> 15%
where the time goes in v5:
time: 120 us; the launch traced here: 118 us
  starting transfers between devices  49.7 us (41%)
  Pallas kernels  32.9 us (27%)
  waiting for transfers between devices  26.9 us (22%)
  local copies, waits for them, and re-layouts  7.41 us (6%)
    ppermute x14, starting transfers between devices, shift(): moved.append(lax.ppermute(values[piece], 'bevx', perm))  24.5 us
    ppermute x14, waiting for transfers between devices, shift(): moved.append(lax.ppermute(values[piece], 'bevx', perm))  15.4 us
    all_to_all x2, starting transfers between devices, exchange(): got = lax.all_to_all(rows, 'bevy', split_axis=0, concat_axis=0, tiled=True)  14.8 us
    pallas_call x4, Pallas kernels, local_call(): pl.pallas_call(kernel, in_specs=[SCALAR] + [pl.BlockSpec(memory_space=plt...  13.1 us
    pallas_call x1, Pallas kernels, attention(): pl.pallas_call(attention_kernel, grid=(width // block,), in_specs=[LOCAL]...  12.4 us
    all_to_all x2, waiting for transfers between devices, exchange(): got = lax.all_to_all(rows, 'bevy', split_axis=0, concat_axis=0, tiled=True)  8.55 us
    all_to_all x1, starting transfers between devices, steps(): lax.all_to_all(route, 'bevx', split_axis=0, concat_axis=0, tiled=True)  5.76 us
    pallas_call x1, Pallas kernels, project(): pl.pallas_call(project_kernel, in_specs=[SCALAR] + [LOCAL] * 4, out_specs...  5.11 us
  transfers between devices with their start and end apart: 21, of which 10 were waited for; matrix products, arithmetic and copies ran while one was open for 3% of the time, Pallas kernels for 15%

profile of v5, /device:TPU:8, one launch (start us, length us, event | category | flops | bytes accessed | tf_op | source)
XLA Modules:
  0.0 118.0 jit_solution(89614494221974151)
XLA Ops:
  0.0 1.1 fusion.2
  1.1 2.0 %collective-permute-start = (bf16[128,768]{1,0:T(8,128)(2,1)S(1)}, bf16[128,768]{1,0:T(8,128)(2,1)S(1)}, u32[]{:S(2)}, u32[]{:S(2)}) collective-permute-start(bf16[128,768]{1,0:T(8,128)(2,1)S(1)} %get-tuple-element.24.refs_2_), channel_id=1, source_target_pairs={{0,2},{2,4},{4,6},{6,8},{8,10},{10,12},{12,14},{14,0},{1,3},{3,5},... | collective-permute-start | bytes 589832 | tf_op jit(solution)/shard_map/ppermute | solution.py:297
  3.1 4.0 %collective-permute-start.2 = (bf16[128,768]{1,0:T(8,128)(2,1)S(1)}, bf16[128,768]{1,0:T(8,128)(2,1)S(1)}, u32[]{:S(2)}, u32[]{:S(2)}) collective-permute-start(bf16[128,768]{1,0:T(8,128)(2,1)S(1)} %get-tuple-element.24.refs_2_), channel_id=1, source_target_pairs={{2,0},{4,2},{6,4},{8,6},{10,8},{12,10},{14,12},{0,14},{3,1},{5,3},... | collective-permute-start | bytes 589832 | tf_op jit(solution)/shard_map/ppermute | solution.py:297
  7.1 3.2 %collective-permute-start.3 = (bf16[128,768]{1,0:T(8,128)(2,1)S(1)}, bf16[128,768]{1,0:T(8,128)(2,1)S(1)}, u32[]{:S(2)}, u32[]{:S(2)}) collective-permute-start(bf16[128,768]{1,0:T(8,128)(2,1)S(1)} %get-tuple-element.23.refs_3_), channel_id=1, source_target_pairs={{2,0},{4,2},{6,4},{8,6},{10,8},{12,10},{14,12},{0,14},{3,1},{5,3},... | collective-permute-start | bytes 589832 | tf_op jit(solution)/shard_map/ppermute | solution.py:297
  10.4 0.7 fusion.1
  11.2 0.1 copy.18
  11.3 0.7 all_to_all.13
  11.9 5.8 %all-to-all-start = ((s32[8,1,128]{2,1,0:T(1,128)}), s32[8,1,128]{2,1,0:T(1,128)S(1)}, u32[]{:S(2)}, u32[]{:S(2)}) async-start(s32[8,1,128]{2,1,0:T(1,128)} %bitcast.4), calls=%async_computation | async-start | bytes 8192 | tf_op jit(solution)/shard_map/all_to_all | solution.py:310
  17.7 0.8 reshape_squeeze.3
  18.5 0.1 copy.23
  18.8 0.1 constant_dynamic-slice_fusion
  19.0 0.3 copy.25
  19.3 0.1 constant_dynamic-slice_fusion.1
  19.4 0.3 copy.24
  19.7 0.2 copy.22
  19.9 2.1 %collective-permute-start.4 = (bf16[128,768]{1,0:T(8,128)(2,1)S(1)}, bf16[128,768]{1,0:T(8,128)(2,1)S(1)}, u32[]{:S(2)}, u32[]{:S(2)}) collective-permute-start(bf16[128,768]{1,0:T(8,128)(2,1)S(1)} %collective-permute-done.refs_4_), channel_id=1, source_target_pairs={{0,2},{2,4},{4,6},{6,8},{8,10},{10,12},{12,14},{14,0},{1,3},{3,5},... | collective-permute-start | bytes 589832 | tf_op jit(solution)/shard_map/ppermute | solution.py:297
  22.0 1.5 %collective-permute-start.5 = (bf16[128,768]{1,0:T(8,128)(2,1)S(1)}, bf16[128,768]{1,0:T(8,128)(2,1)S(1)}, u32[]{:S(2)}, u32[]{:S(2)}) collective-permute-start(bf16[128,768]{1,0:T(8,128)(2,1)S(1)} %collective-permute-done.1.refs_5_), channel_id=1, source_target_pairs={{0,2},{2,4},{4,6},{6,8},{8,10},{10,12},{12,14},{14,0},{1,3},{3,5},... | collective-permute-start | bytes 589832 | tf_op jit(solution)/shard_map/ppermute | solution.py:297
  23.5 1.8 %collective-permute-start.6 = (bf16[128,768]{1,0:T(8,128)(2,1)S(1)}, bf16[128,768]{1,0:T(8,128)(2,1)S(1)}, u32[]{:S(2)}, u32[]{:S(2)}) collective-permute-start(bf16[128,768]{1,0:T(8,128)(2,1)S(1)} %collective-permute-done.2.refs_6_), channel_id=1, source_target_pairs={{2,0},{4,2},{6,4},{8,6},{10,8},{12,10},{14,12},{0,14},{3,1},{5,3},... | collective-permute-start | bytes 589832 | tf_op jit(solution)/shard_map/ppermute | solution.py:297
  25.5 3.5 %collective-permute-done.4.refs_8_ = bf16[128,768]{1,0:T(8,128)(2,1)S(1)} collective-permute-done((bf16[128,768]{1,0:T(8,128)(2,1)S(1)}, bf16[128,768]{1,0:T(8,128)(2,1)S(1)}, u32[]{:S(2)}, u32[]{:S(2)}) %collective-permute-start.4) | collective-permute-done | bytes 196640 | tf_op jit(solution)/shard_map/ppermute | solution.py:297
  29.0 4.0 %collective-permute-done.5.refs_9_ = bf16[128,768]{1,0:T(8,128)(2,1)S(1)} collective-permute-done((bf16[128,768]{1,0:T(8,128)(2,1)S(1)}, bf16[128,768]{1,0:T(8,128)(2,1)S(1)}, u32[]{:S(2)}, u32[]{:S(2)}) %collective-permute-start.5) | collective-permute-done | bytes 196640 | tf_op jit(solution)/shard_map/ppermute | solution.py:297
  33.0 1.4 %collective-permute-done.7.refs_11_ = bf16[128,768]{1,0:T(8,128)(2,1)S(1)} collective-permute-done((bf16[128,768]{1,0:T(8,128)(2,1)S(1)}, bf16[128,768]{1,0:T(8,128)(2,1)S(1)}, u32[]{:S(2)}, u32[]{:S(2)}) %collective-permute-start.7) | collective-permute-done | bytes 196640 | tf_op jit(solution)/shard_map/ppermute | solution.py:297
  34.4 1.2 %pick_rows.2 = bf16[16,5,8,768]{3,2,1,0:T(8,128)(2,1)S(1)} custom-call(s32[2]{0:T(128)S(1)} %pad_add_fusion.refs_0_.at_ref, s32[8,128]{1,0:T(8,128)S(1)} %bitcast.18, bf16[128,768]{1,0:T(8,128)(2,1)S(1)} %get-tuple-element.24.refs_2_, bf16[128,768]{1,0:T(8,128)(2,1)S(1)} %get-tuple-element.23.refs_3_, bf16[128,768]{1,0:T(8,128)(2,1)S(1)} %collective-permute-done.refs_4_, ...), custom_call_target="tpu_custom_call" | custom-call | tf_op jit(solution)/shard_map/pick_rows/pallas_call | solution.py:51
  35.7 0.9 copy-done.5
  36.6 7.5 %all-to-all-start.1 = ((bf16[16,5,8,768]{3,2,1,0:T(8,128)(2,1)}), bf16[16,5,8,768]{3,2,1,0:T(8,128)(2,1)S(1)}, u32[]{:S(2)}, u32[]{:S(2)}) async-start(bf16[16,5,8,768]{3,2,1,0:T(8,128)(2,1)} %copy-done.5), calls=%async_computation.1 | async-start | bytes 1966080 | tf_op jit(solution)/shard_map/all_to_all | solution.py:330
  44.2 2.4 %collective-permute-start.10 = (bf16[128,768]{1,0:T(8,128)(2,1)}, bf16[128,768]{1,0:T(8,128)(2,1)S(1)}, u32[]{:S(2)}, u32[]{:S(2)}) collective-permute-start(bf16[128,768]{1,0:T(8,128)(2,1)} %copy-done.10), channel_id=1, source_target_pairs={{0,2},{2,4},{4,6},{6,8},{8,10},{10,12},{12,14},{14,0},{1,3},{3,5},... | collective-permute-start | bytes 589832 | tf_op jit(solution)/shard_map/ppermute | solution.py:297
  46.6 0.8 collective-permute-start.13
  47.4 1.2 %collective-permute-start.11 = (bf16[128,768]{1,0:T(8,128)(2,1)S(1)}, bf16[128,768]{1,0:T(8,128)(2,1)S(1)}, u32[]{:S(2)}, u32[]{:S(2)}) collective-permute-start(bf16[128,768]{1,0:T(8,128)(2,1)S(1)} %collective-permute-done.5.refs_9_), channel_id=1, source_target_pairs={{0,2},{2,4},{4,6},{6,8},{8,10},{10,12},{12,14},{14,0},{1,3},{3,5},... | collective-permute-start | bytes 589832 | tf_op jit(solution)/shard_map/ppermute | solution.py:297
  48.6 2.1 %collective-permute-start.12 = (bf16[128,768]{1,0:T(8,128)(2,1)}, bf16[128,768]{1,0:T(8,128)(2,1)S(1)}, u32[]{:S(2)}, u32[]{:S(2)}) collective-permute-start(bf16[128,768]{1,0:T(8,128)(2,1)} %copy-done.9), channel_id=1, source_target_pairs={{2,0},{4,2},{6,4},{8,6},{10,8},{12,10},{14,12},{0,14},{3,1},{5,3},... | collective-permute-start | bytes 589832 | tf_op jit(solution)/shard_map/ppermute | solution.py:297
  50.7 2.6 %collective-permute-done.10.refs_2_ = bf16[128,768]{1,0:T(8,128)(2,1)S(1)} collective-permute-done((bf16[128,768]{1,0:T(8,128)(2,1)}, bf16[128,768]{1,0:T(8,128)(2,1)S(1)}, u32[]{:S(2)}, u32[]{:S(2)}) %collective-permute-start.10) | collective-permute-done | bytes 196640 | tf_op jit(solution)/shard_map/ppermute | solution.py:297
  53.3 1.3 %collective-permute-start.14 = (bf16[128,768]{1,0:T(8,128)(2,1)S(1)}, bf16[128,768]{1,0:T(8,128)(2,1)S(1)}, u32[]{:S(2)}, u32[]{:S(2)}) collective-permute-start(bf16[128,768]{1,0:T(8,128)(2,1)S(1)} %collective-permute-done.10.refs_2_), channel_id=1, source_target_pairs={{0,2},{2,4},{4,6},{6,8},{8,10},{10,12},{12,14},{14,0},{1,3},{3,5},... | collective-permute-start | bytes 589832 | tf_op jit(solution)/shard_map/ppermute | solution.py:297
  54.6 2.0 %collective-permute-start.15 = (bf16[128,768]{1,0:T(8,128)(2,1)S(1)}, bf16[128,768]{1,0:T(8,128)(2,1)S(1)}, u32[]{:S(2)}, u32[]{:S(2)}) collective-permute-start(bf16[128,768]{1,0:T(8,128)(2,1)S(1)} %collective-permute-done.13.refs_5_), channel_id=1, source_target_pairs={{2,0},{4,2},{6,4},{8,6},{10,8},{12,10},{14,12},{0,14},{3,1},{5,3},... | collective-permute-start | bytes 589832 | tf_op jit(solution)/shard_map/ppermute | solution.py:297
  56.6 0.9 collective-permute-done.11.refs_3_
  57.5 0.9 collective-permute-done.12.refs_4_
  58.4 1.8 %collective-permute-done.14.refs_6_ = bf16[128,768]{1,0:T(8,128)(2,1)S(1)} collective-permute-done((bf16[128,768]{1,0:T(8,128)(2,1)S(1)}, bf16[128,768]{1,0:T(8,128)(2,1)S(1)}, u32[]{:S(2)}, u32[]{:S(2)}) %collective-permute-start.14) | collective-permute-done | bytes 196640 | tf_op jit(solution)/shard_map/ppermute | solution.py:297
  60.2 0.3 collective-permute-done.15.refs_7_
  60.5 1.0 pick_rows.3
  61.5 0.8 copy-done.6
  62.4 7.2 %all-to-all-start.2 = ((bf16[16,3,8,768]{3,2,1,0:T(8,128)(2,1)}), bf16[16,3,8,768]{3,2,1,0:T(8,128)(2,1)}, u32[]{:S(2)}, u32[]{:S(2)}) async-start(bf16[16,3,8,768]{3,2,1,0:T(8,128)(2,1)} %copy-done.6), calls=%async_computation.2 | async-start | bytes 1179648 | tf_op jit(solution)/shard_map/all_to_all | solution.py:330
  69.6 8.5 %all-to-all-done.2.refs_2_ = bf16[16,3,8,768]{3,2,1,0:T(8,128)(2,1)} async-done(((bf16[16,3,8,768]{3,2,1,0:T(8,128)(2,1)}), bf16[16,3,8,768]{3,2,1,0:T(8,128)(2,1)}, u32[]{:S(2)}, u32[]{:S(2)}) %all-to-all-start.2) | async-done | bytes 589856 | tf_op jit(solution)/shard_map/all_to_all | solution.py:330
  78.2 2.9 %shard_map.112.refs_1_ = f32[768,1024]{1,0:T(8,128)S(1)} custom-call(s32[2]{0:T(128)S(1)} %pad_add_fusion.refs_0_.at_ref, bf16[16,5,8,768]{3,2,1,0:T(8,128)(2,1)S(1)} %all-to-all-done.1.refs_1_, s32[8,128]{1,0:T(8,128)S(1)} %reshape.56.refs_2_.refs_3_, bf16[768,1024]{1,0:T(8,128)(2,1)S(1)} %copy-done.1), custom_call_target="tpu_custom_call" | custom-call | tf_op jit(solution)/shard_map/pallas_call | solution.py:116
  81.1 3.6 %shard_map.113.refs_1_ = f32[768,1024]{1,0:T(8,128)S(1)} custom-call(s32[2]{0:T(128)S(1)} %pad_add_fusion.refs_0_.at_ref, f32[768,1024]{1,0:T(8,128)S(1)} %shard_map.112.refs_1_, bf16[16,5,8,768]{3,2,1,0:T(8,128)(2,1)} %collective-permute-done.9.refs_2_, s32[8,128]{1,0:T(8,128)S(1)} %collective-permute-done.8.refs_3_, bf16[768,1024]{1,0:T(8,128)(2,1)S(1)} %copy-done.1), custom_call_target="tpu_custom_call" | custom-call | tf_op jit(solution)/shard_map/pallas_call | solution.py:116
  84.8 1.6 %copy-done.2 = f32[768,1024]{1,0:T(8,128)} copy-done((f32[768,1024]{1,0:T(8,128)}, f32[768,1024]{1,0:T(8,128)S(1)}, u32[]{:S(2)}) %copy-start.2) | copy-done | bytes 3145752
  86.4 3.9 %shard_map.114.refs_1_ = f32[768,1024]{1,0:T(8,128)S(1)} custom-call(s32[2]{0:T(128)S(1)} %pad_add_fusion.refs_0_.at_ref, f32[768,1024]{1,0:T(8,128)} %copy-done.2, bf16[16,3,8,768]{3,2,1,0:T(8,128)(2,1)} %all-to-all-done.2.refs_2_, s32[8,128]{1,0:T(8,128)S(1)} %reshape.56.refs_2_.refs_3_, bf16[768,1024]{1,0:T(8,128)(2,1)S(1)} %copy-done.1), custom_call_target="tpu_custom_call" | custom-call | tf_op jit(solution)/shard_map/pallas_call | solution.py:116
  90.3 2.6 %shard_map.115 = (f32[512,1024]{1,0:T(8,128)S(1)}, bf16[768,1024]{1,0:T(8,128)(2,1)S(1)}, bf16[256,1024]{1,0:T(8,128)(2,1)S(1)}) custom-call(s32[2]{0:T(128)S(1)} %pad_add_fusion.refs_0_.at_ref, f32[768,1024]{1,0:T(8,128)S(1)} %shard_map.114.refs_1_, bf16[16,3,8,768]{3,2,1,0:T(8,128)(2,1)S(1)} %collective-permute-done.16.refs_2_, ...), custom_call_target="tpu_custom_call" | custom-call | tf_op jit(solution)/shard_map/pallas_call | solution.py:116
  93.0 4.6 %collective-permute-start.17 = (bf16[256,1024]{1,0:T(8,128)(2,1)S(1)}, bf16[256,1024]{1,0:T(8,128)(2,1)S(1)}, u32[]{:S(2)}, u32[]{:S(2)}) collective-permute-start(bf16[256,1024]{1,0:T(8,128)(2,1)S(1)} %get-tuple-element.20), channel_id=1, source_target_pairs={{16,1},{32,17},{48,33},{64,49},{80,65},{96,81},{112,97},{128,113},... | collective-permute-start | bytes 1572872 | tf_op jit(solution)/shard_map/ppermute | solution.py:373
  97.6 5.1 %near_projections.1 = (bf16[512,1024]{1,0:T(8,128)(2,1)S(1)}, bf16[768,1024]{1,0:T(8,128)(2,1)S(1)}, bf16[1024,768]{1,0:T(8,128)(2,1)S(1)}) custom-call(s32[2]{0:T(128)S(1)} %pad_add_fusion.refs_0_.at_ref, bf16[768,1024]{1,0:T(8,128)(2,1)S(1)} %get-tuple-element.16.x_ref, bf16[1024,1024]{1,0:T(8,128)(2,1)S(1)} %copy-done.8, ...), custom_call_target="tpu_custom_call" | custom-call | tf_op jit(solution)/shard_map/near_projections/pallas_call | solution.py:147
  102.7 2.9 %collective-permute-done.17.far_ref = bf16[256,1024]{1,0:T(8,128)(2,1)S(1)} collective-permute-done((bf16[256,1024]{1,0:T(8,128)(2,1)S(1)}, bf16[256,1024]{1,0:T(8,128)(2,1)S(1)}, u32[]{:S(2)}, u32[]{:S(2)}) %collective-permute-start.17) | collective-permute-done | bytes 524320 | tf_op jit(solution)/shard_map/ppermute | solution.py:373
  105.6 12.4 %window_attention.1 = bf16[512,1024]{1,0:T(8,128)(2,1)} custom-call(bf16[512,1024]{1,0:T(8,128)(2,1)S(1)} %get-tuple-element.17.q_ref, bf16[768,1024]{1,0:T(8,128)(2,1)S(1)} %get-tuple-element.18.k_ref, bf16[1024,768]{1,0:T(8,128)(2,1)S(1)} %get-tuple-element.19.v_ref, bf16[256,1024]{1,0:T(8,128)(2,1)S(1)} %collective-permute-done.17.far_ref, ...), custom_call_target="tpu_custom_call" | custom-call | tf_op jit(solution)/shard_map/window_attention/pallas_call | solution.py:242
  (45 shorter events, 0.6 us)
Async XLA Ops:
  0.0 18.8 %copy-start = (bf16[256,64,16]{0,2,1:T(8,128)(2,1)S(1)}, bf16[256,64,16]{0,2,1:T(8,128)(2,1)}, u32[]{:S(2)}) copy-start(bf16[256,64,16]{0,2,1:T(8,128)(2,1)} %param.21) | copy-start | bytes 1572868
  1.1 18.8 %collective-permute-start = (bf16[128,768]{1,0:T(8,128)(2,1)S(1)}, bf16[128,768]{1,0:T(8,128)(2,1)S(1)}, u32[]{:S(2)}, u32[]{:S(2)}) collective-permute-start(bf16[128,768]{1,0:T(8,128)(2,1)S(1)} %get-tuple-element.24.refs_2_), channel_id=1, source_target_pairs={{0,2},{2,4},{4,6},{6,8},{8,10},{10,12},{12,14},{14,0},{1,3},{3,5},... | collective-permute-start | bytes 589832 | tf_op jit(solution)/shard_map/ppermute | solution.py:297
  3.1 20.4 %collective-permute-start.2 = (bf16[128,768]{1,0:T(8,128)(2,1)S(1)}, bf16[128,768]{1,0:T(8,128)(2,1)S(1)}, u32[]{:S(2)}, u32[]{:S(2)}) collective-permute-start(bf16[128,768]{1,0:T(8,128)(2,1)S(1)} %get-tuple-element.24.refs_2_), channel_id=1, source_target_pairs={{2,0},{4,2},{6,4},{8,6},{10,8},{12,10},{14,12},{0,14},{3,1},{5,3},... | collective-permute-start | bytes 589832 | tf_op jit(solution)/shard_map/ppermute | solution.py:297
  7.1 14.9 %collective-permute-start.1 = (bf16[128,768]{1,0:T(8,128)(2,1)S(1)}, bf16[128,768]{1,0:T(8,128)(2,1)S(1)}, u32[]{:S(2)}, u32[]{:S(2)}) collective-permute-start(bf16[128,768]{1,0:T(8,128)(2,1)S(1)} %get-tuple-element.23.refs_3_), channel_id=1, source_target_pairs={{0,2},{2,4},{4,6},{6,8},{8,10},{10,12},{12,14},{14,0},{1,3},{3,5},... | collective-permute-start | bytes 589832 | tf_op jit(solution)/shard_map/ppermute | solution.py:297
  7.1 18.1 %collective-permute-start.3 = (bf16[128,768]{1,0:T(8,128)(2,1)S(1)}, bf16[128,768]{1,0:T(8,128)(2,1)S(1)}, u32[]{:S(2)}, u32[]{:S(2)}) collective-permute-start(bf16[128,768]{1,0:T(8,128)(2,1)S(1)} %get-tuple-element.23.refs_3_), channel_id=1, source_target_pairs={{2,0},{4,2},{6,4},{8,6},{10,8},{12,10},{14,12},{0,14},{3,1},{5,3},... | collective-permute-start | bytes 589832 | tf_op jit(solution)/shard_map/ppermute | solution.py:297
  11.9 13.6 %all-to-all-start = ((s32[8,1,128]{2,1,0:T(1,128)}), s32[8,1,128]{2,1,0:T(1,128)S(1)}, u32[]{:S(2)}, u32[]{:S(2)}) async-start(s32[8,1,128]{2,1,0:T(1,128)} %bitcast.4), calls=%async_computation | async-start | bytes 8192 | tf_op jit(solution)/shard_map/all_to_all | solution.py:310
  18.7 18.0 %collective-permute-start.8 = (s32[8,128]{1,0:T(8,128)S(1)}, s32[8,128]{1,0:T(8,128)S(1)}, u32[]{:S(2)}, u32[]{:S(2)}) collective-permute-start(s32[8,128]{1,0:T(8,128)S(1)} %reshape.56.refs_2_.refs_3_), channel_id=1, source_target_pairs={{0,1},{1,0},{2,3},{3,2},{4,5},{5,4},{6,7},{7,6},{8,9},{9,8},{10,11... | collective-permute-start | bytes 12296 | tf_op jit(solution)/shard_map/ppermute | solution.py:309
  19.9 9.1 %collective-permute-start.4 = (bf16[128,768]{1,0:T(8,128)(2,1)S(1)}, bf16[128,768]{1,0:T(8,128)(2,1)S(1)}, u32[]{:S(2)}, u32[]{:S(2)}) collective-permute-start(bf16[128,768]{1,0:T(8,128)(2,1)S(1)} %collective-permute-done.refs_4_), channel_id=1, source_target_pairs={{0,2},{2,4},{4,6},{6,8},{8,10},{10,12},{12,14},{14,0},{1,3},{3,5},... | collective-permute-start | bytes 589832 | tf_op jit(solution)/shard_map/ppermute | solution.py:297
  22.0 11.0 %collective-permute-start.5 = (bf16[128,768]{1,0:T(8,128)(2,1)S(1)}, bf16[128,768]{1,0:T(8,128)(2,1)S(1)}, u32[]{:S(2)}, u32[]{:S(2)}) collective-permute-start(bf16[128,768]{1,0:T(8,128)(2,1)S(1)} %collective-permute-done.1.refs_5_), channel_id=1, source_target_pairs={{0,2},{2,4},{4,6},{6,8},{8,10},{10,12},{12,14},{14,0},{1,3},{3,5},... | collective-permute-start | bytes 589832 | tf_op jit(solution)/shard_map/ppermute | solution.py:297
  23.5 9.5 %collective-permute-start.6 = (bf16[128,768]{1,0:T(8,128)(2,1)S(1)}, bf16[128,768]{1,0:T(8,128)(2,1)S(1)}, u32[]{:S(2)}, u32[]{:S(2)}) collective-permute-start(bf16[128,768]{1,0:T(8,128)(2,1)S(1)} %collective-permute-done.2.refs_6_), channel_id=1, source_target_pairs={{2,0},{4,2},{6,4},{8,6},{10,8},{12,10},{14,12},{0,14},{3,1},{5,3},... | collective-permute-start | bytes 589832 | tf_op jit(solution)/shard_map/ppermute | solution.py:297
  25.3 9.1 %collective-permute-start.7 = (bf16[128,768]{1,0:T(8,128)(2,1)S(1)}, bf16[128,768]{1,0:T(8,128)(2,1)S(1)}, u32[]{:S(2)}, u32[]{:S(2)}) collective-permute-start(bf16[128,768]{1,0:T(8,128)(2,1)S(1)} %collective-permute-done.3.refs_7_), channel_id=1, source_target_pairs={{2,0},{4,2},{6,4},{8,6},{10,8},{12,10},{14,12},{0,14},{3,1},{5,3},... | collective-permute-start | bytes 589832 | tf_op jit(solution)/shard_map/ppermute | solution.py:297
  29.0 5.4 %copy-start.10 = (bf16[128,768]{1,0:T(8,128)(2,1)}, bf16[128,768]{1,0:T(8,128)(2,1)S(1)}, u32[]{:S(2)}) copy-start(bf16[128,768]{1,0:T(8,128)(2,1)S(1)} %collective-permute-done.4.refs_8_) | copy-start | bytes 589828
  33.0 1.4 %copy-start.9 = (bf16[128,768]{1,0:T(8,128)(2,1)}, bf16[128,768]{1,0:T(8,128)(2,1)S(1)}, u32[]{:S(2)}) copy-start(bf16[128,768]{1,0:T(8,128)(2,1)S(1)} %collective-permute-done.6.refs_10_) | copy-start | bytes 589828
  34.4 2.2 %copy-start.11 = (bf16[128,768]{1,0:T(8,128)(2,1)}, bf16[128,768]{1,0:T(8,128)(2,1)S(1)}, u32[]{:S(2)}) copy-start(bf16[128,768]{1,0:T(8,128)(2,1)S(1)} %collective-permute-done.7.refs_11_) | copy-start | bytes 589828
  35.7 0.9 copy-start.5
  36.6 41.5 %copy-start.1 = (bf16[768,1024]{1,0:T(8,128)(2,1)S(1)}, bf16[768,1024]{1,0:T(8,128)(2,1)}, u32[]{:S(2)}) copy-start(bf16[768,1024]{1,0:T(8,128)(2,1)} %refs_4_.5) | copy-start | bytes 4718596
  36.6 25.7 %all-to-all-start.1 = ((bf16[16,5,8,768]{3,2,1,0:T(8,128)(2,1)}), bf16[16,5,8,768]{3,2,1,0:T(8,128)(2,1)S(1)}, u32[]{:S(2)}, u32[]{:S(2)}) async-start(bf16[16,5,8,768]{3,2,1,0:T(8,128)(2,1)} %copy-done.5), calls=%async_computation.1 | async-start | bytes 1966080 | tf_op jit(solution)/shard_map/all_to_all | solution.py:330
  44.2 9.1 %collective-permute-start.10 = (bf16[128,768]{1,0:T(8,128)(2,1)}, bf16[128,768]{1,0:T(8,128)(2,1)S(1)}, u32[]{:S(2)}, u32[]{:S(2)}) collective-permute-start(bf16[128,768]{1,0:T(8,128)(2,1)} %copy-done.10), channel_id=1, source_target_pairs={{0,2},{2,4},{4,6},{6,8},{8,10},{10,12},{12,14},{14,0},{1,3},{3,5},... | collective-permute-start | bytes 589832 | tf_op jit(solution)/shard_map/ppermute | solution.py:297
  46.6 8.0 %collective-permute-start.13 = (bf16[128,768]{1,0:T(8,128)(2,1)}, bf16[128,768]{1,0:T(8,128)(2,1)S(1)}, u32[]{:S(2)}, u32[]{:S(2)}) collective-permute-start(bf16[128,768]{1,0:T(8,128)(2,1)} %copy-done.11), channel_id=1, source_target_pairs={{2,0},{4,2},{6,4},{8,6},{10,8},{12,10},{14,12},{0,14},{3,1},{5,3},... | collective-permute-start | bytes 589832 | tf_op jit(solution)/shard_map/ppermute | solution.py:297
  47.4 10.1 %collective-permute-start.11 = (bf16[128,768]{1,0:T(8,128)(2,1)S(1)}, bf16[128,768]{1,0:T(8,128)(2,1)S(1)}, u32[]{:S(2)}, u32[]{:S(2)}) collective-permute-start(bf16[128,768]{1,0:T(8,128)(2,1)S(1)} %collective-permute-done.5.refs_9_), channel_id=1, source_target_pairs={{0,2},{2,4},{4,6},{6,8},{8,10},{10,12},{12,14},{14,0},{1,3},{3,5},... | collective-permute-start | bytes 589832 | tf_op jit(solution)/shard_map/ppermute | solution.py:297
  48.6 9.8 %collective-permute-start.12 = (bf16[128,768]{1,0:T(8,128)(2,1)}, bf16[128,768]{1,0:T(8,128)(2,1)S(1)}, u32[]{:S(2)}, u32[]{:S(2)}) collective-permute-start(bf16[128,768]{1,0:T(8,128)(2,1)} %copy-done.9), channel_id=1, source_target_pairs={{2,0},{4,2},{6,4},{8,6},{10,8},{12,10},{14,12},{0,14},{3,1},{5,3},... | collective-permute-start | bytes 589832 | tf_op jit(solution)/shard_map/ppermute | solution.py:297
  53.3 6.9 %collective-permute-start.14 = (bf16[128,768]{1,0:T(8,128)(2,1)S(1)}, bf16[128,768]{1,0:T(8,128)(2,1)S(1)}, u32[]{:S(2)}, u32[]{:S(2)}) collective-permute-start(bf16[128,768]{1,0:T(8,128)(2,1)S(1)} %collective-permute-done.10.refs_2_), channel_id=1, source_target_pairs={{0,2},{2,4},{4,6},{6,8},{8,10},{10,12},{12,14},{14,0},{1,3},{3,5},... | collective-permute-start | bytes 589832 | tf_op jit(solution)/shard_map/ppermute | solution.py:297
  54.6 5.9 %collective-permute-start.15 = (bf16[128,768]{1,0:T(8,128)(2,1)S(1)}, bf16[128,768]{1,0:T(8,128)(2,1)S(1)}, u32[]{:S(2)}, u32[]{:S(2)}) collective-permute-start(bf16[128,768]{1,0:T(8,128)(2,1)S(1)} %collective-permute-done.13.refs_5_), channel_id=1, source_target_pairs={{2,0},{4,2},{6,4},{8,6},{10,8},{12,10},{14,12},{0,14},{3,1},{5,3},... | collective-permute-start | bytes 589832 | tf_op jit(solution)/shard_map/ppermute | solution.py:297
  61.5 0.8 copy-start.6
  62.4 15.8 %all-to-all-start.2 = ((bf16[16,3,8,768]{3,2,1,0:T(8,128)(2,1)}), bf16[16,3,8,768]{3,2,1,0:T(8,128)(2,1)}, u32[]{:S(2)}, u32[]{:S(2)}) async-start(bf16[16,3,8,768]{3,2,1,0:T(8,128)(2,1)} %copy-done.6), calls=%async_computation.2 | async-start | bytes 1179648 | tf_op jit(solution)/shard_map/all_to_all | solution.py:330
  69.6 11.5 %collective-permute-start.9 = (bf16[16,5,8,768]{3,2,1,0:T(8,128)(2,1)S(1)}, bf16[16,5,8,768]{3,2,1,0:T(8,128)(2,1)}, u32[]{:S(2)}, u32[]{:S(2)}) collective-permute-start(bf16[16,5,8,768]{3,2,1,0:T(8,128)(2,1)S(1)} %all-to-all-done.1.refs_1_), channel_id=1, source_target_pairs={{0,1},{1,0},{2,3},{3,2},{4,5},{5,4},{6,7},{7,6},{8,9},{9,8},{10,11... | collective-permute-start | bytes 2949128 | tf_op jit(solution)/shard_map/ppermute | solution.py:331
  78.1 12.2 %collective-permute-start.16 = (bf16[16,3,8,768]{3,2,1,0:T(8,128)(2,1)}, bf16[16,3,8,768]{3,2,1,0:T(8,128)(2,1)S(1)}, u32[]{:S(2)}, u32[]{:S(2)}) collective-permute-start(bf16[16,3,8,768]{3,2,1,0:T(8,128)(2,1)} %all-to-all-done.2.refs_2_), channel_id=1, source_target_pairs={{0,1},{1,0},{2,3},{3,2},{4,5},{5,4},{6,7},{7,6},{8,9},{9,8},{10,11... | collective-permute-start | bytes 1769480 | tf_op jit(solution)/shard_map/ppermute | solution.py:331
  84.7 1.6 %copy-start.2 = (f32[768,1024]{1,0:T(8,128)}, f32[768,1024]{1,0:T(8,128)S(1)}, u32[]{:S(2)}) copy-start(f32[768,1024]{1,0:T(8,128)S(1)} %shard_map.113.refs_1_) | copy-start | bytes 9437188
  86.4 3.9 %copy-start.12 = (f32[1024]{0:T(1024)S(1)}, f32[1024]{0:T(1024)}, u32[]{:S(2)}) copy-start(f32[1024]{0:T(1024)} %param.16) | copy-start | bytes 12292
  86.4 11.2 %copy-start.8 = (bf16[1024,1024]{1,0:T(8,128)(2,1)S(1)}, bf16[1024,1024]{1,0:T(8,128)(2,1)}, u32[]{:S(2)}) copy-start(bf16[1024,1024]{1,0:T(8,128)(2,1)} %wq_ref.1) | copy-start | bytes 6291460
  90.3 7.2 %copy-start.3 = (bf16[1024,1024]{1,0:T(8,128)(2,1)S(1)}, bf16[1024,1024]{1,0:T(8,128)(2,1)}, u32[]{:S(2)}) copy-start(bf16[1024,1024]{1,0:T(8,128)(2,1)} %wk_ref.3) | copy-start | bytes 6291460
  90.3 7.2 %copy-start.4 = (bf16[1024,1024]{1,0:T(8,128)(2,1)S(1)}, bf16[1024,1024]{1,0:T(8,128)(2,1)}, u32[]{:S(2)}) copy-start(bf16[1024,1024]{1,0:T(8,128)(2,1)} %wv_ref.3) | copy-start | bytes 6291460
  93.0 12.6 %collective-permute-start.17 = (bf16[256,1024]{1,0:T(8,128)(2,1)S(1)}, bf16[256,1024]{1,0:T(8,128)(2,1)S(1)}, u32[]{:S(2)}, u32[]{:S(2)}) collective-permute-start(bf16[256,1024]{1,0:T(8,128)(2,1)S(1)} %get-tuple-element.20), channel_id=1, source_target_pairs={{16,1},{32,17},{48,33},{64,49},{80,65},{96,81},{112,97},{128,113},... | collective-permute-start | bytes 1572872 | tf_op jit(solution)/shard_map/ppermute | solution.py:373
  97.6 8.0 %copy-start.7 = (bf16[1024,1024]{1,0:T(8,128)(2,1)S(1)}, bf16[1024,1024]{1,0:T(8,128)(2,1)}, u32[]{:S(2)}) copy-start(bf16[1024,1024]{1,0:T(8,128)(2,1)} %wo_ref.1) | copy-start | bytes 6291460

commit v6 on v5

--- a/solution.py
+++ b/solution.py
@@ -21,25 +21,18 @@
 
 def pick_kernel(offsets, n_x, at_ref, route_ref, *refs):
     blocks, out_ref = refs[:-1], refs[-1]
-    used = 0
-    for i, offset in enumerate(offsets):
-        parts = 2
-        line = (at_ref[0] + (offset + n_x)) % n_x
-        index = route_ref[pl.ds(line, 1), :]
+    lines = [(at_ref[0] + (offset + n_x)) % n_x for offset in offsets]
+    lines += lines[:1] * (8 - len(lines))
+    index = jnp.concatenate([route_ref[pl.ds(line, 1), :] for line in lines], axis=0).T
+    for i in range(len(offsets)):
+        rows = None
         base = 0
-        rows = None
-        for block in blocks[used : used + parts]:
-            ids = lax.broadcasted_iota(jnp.int32, (block.shape[0], index.shape[1]), 0) + base
-            one_hot = jnp.where(ids == index, 1.0, 0.0).astype(jnp.bfloat16)
-            got = lax.dot_general(
-                one_hot,
-                block[...],
-                (((0,), (0,)), ((), ())),
-                preferred_element_type=jnp.float32,
-            )
+        for block in blocks[2 * i : 2 * i + 2]:
+            ids = lax.broadcasted_iota(jnp.int32, (index.shape[0], block.shape[0]), 1) + base
+            one_hot = jnp.where(ids == index[:, i : i + 1], 1.0, 0.0).astype(jnp.bfloat16)
+            got = jnp.dot(one_hot, block[...], preferred_element_type=jnp.float32)
             rows = got if rows is None else rows + got
             base += block.shape[0]
-        used += parts
         out_ref[:, i] = rows.reshape(out_ref.shape[0], out_ref.shape[2], out_ref.shape[3]).astype(
             jnp.bfloat16
         )
@@ -72,12 +65,11 @@
         projected = jnp.dot(
             jnp.concatenate(pieces, axis=0), w_ref[...], preferred_element_type=jnp.float32
         ).astype(jnp.bfloat16)
-        added = jnp.dot(
-            jnp.concatenate(hots, axis=1), projected, preferred_element_type=jnp.float32
-        )
         if ready is not None:
             ready()
-        total[...] += added
+        total[...] += jnp.dot(
+            jnp.concatenate(hots, axis=1), projected, preferred_element_type=jnp.float32
+        )
 
 
 def first_sum_kernel(n_x, at_ref, a_ref, ac_ref, w_ref, out_ref):
@@ -331,7 +323,7 @@
         return got, lax.ppermute(got, "cam", swap)
 
     rows = pick(EARLY, n_x, n_y, at, route, (*own, *u1, *d1, *u2, *d2))
-    rows, bias, cells_other = lax.optimization_barrier((rows, bias, cells_other))
+    rows, bias = lax.optimization_barrier((rows, bias))
     early, early_other = exchange(rows)
     total = jax.ShapeDtypeStruct((ext, width), jnp.float32)
     [lifted] = local_call(

time: 120 us -> 117 us (0.975); the launches traced: 118 us -> 116 us
  Pallas kernels: 32.9 us -> 34.9 us
  waiting for transfers between devices: 26.9 us -> 24.9 us
  local copies, waits for them, and re-layouts: 7.41 us -> 5.79 us
    ppermute x14, waiting for transfers between devices: 15.4 us -> 11.7 us  [shift(): moved.append(lax.ppermute(values[piece], 'bevx', perm))]
  transfers between devices with their start and end apart: 21 -> 21, of which waited for: 10 -> 10; matrix products, arithmetic and copies ran while one was open for 3% -> 2% of each run, Pallas kernels for 15% -> 15%
where the time goes in v6:
time: 117 us; the launch traced here: 116 us
  starting transfers between devices  49.5 us (42%)
  Pallas kernels  34.9 us (30%)
  waiting for transfers between devices  24.9 us (21%)
  local copies, waits for them, and re-layouts  5.79 us (5%)
    ppermute x14, starting transfers between devices, shift(): moved.append(lax.ppermute(values[piece], 'bevx', perm))  24.7 us
    all_to_all x2, starting transfers between devices, exchange(): got = lax.all_to_all(rows, 'bevy', split_axis=0, concat_axis=0, tiled=True)  14.6 us
    pallas_call x4, Pallas kernels, local_call(): pl.pallas_call(kernel, in_specs=[SCALAR] + [pl.BlockSpec(memory_space=plt...  14 us
    pallas_call x1, Pallas kernels, attention(): pl.pallas_call(attention_kernel, grid=(width // block,), in_specs=[LOCAL]...  12.4 us
    ppermute x14, waiting for transfers between devices, shift(): moved.append(lax.ppermute(values[piece], 'bevx', perm))  11.7 us
    all_to_all x2, waiting for transfers between devices, exchange(): got = lax.all_to_all(rows, 'bevy', split_axis=0, concat_axis=0, tiled=True)  8.57 us
    all_to_all x1, starting transfers between devices, steps(): lax.all_to_all(route, 'bevx', split_axis=0, concat_axis=0, tiled=True)  5.76 us
    pallas_call x1, Pallas kernels, project(): pl.pallas_call(project_kernel, in_specs=[SCALAR] + [LOCAL] * 4, out_specs...  5.11 us
  transfers between devices with their start and end apart: 21, of which 10 were waited for; matrix products, arithmetic and copies ran while one was open for 2% of the time, Pallas kernels for 15%

profile of v6, /device:TPU:8, one launch (start us, length us, event | category | flops | bytes accessed | tf_op | source)
XLA Modules:
  0.0 116.3 jit_solution(8473998539768721409)
XLA Ops:
  0.0 1.1 fusion.2
  1.1 2.0 %collective-permute-start = (bf16[128,768]{1,0:T(8,128)(2,1)S(1)}, bf16[128,768]{1,0:T(8,128)(2,1)S(1)}, u32[]{:S(2)}, u32[]{:S(2)}) collective-permute-start(bf16[128,768]{1,0:T(8,128)(2,1)S(1)} %get-tuple-element.22.refs_2_), channel_id=1, source_target_pairs={{0,2},{2,4},{4,6},{6,8},{8,10},{10,12},{12,14},{14,0},{1,3},{3,5},... | collective-permute-start | bytes 589832 | tf_op jit(solution)/shard_map/ppermute | solution.py:289
  3.1 4.0 %collective-permute-start.2 = (bf16[128,768]{1,0:T(8,128)(2,1)S(1)}, bf16[128,768]{1,0:T(8,128)(2,1)S(1)}, u32[]{:S(2)}, u32[]{:S(2)}) collective-permute-start(bf16[128,768]{1,0:T(8,128)(2,1)S(1)} %get-tuple-element.22.refs_2_), channel_id=1, source_target_pairs={{2,0},{4,2},{6,4},{8,6},{10,8},{12,10},{14,12},{0,14},{3,1},{5,3},... | collective-permute-start | bytes 589832 | tf_op jit(solution)/shard_map/ppermute | solution.py:289
  7.1 3.2 %collective-permute-start.3 = (bf16[128,768]{1,0:T(8,128)(2,1)S(1)}, bf16[128,768]{1,0:T(8,128)(2,1)S(1)}, u32[]{:S(2)}, u32[]{:S(2)}) collective-permute-start(bf16[128,768]{1,0:T(8,128)(2,1)S(1)} %get-tuple-element.21.refs_3_), channel_id=1, source_target_pairs={{2,0},{4,2},{6,4},{8,6},{10,8},{12,10},{14,12},{0,14},{3,1},{5,3},... | collective-permute-start | bytes 589832 | tf_op jit(solution)/shard_map/ppermute | solution.py:289
  10.4 0.7 fusion.1
  11.2 0.1 copy.18
  11.3 0.7 all_to_all.13
  11.9 5.8 %all-to-all-start = ((s32[8,1,128]{2,1,0:T(1,128)}), s32[8,1,128]{2,1,0:T(1,128)S(1)}, u32[]{:S(2)}, u32[]{:S(2)}) async-start(s32[8,1,128]{2,1,0:T(1,128)} %bitcast.4), calls=%async_computation | async-start | bytes 8192 | tf_op jit(solution)/shard_map/all_to_all | solution.py:302
  17.7 0.1 constant_dynamic-slice_fusion
  17.9 0.3 copy.25
  18.2 0.1 constant_dynamic-slice_fusion.1
  18.3 0.3 copy.24
  18.6 0.2 copy.22
  18.8 2.1 %collective-permute-start.4 = (bf16[128,768]{1,0:T(8,128)(2,1)S(1)}, bf16[128,768]{1,0:T(8,128)(2,1)S(1)}, u32[]{:S(2)}, u32[]{:S(2)}) collective-permute-start(bf16[128,768]{1,0:T(8,128)(2,1)S(1)} %collective-permute-done.refs_4_), channel_id=1, source_target_pairs={{0,2},{2,4},{4,6},{6,8},{8,10},{10,12},{12,14},{14,0},{1,3},{3,5},... | collective-permute-start | bytes 589832 | tf_op jit(solution)/shard_map/ppermute | solution.py:289
  20.9 1.5 %collective-permute-start.5 = (bf16[128,768]{1,0:T(8,128)(2,1)S(1)}, bf16[128,768]{1,0:T(8,128)(2,1)S(1)}, u32[]{:S(2)}, u32[]{:S(2)}) collective-permute-start(bf16[128,768]{1,0:T(8,128)(2,1)S(1)} %collective-permute-done.1.refs_5_), channel_id=1, source_target_pairs={{0,2},{2,4},{4,6},{6,8},{8,10},{10,12},{12,14},{14,0},{1,3},{3,5},... | collective-permute-start | bytes 589832 | tf_op jit(solution)/shard_map/ppermute | solution.py:289
  22.4 1.8 %collective-permute-start.6 = (bf16[128,768]{1,0:T(8,128)(2,1)S(1)}, bf16[128,768]{1,0:T(8,128)(2,1)S(1)}, u32[]{:S(2)}, u32[]{:S(2)}) collective-permute-start(bf16[128,768]{1,0:T(8,128)(2,1)S(1)} %collective-permute-done.2.refs_6_), channel_id=1, source_target_pairs={{2,0},{4,2},{6,4},{8,6},{10,8},{12,10},{14,12},{0,14},{3,1},{5,3},... | collective-permute-start | bytes 589832 | tf_op jit(solution)/shard_map/ppermute | solution.py:289
  24.2 0.1 collective-permute-start.7
  24.4 1.0 all-to-all-done
  25.4 2.1 %collective-permute-done.4.refs_8_ = bf16[128,768]{1,0:T(8,128)(2,1)S(1)} collective-permute-done((bf16[128,768]{1,0:T(8,128)(2,1)S(1)}, bf16[128,768]{1,0:T(8,128)(2,1)S(1)}, u32[]{:S(2)}, u32[]{:S(2)}) %collective-permute-start.4) | collective-permute-done | bytes 196640 | tf_op jit(solution)/shard_map/ppermute | solution.py:289
  27.5 2.1 %collective-permute-done.5.refs_9_ = bf16[128,768]{1,0:T(8,128)(2,1)S(1)} collective-permute-done((bf16[128,768]{1,0:T(8,128)(2,1)S(1)}, bf16[128,768]{1,0:T(8,128)(2,1)S(1)}, u32[]{:S(2)}, u32[]{:S(2)}) %collective-permute-start.5) | collective-permute-done | bytes 196640 | tf_op jit(solution)/shard_map/ppermute | solution.py:289
  29.6 1.4 %collective-permute-done.7.refs_11_ = bf16[128,768]{1,0:T(8,128)(2,1)S(1)} collective-permute-done((bf16[128,768]{1,0:T(8,128)(2,1)S(1)}, bf16[128,768]{1,0:T(8,128)(2,1)S(1)}, u32[]{:S(2)}, u32[]{:S(2)}) %collective-permute-start.7) | collective-permute-done | bytes 196640 | tf_op jit(solution)/shard_map/ppermute | solution.py:289
  31.0 2.3 %pick_rows.2 = bf16[16,5,8,768]{3,2,1,0:T(8,128)(2,1)} custom-call(s32[2]{0:T(128)S(1)} %pad_add_fusion.refs_0_.at_ref, s32[8,128]{1,0:T(8,128)S(1)} %bitcast.18, bf16[128,768]{1,0:T(8,128)(2,1)S(1)} %get-tuple-element.22.refs_2_, bf16[128,768]{1,0:T(8,128)(2,1)S(1)} %get-tuple-element.21.refs_3_, bf16[128,768]{1,0:T(8,128)(2,1)S(1)} %collective-permute-done.refs_4_, ...), custom_call_target="tpu_custom_call" | custom-call | tf_op jit(solution)/shard_map/pick_rows/pallas_call | solution.py:44
  33.3 7.4 %all-to-all-start.1 = ((bf16[16,5,8,768]{3,2,1,0:T(8,128)(2,1)}), bf16[16,5,8,768]{3,2,1,0:T(8,128)(2,1)S(1)}, u32[]{:S(2)}, u32[]{:S(2)}) async-start(bf16[16,5,8,768]{3,2,1,0:T(8,128)(2,1)} %pick_rows.2), calls=%async_computation.1 | async-start | bytes 1966080 | tf_op jit(solution)/shard_map/all_to_all | solution.py:322
  40.7 2.5 %collective-permute-start.10 = (bf16[128,768]{1,0:T(8,128)(2,1)}, bf16[128,768]{1,0:T(8,128)(2,1)S(1)}, u32[]{:S(2)}, u32[]{:S(2)}) collective-permute-start(bf16[128,768]{1,0:T(8,128)(2,1)} %copy-done.9), channel_id=1, source_target_pairs={{0,2},{2,4},{4,6},{6,8},{8,10},{10,12},{12,14},{14,0},{1,3},{3,5},... | collective-permute-start | bytes 589832 | tf_op jit(solution)/shard_map/ppermute | solution.py:289
  43.2 0.8 collective-permute-start.13
  44.1 1.2 %collective-permute-start.11 = (bf16[128,768]{1,0:T(8,128)(2,1)S(1)}, bf16[128,768]{1,0:T(8,128)(2,1)S(1)}, u32[]{:S(2)}, u32[]{:S(2)}) collective-permute-start(bf16[128,768]{1,0:T(8,128)(2,1)S(1)} %collective-permute-done.5.refs_9_), channel_id=1, source_target_pairs={{0,2},{2,4},{4,6},{6,8},{8,10},{10,12},{12,14},{14,0},{1,3},{3,5},... | collective-permute-start | bytes 589832 | tf_op jit(solution)/shard_map/ppermute | solution.py:289
  45.2 2.1 %collective-permute-start.12 = (bf16[128,768]{1,0:T(8,128)(2,1)}, bf16[128,768]{1,0:T(8,128)(2,1)S(1)}, u32[]{:S(2)}, u32[]{:S(2)}) collective-permute-start(bf16[128,768]{1,0:T(8,128)(2,1)} %copy-done.8), channel_id=1, source_target_pairs={{2,0},{4,2},{6,4},{8,6},{10,8},{12,10},{14,12},{0,14},{3,1},{5,3},... | collective-permute-start | bytes 589832 | tf_op jit(solution)/shard_map/ppermute | solution.py:289
  47.3 1.8 %collective-permute-done.10.refs_2_ = bf16[128,768]{1,0:T(8,128)(2,1)S(1)} collective-permute-done((bf16[128,768]{1,0:T(8,128)(2,1)}, bf16[128,768]{1,0:T(8,128)(2,1)S(1)}, u32[]{:S(2)}, u32[]{:S(2)}) %collective-permute-start.10) | collective-permute-done | bytes 196640 | tf_op jit(solution)/shard_map/ppermute | solution.py:289
  49.0 2.1 %collective-permute-start.14 = (bf16[128,768]{1,0:T(8,128)(2,1)S(1)}, bf16[128,768]{1,0:T(8,128)(2,1)S(1)}, u32[]{:S(2)}, u32[]{:S(2)}) collective-permute-start(bf16[128,768]{1,0:T(8,128)(2,1)S(1)} %collective-permute-done.10.refs_2_), channel_id=1, source_target_pairs={{0,2},{2,4},{4,6},{6,8},{8,10},{10,12},{12,14},{14,0},{1,3},{3,5},... | collective-permute-start | bytes 589832 | tf_op jit(solution)/shard_map/ppermute | solution.py:289
  51.2 1.3 %collective-permute-start.15 = (bf16[128,768]{1,0:T(8,128)(2,1)S(1)}, bf16[128,768]{1,0:T(8,128)(2,1)S(1)}, u32[]{:S(2)}, u32[]{:S(2)}) collective-permute-start(bf16[128,768]{1,0:T(8,128)(2,1)S(1)} %collective-permute-done.13.refs_5_), channel_id=1, source_target_pairs={{2,0},{4,2},{6,4},{8,6},{10,8},{12,10},{14,12},{0,14},{3,1},{5,3},... | collective-permute-start | bytes 589832 | tf_op jit(solution)/shard_map/ppermute | solution.py:289
  52.5 0.8 collective-permute-done.12.refs_4_
  53.3 2.6 %collective-permute-done.14.refs_6_ = bf16[128,768]{1,0:T(8,128)(2,1)S(1)} collective-permute-done((bf16[128,768]{1,0:T(8,128)(2,1)S(1)}, bf16[128,768]{1,0:T(8,128)(2,1)S(1)}, u32[]{:S(2)}, u32[]{:S(2)}) %collective-permute-start.14) | collective-permute-done | bytes 196640 | tf_op jit(solution)/shard_map/ppermute | solution.py:289
  55.9 0.9 collective-permute-done.15.refs_7_
  56.9 1.1 pick_rows.3
  58.0 0.8 copy-done.5
  58.8 7.2 %all-to-all-start.2 = ((bf16[16,3,8,768]{3,2,1,0:T(8,128)(2,1)}), bf16[16,3,8,768]{3,2,1,0:T(8,128)(2,1)}, u32[]{:S(2)}, u32[]{:S(2)}) async-start(bf16[16,3,8,768]{3,2,1,0:T(8,128)(2,1)} %copy-done.5), calls=%async_computation.2 | async-start | bytes 1179648 | tf_op jit(solution)/shard_map/all_to_all | solution.py:322
  66.1 8.6 %all-to-all-done.2.refs_2_ = bf16[16,3,8,768]{3,2,1,0:T(8,128)(2,1)} async-done(((bf16[16,3,8,768]{3,2,1,0:T(8,128)(2,1)}), bf16[16,3,8,768]{3,2,1,0:T(8,128)(2,1)}, u32[]{:S(2)}, u32[]{:S(2)}) %all-to-all-start.2) | async-done | bytes 589856 | tf_op jit(solution)/shard_map/all_to_all | solution.py:322
  74.7 0.1 copy.23
  74.9 0.6 collective-permute-start.9
  75.5 2.9 %shard_map.112.refs_1_ = f32[768,1024]{1,0:T(8,128)S(1)} custom-call(s32[2]{0:T(128)S(1)} %pad_add_fusion.refs_0_.at_ref, bf16[16,5,8,768]{3,2,1,0:T(8,128)(2,1)S(1)} %all-to-all-done.1.refs_1_, s32[8,128]{1,0:T(8,128)S(1)} %reshape.56.refs_2_.refs_3_, bf16[768,1024]{1,0:T(8,128)(2,1)S(1)} %copy-done.1), custom_call_target="tpu_custom_call" | custom-call | tf_op jit(solution)/shard_map/pallas_call | solution.py:108
  78.5 3.6 %shard_map.113.refs_1_ = f32[768,1024]{1,0:T(8,128)S(1)} custom-call(s32[2]{0:T(128)S(1)} %pad_add_fusion.refs_0_.at_ref, f32[768,1024]{1,0:T(8,128)S(1)} %shard_map.112.refs_1_, bf16[16,5,8,768]{3,2,1,0:T(8,128)(2,1)} %collective-permute-done.8.refs_2_, s32[8,128]{1,0:T(8,128)S(1)} %collective-permute-done.9.refs_3_, bf16[768,1024]{1,0:T(8,128)(2,1)S(1)} %copy-done.1), custom_call_target="tpu_custom_call" | custom-call | tf_op jit(solution)/shard_map/pallas_call | solution.py:108
  82.1 1.6 %copy-done.2 = f32[768,1024]{1,0:T(8,128)} copy-done((f32[768,1024]{1,0:T(8,128)}, f32[768,1024]{1,0:T(8,128)S(1)}, u32[]{:S(2)}) %copy-start.2) | copy-done | bytes 3145752
  83.8 4.1 %shard_map.114.refs_1_ = f32[768,1024]{1,0:T(8,128)S(1)} custom-call(s32[2]{0:T(128)S(1)} %pad_add_fusion.refs_0_.at_ref, f32[768,1024]{1,0:T(8,128)} %copy-done.2, bf16[16,3,8,768]{3,2,1,0:T(8,128)(2,1)} %all-to-all-done.2.refs_2_, s32[8,128]{1,0:T(8,128)S(1)} %reshape.56.refs_2_.refs_3_, bf16[768,1024]{1,0:T(8,128)(2,1)S(1)} %copy-done.1), custom_call_target="tpu_custom_call" | custom-call | tf_op jit(solution)/shard_map/pallas_call | solution.py:108
  87.9 3.3 %shard_map.115 = (f32[512,1024]{1,0:T(8,128)S(1)}, bf16[768,1024]{1,0:T(8,128)(2,1)S(1)}, bf16[256,1024]{1,0:T(8,128)(2,1)S(1)}) custom-call(s32[2]{0:T(128)S(1)} %pad_add_fusion.refs_0_.at_ref, f32[768,1024]{1,0:T(8,128)S(1)} %shard_map.114.refs_1_, bf16[16,3,8,768]{3,2,1,0:T(8,128)(2,1)} %collective-permute-done.16.refs_2_, ...), custom_call_target="tpu_custom_call" | custom-call | tf_op jit(solution)/shard_map/pallas_call | solution.py:108
  91.2 3.8 %collective-permute-start.17 = (bf16[256,1024]{1,0:T(8,128)(2,1)S(1)}, bf16[256,1024]{1,0:T(8,128)(2,1)S(1)}, u32[]{:S(2)}, u32[]{:S(2)}) collective-permute-start(bf16[256,1024]{1,0:T(8,128)(2,1)S(1)} %get-tuple-element.18), channel_id=1, source_target_pairs={{16,1},{32,17},{48,33},{64,49},{80,65},{96,81},{112,97},{128,113},... | collective-permute-start | bytes 1572872 | tf_op jit(solution)/shard_map/ppermute | solution.py:365
  95.1 5.1 %near_projections.1 = (bf16[512,1024]{1,0:T(8,128)(2,1)S(1)}, bf16[768,1024]{1,0:T(8,128)(2,1)S(1)}, bf16[1024,768]{1,0:T(8,128)(2,1)S(1)}) custom-call(s32[2]{0:T(128)S(1)} %pad_add_fusion.refs_0_.at_ref, bf16[768,1024]{1,0:T(8,128)(2,1)S(1)} %get-tuple-element.14.x_ref, bf16[1024,1024]{1,0:T(8,128)(2,1)S(1)} %copy-done.7, ...), custom_call_target="tpu_custom_call" | custom-call | tf_op jit(solution)/shard_map/near_projections/pallas_call | solution.py:139
  100.2 3.6 %collective-permute-done.17.far_ref = bf16[256,1024]{1,0:T(8,128)(2,1)S(1)} collective-permute-done((bf16[256,1024]{1,0:T(8,128)(2,1)S(1)}, bf16[256,1024]{1,0:T(8,128)(2,1)S(1)}, u32[]{:S(2)}, u32[]{:S(2)}) %collective-permute-start.17) | collective-permute-done | bytes 524320 | tf_op jit(solution)/shard_map/ppermute | solution.py:365
  103.8 12.4 %window_attention.1 = bf16[512,1024]{1,0:T(8,128)(2,1)} custom-call(bf16[512,1024]{1,0:T(8,128)(2,1)S(1)} %get-tuple-element.15.q_ref, bf16[768,1024]{1,0:T(8,128)(2,1)S(1)} %get-tuple-element.16.k_ref, bf16[1024,768]{1,0:T(8,128)(2,1)S(1)} %get-tuple-element.17.v_ref, bf16[256,1024]{1,0:T(8,128)(2,1)S(1)} %collective-permute-done.17.far_ref, ...), custom_call_target="tpu_custom_call" | custom-call | tf_op jit(solution)/shard_map/window_attention/pallas_call | solution.py:234
  (45 shorter events, 0.5 us)
Async XLA Ops:
  0.0 17.7 %copy-start = (bf16[256,64,16]{0,2,1:T(8,128)(2,1)S(1)}, bf16[256,64,16]{0,2,1:T(8,128)(2,1)}, u32[]{:S(2)}) copy-start(bf16[256,64,16]{0,2,1:T(8,128)(2,1)} %param.21) | copy-start | bytes 1572868
  1.1 17.7 %collective-permute-start = (bf16[128,768]{1,0:T(8,128)(2,1)S(1)}, bf16[128,768]{1,0:T(8,128)(2,1)S(1)}, u32[]{:S(2)}, u32[]{:S(2)}) collective-permute-start(bf16[128,768]{1,0:T(8,128)(2,1)S(1)} %get-tuple-element.22.refs_2_), channel_id=1, source_target_pairs={{0,2},{2,4},{4,6},{6,8},{8,10},{10,12},{12,14},{14,0},{1,3},{3,5},... | collective-permute-start | bytes 589832 | tf_op jit(solution)/shard_map/ppermute | solution.py:289
  3.1 19.3 %collective-permute-start.2 = (bf16[128,768]{1,0:T(8,128)(2,1)S(1)}, bf16[128,768]{1,0:T(8,128)(2,1)S(1)}, u32[]{:S(2)}, u32[]{:S(2)}) collective-permute-start(bf16[128,768]{1,0:T(8,128)(2,1)S(1)} %get-tuple-element.22.refs_2_), channel_id=1, source_target_pairs={{2,0},{4,2},{6,4},{8,6},{10,8},{12,10},{14,12},{0,14},{3,1},{5,3},... | collective-permute-start | bytes 589832 | tf_op jit(solution)/shard_map/ppermute | solution.py:289
  7.1 13.8 %collective-permute-start.1 = (bf16[128,768]{1,0:T(8,128)(2,1)S(1)}, bf16[128,768]{1,0:T(8,128)(2,1)S(1)}, u32[]{:S(2)}, u32[]{:S(2)}) collective-permute-start(bf16[128,768]{1,0:T(8,128)(2,1)S(1)} %get-tuple-element.21.refs_3_), channel_id=1, source_target_pairs={{0,2},{2,4},{4,6},{6,8},{8,10},{10,12},{12,14},{14,0},{1,3},{3,5},... | collective-permute-start | bytes 589832 | tf_op jit(solution)/shard_map/ppermute | solution.py:289
  7.1 17.0 %collective-permute-start.3 = (bf16[128,768]{1,0:T(8,128)(2,1)S(1)}, bf16[128,768]{1,0:T(8,128)(2,1)S(1)}, u32[]{:S(2)}, u32[]{:S(2)}) collective-permute-start(bf16[128,768]{1,0:T(8,128)(2,1)S(1)} %get-tuple-element.21.refs_3_), channel_id=1, source_target_pairs={{2,0},{4,2},{6,4},{8,6},{10,8},{12,10},{14,12},{0,14},{3,1},{5,3},... | collective-permute-start | bytes 589832 | tf_op jit(solution)/shard_map/ppermute | solution.py:289
  11.9 13.5 %all-to-all-start = ((s32[8,1,128]{2,1,0:T(1,128)}), s32[8,1,128]{2,1,0:T(1,128)S(1)}, u32[]{:S(2)}, u32[]{:S(2)}) async-start(s32[8,1,128]{2,1,0:T(1,128)} %bitcast.4), calls=%async_computation | async-start | bytes 8192 | tf_op jit(solution)/shard_map/all_to_all | solution.py:302
  18.8 8.7 %collective-permute-start.4 = (bf16[128,768]{1,0:T(8,128)(2,1)S(1)}, bf16[128,768]{1,0:T(8,128)(2,1)S(1)}, u32[]{:S(2)}, u32[]{:S(2)}) collective-permute-start(bf16[128,768]{1,0:T(8,128)(2,1)S(1)} %collective-permute-done.refs_4_), channel_id=1, source_target_pairs={{0,2},{2,4},{4,6},{6,8},{8,10},{10,12},{12,14},{14,0},{1,3},{3,5},... | collective-permute-start | bytes 589832 | tf_op jit(solution)/shard_map/ppermute | solution.py:289
  20.9 8.7 %collective-permute-start.5 = (bf16[128,768]{1,0:T(8,128)(2,1)S(1)}, bf16[128,768]{1,0:T(8,128)(2,1)S(1)}, u32[]{:S(2)}, u32[]{:S(2)}) collective-permute-start(bf16[128,768]{1,0:T(8,128)(2,1)S(1)} %collective-permute-done.1.refs_5_), channel_id=1, source_target_pairs={{0,2},{2,4},{4,6},{6,8},{8,10},{10,12},{12,14},{14,0},{1,3},{3,5},... | collective-permute-start | bytes 589832 | tf_op jit(solution)/shard_map/ppermute | solution.py:289
  22.4 7.2 %collective-permute-start.6 = (bf16[128,768]{1,0:T(8,128)(2,1)S(1)}, bf16[128,768]{1,0:T(8,128)(2,1)S(1)}, u32[]{:S(2)}, u32[]{:S(2)}) collective-permute-start(bf16[128,768]{1,0:T(8,128)(2,1)S(1)} %collective-permute-done.2.refs_6_), channel_id=1, source_target_pairs={{2,0},{4,2},{6,4},{8,6},{10,8},{12,10},{14,12},{0,14},{3,1},{5,3},... | collective-permute-start | bytes 589832 | tf_op jit(solution)/shard_map/ppermute | solution.py:289
  24.2 6.8 %collective-permute-start.7 = (bf16[128,768]{1,0:T(8,128)(2,1)S(1)}, bf16[128,768]{1,0:T(8,128)(2,1)S(1)}, u32[]{:S(2)}, u32[]{:S(2)}) collective-permute-start(bf16[128,768]{1,0:T(8,128)(2,1)S(1)} %collective-permute-done.3.refs_7_), channel_id=1, source_target_pairs={{2,0},{4,2},{6,4},{8,6},{10,8},{12,10},{14,12},{0,14},{3,1},{5,3},... | collective-permute-start | bytes 589832 | tf_op jit(solution)/shard_map/ppermute | solution.py:289
  27.5 5.8 %copy-start.9 = (bf16[128,768]{1,0:T(8,128)(2,1)}, bf16[128,768]{1,0:T(8,128)(2,1)S(1)}, u32[]{:S(2)}) copy-start(bf16[128,768]{1,0:T(8,128)(2,1)S(1)} %collective-permute-done.4.refs_8_) | copy-start | bytes 589828
  29.6 3.7 %copy-start.8 = (bf16[128,768]{1,0:T(8,128)(2,1)}, bf16[128,768]{1,0:T(8,128)(2,1)S(1)}, u32[]{:S(2)}) copy-start(bf16[128,768]{1,0:T(8,128)(2,1)S(1)} %collective-permute-done.6.refs_10_) | copy-start | bytes 589828
  31.0 2.3 %copy-start.10 = (bf16[128,768]{1,0:T(8,128)(2,1)}, bf16[128,768]{1,0:T(8,128)(2,1)S(1)}, u32[]{:S(2)}) copy-start(bf16[128,768]{1,0:T(8,128)(2,1)S(1)} %collective-permute-done.7.refs_11_) | copy-start | bytes 589828
  33.3 41.3 %copy-start.12 = (s32[128,1,1,8]{0,3,2,1:T(8,128)S(1)}, s32[128,1,1,8]{0,3,2,1:T(8,128)}, u32[]{:S(2)}) copy-start(s32[128,1,1,8]{0,3,2,1:T(8,128)} %param.14) | copy-start | bytes 12292
  33.3 25.5 %all-to-all-start.1 = ((bf16[16,5,8,768]{3,2,1,0:T(8,128)(2,1)}), bf16[16,5,8,768]{3,2,1,0:T(8,128)(2,1)S(1)}, u32[]{:S(2)}, u32[]{:S(2)}) async-start(bf16[16,5,8,768]{3,2,1,0:T(8,128)(2,1)} %pick_rows.2), calls=%async_computation.1 | async-start | bytes 1966080 | tf_op jit(solution)/shard_map/all_to_all | solution.py:322
  40.7 34.8 %copy-start.1 = (bf16[768,1024]{1,0:T(8,128)(2,1)S(1)}, bf16[768,1024]{1,0:T(8,128)(2,1)}, u32[]{:S(2)}) copy-start(bf16[768,1024]{1,0:T(8,128)(2,1)} %refs_4_.5) | copy-start | bytes 4718596
  40.7 8.3 %collective-permute-start.10 = (bf16[128,768]{1,0:T(8,128)(2,1)}, bf16[128,768]{1,0:T(8,128)(2,1)S(1)}, u32[]{:S(2)}, u32[]{:S(2)}) collective-permute-start(bf16[128,768]{1,0:T(8,128)(2,1)} %copy-done.9), channel_id=1, source_target_pairs={{0,2},{2,4},{4,6},{6,8},{8,10},{10,12},{12,14},{14,0},{1,3},{3,5},... | collective-permute-start | bytes 589832 | tf_op jit(solution)/shard_map/ppermute | solution.py:289
  43.2 8.0 %collective-permute-start.13 = (bf16[128,768]{1,0:T(8,128)(2,1)}, bf16[128,768]{1,0:T(8,128)(2,1)S(1)}, u32[]{:S(2)}, u32[]{:S(2)}) collective-permute-start(bf16[128,768]{1,0:T(8,128)(2,1)} %copy-done.10), channel_id=1, source_target_pairs={{2,0},{4,2},{6,4},{8,6},{10,8},{12,10},{14,12},{0,14},{3,1},{5,3},... | collective-permute-start | bytes 589832 | tf_op jit(solution)/shard_map/ppermute | solution.py:289
  44.1 8.4 %collective-permute-start.11 = (bf16[128,768]{1,0:T(8,128)(2,1)S(1)}, bf16[128,768]{1,0:T(8,128)(2,1)S(1)}, u32[]{:S(2)}, u32[]{:S(2)}) collective-permute-start(bf16[128,768]{1,0:T(8,128)(2,1)S(1)} %collective-permute-done.5.refs_9_), channel_id=1, source_target_pairs={{0,2},{2,4},{4,6},{6,8},{8,10},{10,12},{12,14},{14,0},{1,3},{3,5},... | collective-permute-start | bytes 589832 | tf_op jit(solution)/shard_map/ppermute | solution.py:289
  45.2 8.1 %collective-permute-start.12 = (bf16[128,768]{1,0:T(8,128)(2,1)}, bf16[128,768]{1,0:T(8,128)(2,1)S(1)}, u32[]{:S(2)}, u32[]{:S(2)}) collective-permute-start(bf16[128,768]{1,0:T(8,128)(2,1)} %copy-done.8), channel_id=1, source_target_pairs={{2,0},{4,2},{6,4},{8,6},{10,8},{12,10},{14,12},{0,14},{3,1},{5,3},... | collective-permute-start | bytes 589832 | tf_op jit(solution)/shard_map/ppermute | solution.py:289
  49.0 6.9 %collective-permute-start.14 = (bf16[128,768]{1,0:T(8,128)(2,1)S(1)}, bf16[128,768]{1,0:T(8,128)(2,1)S(1)}, u32[]{:S(2)}, u32[]{:S(2)}) collective-permute-start(bf16[128,768]{1,0:T(8,128)(2,1)S(1)} %collective-permute-done.10.refs_2_), channel_id=1, source_target_pairs={{0,2},{2,4},{4,6},{6,8},{8,10},{10,12},{12,14},{14,0},{1,3},{3,5},... | collective-permute-start | bytes 589832 | tf_op jit(solution)/shard_map/ppermute | solution.py:289
  51.2 5.7 %collective-permute-start.15 = (bf16[128,768]{1,0:T(8,128)(2,1)S(1)}, bf16[128,768]{1,0:T(8,128)(2,1)S(1)}, u32[]{:S(2)}, u32[]{:S(2)}) collective-permute-start(bf16[128,768]{1,0:T(8,128)(2,1)S(1)} %collective-permute-done.13.refs_5_), channel_id=1, source_target_pairs={{2,0},{4,2},{6,4},{8,6},{10,8},{12,10},{14,12},{0,14},{3,1},{5,3},... | collective-permute-start | bytes 589832 | tf_op jit(solution)/shard_map/ppermute | solution.py:289
  58.0 0.8 copy-start.5
  58.8 15.8 %all-to-all-start.2 = ((bf16[16,3,8,768]{3,2,1,0:T(8,128)(2,1)}), bf16[16,3,8,768]{3,2,1,0:T(8,128)(2,1)}, u32[]{:S(2)}, u32[]{:S(2)}) async-start(bf16[16,3,8,768]{3,2,1,0:T(8,128)(2,1)} %copy-done.5), calls=%async_computation.2 | async-start | bytes 1179648 | tf_op jit(solution)/shard_map/all_to_all | solution.py:322
  66.1 12.4 %collective-permute-start.8 = (bf16[16,5,8,768]{3,2,1,0:T(8,128)(2,1)S(1)}, bf16[16,5,8,768]{3,2,1,0:T(8,128)(2,1)}, u32[]{:S(2)}, u32[]{:S(2)}) collective-permute-start(bf16[16,5,8,768]{3,2,1,0:T(8,128)(2,1)S(1)} %all-to-all-done.1.refs_1_), channel_id=1, source_target_pairs={{0,1},{1,0},{2,3},{3,2},{4,5},{5,4},{6,7},{7,6},{8,9},{9,8},{10,11... | collective-permute-start | bytes 2949128 | tf_op jit(solution)/shard_map/ppermute | solution.py:323
  74.6 13.2 %collective-permute-start.16 = (bf16[16,3,8,768]{3,2,1,0:T(8,128)(2,1)}, bf16[16,3,8,768]{3,2,1,0:T(8,128)(2,1)}, u32[]{:S(2)}, u32[]{:S(2)}) collective-permute-start(bf16[16,3,8,768]{3,2,1,0:T(8,128)(2,1)} %all-to-all-done.2.refs_2_), channel_id=1, source_target_pairs={{0,1},{1,0},{2,3},{3,2},{4,5},{5,4},{6,7},{7,6},{8,9},{9,8},{10,11... | collective-permute-start | bytes 1769480 | tf_op jit(solution)/shard_map/ppermute | solution.py:323
  74.9 3.5 %collective-permute-start.9 = (s32[8,128]{1,0:T(8,128)S(1)}, s32[8,128]{1,0:T(8,128)S(1)}, u32[]{:S(2)}, u32[]{:S(2)}) collective-permute-start(s32[8,128]{1,0:T(8,128)S(1)} %reshape.56.refs_2_.refs_3_), channel_id=1, source_target_pairs={{0,1},{1,0},{2,3},{3,2},{4,5},{5,4},{6,7},{7,6},{8,9},{9,8},{10,11... | collective-permute-start | bytes 12296 | tf_op jit(solution)/shard_map/ppermute | solution.py:301
  82.1 1.6 %copy-start.2 = (f32[768,1024]{1,0:T(8,128)}, f32[768,1024]{1,0:T(8,128)S(1)}, u32[]{:S(2)}) copy-start(f32[768,1024]{1,0:T(8,128)S(1)} %shard_map.113.refs_1_) | copy-start | bytes 9437188
  83.8 4.1 %copy-start.11 = (f32[1024]{0:T(1024)S(1)}, f32[1024]{0:T(1024)}, u32[]{:S(2)}) copy-start(f32[1024]{0:T(1024)} %param.16) | copy-start | bytes 12292
  83.8 11.3 %copy-start.7 = (bf16[1024,1024]{1,0:T(8,128)(2,1)S(1)}, bf16[1024,1024]{1,0:T(8,128)(2,1)}, u32[]{:S(2)}) copy-start(bf16[1024,1024]{1,0:T(8,128)(2,1)} %wq_ref.1) | copy-start | bytes 6291460
  87.9 7.2 %copy-start.3 = (bf16[1024,1024]{1,0:T(8,128)(2,1)S(1)}, bf16[1024,1024]{1,0:T(8,128)(2,1)}, u32[]{:S(2)}) copy-start(bf16[1024,1024]{1,0:T(8,128)(2,1)} %wk_ref.3) | copy-start | bytes 6291460
  87.9 7.2 %copy-start.4 = (bf16[1024,1024]{1,0:T(8,128)(2,1)S(1)}, bf16[1024,1024]{1,0:T(8,128)(2,1)}, u32[]{:S(2)}) copy-start(bf16[1024,1024]{1,0:T(8,128)(2,1)} %wv_ref.3) | copy-start | bytes 6291460
  91.2 12.6 %collective-permute-start.17 = (bf16[256,1024]{1,0:T(8,128)(2,1)S(1)}, bf16[256,1024]{1,0:T(8,128)(2,1)S(1)}, u32[]{:S(2)}, u32[]{:S(2)}) collective-permute-start(bf16[256,1024]{1,0:T(8,128)(2,1)S(1)} %get-tuple-element.18), channel_id=1, source_target_pairs={{16,1},{32,17},{48,33},{64,49},{80,65},{96,81},{112,97},{128,113},... | collective-permute-start | bytes 1572872 | tf_op jit(solution)/shard_map/ppermute | solution.py:365
  95.1 8.8 %copy-start.6 = (bf16[1024,1024]{1,0:T(8,128)(2,1)S(1)}, bf16[1024,1024]{1,0:T(8,128)(2,1)}, u32[]{:S(2)}) copy-start(bf16[1024,1024]{1,0:T(8,128)(2,1)} %wo_ref.1) | copy-start | bytes 6291460

commit v7 on v3

--- a/solution.py
+++ b/solution.py
@@ -58,6 +58,31 @@
     )(at, route, *blocks)
 
 
+def cut_kernel(half, a_ref, b_ref, low_ref, high_ref, sems):
+    copies = (
+        pltpu.make_async_copy(a_ref.at[pl.ds(0, half)], low_ref, sems.at[0]),
+        pltpu.make_async_copy(b_ref.at[pl.ds(half, half)], high_ref, sems.at[1]),
+    )
+    for copy in copies:
+        copy.start()
+    for copy in copies:
+        copy.wait()
+
+
+def cut(a, b):
+    half = a.shape[0] // 2
+    piece = jax.ShapeDtypeStruct((half, a.shape[1]), a.dtype)
+    return pl.pallas_call(
+        lambda *refs: cut_kernel(half, *refs),
+        in_specs=[pl.BlockSpec(memory_space=pl.ANY)] * 2,
+        out_specs=[LOCAL] * 2,
+        out_shape=[piece, piece],
+        scratch_shapes=[pltpu.SemaphoreType.DMA((2,))],
+        compiler_params=pltpu.CompilerParams(vmem_limit_bytes=2 << 20),
+        name="cut_halves",
+    )(a, b)
+
+
 def summed(offsets, n_x, at_ref, pairs, w_ref, total, ready=None):
     for rows_ref, cell_ref in pairs:
         pieces = []
@@ -273,7 +298,6 @@
     n_y = lax.axis_size("bevy")
     n_x = lax.axis_size("bevx")
     slot_count = route_token.shape[3]
-    tokens = image_tokens.shape[0]
     width = lift_weight.shape[1]
     head_count = key_bias.shape[2]
     grid_rows = key_bias.shape[0]
@@ -310,9 +334,9 @@
     d2 = shift(d1, down)
     u3 = shift(u2, up)
     d3 = shift(d2, down)
-    half = tokens // 2
-    u4 = shift(u3[:half], up)
-    d4 = shift(d3[half:], down)
+    low, high = cut(u3, d3)
+    u4 = shift(low, up)
+    d4 = shift(high, down)
 
     near_row = (row * 2 + core) * ROWS_DEV - core * HALO
     far_row = (row * 2 + core) * ROWS_DEV + jnp.where(core == 0, -HALO, ROWS_DEV)

time: 118 us -> 120 us (1.017)
  waiting for transfers between devices: 33 us -> 34.8 us
    ppermute x8, waiting for transfers between devices: 18.2 us -> 20.1 us  [shift(): return lax.ppermute(value, 'bevx', perm)]
  transfers between devices with their start and end apart: 15 -> 15, of which waited for: 8 -> 9; matrix products, arithmetic and copies ran while one was open for 5% -> 5% of each run, Pallas kernels for 16% -> 16%
where the time goes in v7:
time: 120 us; the launch traced here: 118 us
  starting transfers between devices  40.6 us (34%)
  waiting for transfers between devices  34.8 us (29%)
  Pallas kernels  34 us (28%)
  local copies, waits for them, and re-layouts  6.67 us (6%)
  other arithmetic  1.51 us (1%)
    ppermute x8, waiting for transfers between devices, shift(): return lax.ppermute(value, 'bevx', perm)  20.1 us
    ppermute x8, starting transfers between devices, shift(): return lax.ppermute(value, 'bevx', perm)  15.9 us
    all_to_all x2, starting transfers between devices, exchange(): got = lax.all_to_all(rows, 'bevy', split_axis=0, concat_axis=0, tiled=True)  14.6 us
    pallas_call x4, Pallas kernels, local_call(): pl.pallas_call(kernel, in_specs=[SCALAR] + [pl.BlockSpec(memory_space=plt...  13.1 us
    pallas_call x1, Pallas kernels, attention(): pl.pallas_call(attention_kernel, grid=(width // block,), in_specs=[LOCAL]...  12.4 us
    all_to_all x2, waiting for transfers between devices, exchange(): got = lax.all_to_all(rows, 'bevy', split_axis=0, concat_axis=0, tiled=True)  8.57 us
    all_to_all x1, starting transfers between devices, steps(): lax.all_to_all(route, 'bevx', split_axis=0, concat_axis=0, tiled=True)  5.77 us
    pallas_call x1, Pallas kernels, project(): pl.pallas_call(project_kernel, in_specs=[SCALAR] + [LOCAL] * 4, out_specs...  5.11 us
  transfers between devices with their start and end apart: 15, of which 9 were waited for; matrix products, arithmetic and copies ran while one was open for 5% of the time, Pallas kernels for 16%

profile of v7, /device:TPU:8, one launch (start us, length us, event | category | flops | bytes accessed | tf_op | source)
XLA Modules:
  0.0 118.0 jit_solution(6246435879221808338)
XLA Ops:
  0.0 1.9 %collective-permute-start = (bf16[256,768]{1,0:T(8,128)(2,1)}, bf16[256,768]{1,0:T(8,128)(2,1)S(1)}, u32[]{:S(2)}, u32[]{:S(2)}) collective-permute-start(bf16[256,768]{1,0:T(8,128)(2,1)} %refs_2_.1), channel_id=1, source_target_pairs={{0,2},{2,4},{4,6},{6,8},{8,10},{10,12},{12,14},{14,0},{1,3},{3,5},... | collective-permute-start | bytes 1179656 | tf_op jit(solution)/shard_map/ppermute | solution.py:316
  1.9 4.0 %collective-permute-start.1 = (bf16[256,768]{1,0:T(8,128)(2,1)}, bf16[256,768]{1,0:T(8,128)(2,1)S(1)}, u32[]{:S(2)}, u32[]{:S(2)}) collective-permute-start(bf16[256,768]{1,0:T(8,128)(2,1)} %refs_2_.1), channel_id=1, source_target_pairs={{2,0},{4,2},{6,4},{8,6},{10,8},{12,10},{14,12},{0,14},{3,1},{5,3},... | collective-permute-start | bytes 1179656 | tf_op jit(solution)/shard_map/ppermute | solution.py:316
  5.9 0.8 squeeze.3
  6.7 0.5 broadcast.14
  7.2 1.3 %reduce.3 = s32[128]{0:T(128)S(1)} reduce(s32[1,1,128]{2,1,0:T(1,128)} %param.15, s32[]{:T(128)} %broadcast.14), dimensions={0,1}, to_apply=%param.15.reduce_sub_computation.3 | reduce | bytes 1028 | tf_op args[4]
  8.6 0.1 lt.18
  8.7 0.1 copy.19
  8.8 0.7 reshape.26
  9.4 0.8 reshape_squeeze.3
  10.2 0.1 copy.20
  10.3 0.1 reshape.27.refs_2_.refs_3_
  10.4 5.8 %all-to-all-start = ((s32[8,1,128]{2,1,0:T(1,128)}), s32[8,1,128]{2,1,0:T(1,128)S(1)}, u32[]{:S(2)}, u32[]{:S(2)}) async-start(s32[8,1,128]{2,1,0:T(1,128)} %bitcast.5), calls=%async_computation | async-start | bytes 8192 | tf_op jit(solution)/shard_map/all_to_all | solution.py:331
  16.2 0.1 constant_dynamic-slice_fusion
  16.4 0.3 copy.26
  16.7 2.1 %collective-permute-start.2 = (bf16[256,768]{1,0:T(8,128)(2,1)S(1)}, bf16[256,768]{1,0:T(8,128)(2,1)S(1)}, u32[]{:S(2)}, u32[]{:S(2)}) collective-permute-start(bf16[256,768]{1,0:T(8,128)(2,1)S(1)} %collective-permute-done.refs_3_), channel_id=1, source_target_pairs={{0,2},{2,4},{4,6},{6,8},{8,10},{10,12},{12,14},{14,0},{1,3},{3,5},... | collective-permute-start | bytes 1179656 | tf_op jit(solution)/shard_map/ppermute | solution.py:316
  18.8 1.3 %collective-permute-start.3 = (bf16[256,768]{1,0:T(8,128)(2,1)S(1)}, bf16[256,768]{1,0:T(8,128)(2,1)S(1)}, u32[]{:S(2)}, u32[]{:S(2)}) collective-permute-start(bf16[256,768]{1,0:T(8,128)(2,1)S(1)} %collective-permute-done.1.refs_4_), channel_id=1, source_target_pairs={{2,0},{4,2},{6,4},{8,6},{10,8},{12,10},{14,12},{0,14},{3,1},{5,3},... | collective-permute-start | bytes 1179656 | tf_op jit(solution)/shard_map/ppermute | solution.py:316
  20.1 0.1 constant_dynamic-slice_fusion.1
  20.2 0.3 copy.25
  20.5 0.2 copy.24
  20.7 0.1 fusion.bias_ref
  20.8 0.1 pad_add_fusion.refs_0_.at_ref
  20.9 3.0 %all-to-all-done = s32[8,1,128]{2,1,0:T(1,128)S(1)} async-done(((s32[8,1,128]{2,1,0:T(1,128)}), s32[8,1,128]{2,1,0:T(1,128)S(1)}, u32[]{:S(2)}, u32[]{:S(2)}) %all-to-all-start) | async-done | bytes 4128 | tf_op jit(solution)/shard_map/all_to_all | solution.py:331
  23.9 5.9 %collective-permute-done.2.refs_5_ = bf16[256,768]{1,0:T(8,128)(2,1)S(1)} collective-permute-done((bf16[256,768]{1,0:T(8,128)(2,1)S(1)}, bf16[256,768]{1,0:T(8,128)(2,1)S(1)}, u32[]{:S(2)}, u32[]{:S(2)}) %collective-permute-start.2) | collective-permute-done | bytes 393248 | tf_op jit(solution)/shard_map/ppermute | solution.py:316
  29.8 0.2 collective-permute-done.3.refs_6_
  30.0 2.0 %pick_rows.2 = bf16[16,5,8,768]{3,2,1,0:T(8,128)(2,1)} custom-call(s32[2]{0:T(128)S(1)} %pad_add_fusion.refs_0_.at_ref, s32[8,128]{1,0:T(8,128)S(1)} %bitcast.20, bf16[256,768]{1,0:T(8,128)(2,1)S(1)} %copy-done.8, bf16[256,768]{1,0:T(8,128)(2,1)S(1)} %collective-permute-done.refs_3_, bf16[256,768]{1,0:T(8,128)(2,1)S(1)} %collective-permute-done.1.refs_4_, ...), custom_call_target="tpu_custom_call" | custom-call | tf_op jit(solution)/shard_map/pick_rows/pallas_call | solution.py:51
  32.0 7.4 %all-to-all-start.1 = ((bf16[16,5,8,768]{3,2,1,0:T(8,128)(2,1)}), bf16[16,5,8,768]{3,2,1,0:T(8,128)(2,1)S(1)}, u32[]{:S(2)}, u32[]{:S(2)}) async-start(bf16[16,5,8,768]{3,2,1,0:T(8,128)(2,1)} %pick_rows.2), calls=%async_computation.1 | async-start | bytes 1966080 | tf_op jit(solution)/shard_map/all_to_all | solution.py:354
  39.4 1.5 %collective-permute-start.6 = (bf16[256,768]{1,0:T(8,128)(2,1)}, bf16[256,768]{1,0:T(8,128)(2,1)S(1)}, u32[]{:S(2)}, u32[]{:S(2)}) collective-permute-start(bf16[256,768]{1,0:T(8,128)(2,1)} %copy-done.9), channel_id=1, source_target_pairs={{0,2},{2,4},{4,6},{6,8},{8,10},{10,12},{12,14},{14,0},{1,3},{3,5},... | collective-permute-start | bytes 1179656 | tf_op jit(solution)/shard_map/ppermute | solution.py:316
  40.9 1.8 %collective-permute-start.7 = (bf16[256,768]{1,0:T(8,128)(2,1)}, bf16[256,768]{1,0:T(8,128)(2,1)S(1)}, u32[]{:S(2)}, u32[]{:S(2)}) collective-permute-start(bf16[256,768]{1,0:T(8,128)(2,1)} %copy-done.10), channel_id=1, source_target_pairs={{2,0},{4,2},{6,4},{8,6},{10,8},{12,10},{14,12},{0,14},{3,1},{5,3},... | collective-permute-start | bytes 1179656 | tf_op jit(solution)/shard_map/ppermute | solution.py:316
  42.7 8.3 %collective-permute-done.6.refs_0_.refs_2_ = bf16[256,768]{1,0:T(8,128)(2,1)S(1)} collective-permute-done((bf16[256,768]{1,0:T(8,128)(2,1)}, bf16[256,768]{1,0:T(8,128)(2,1)S(1)}, u32[]{:S(2)}, u32[]{:S(2)}) %collective-permute-start.6) | collective-permute-done | bytes 393248 | tf_op jit(solution)/shard_map/ppermute | solution.py:316
  51.0 0.6 collective-permute-done.7.refs_1_.refs_3_
  51.6 0.5 cut_halves.1
  52.1 2.7 %collective-permute-start.8 = (bf16[128,768]{1,0:T(8,128)(2,1)S(1)}, bf16[128,768]{1,0:T(8,128)(2,1)S(1)}, u32[]{:S(2)}, u32[]{:S(2)}) collective-permute-start(bf16[128,768]{1,0:T(8,128)(2,1)S(1)} %get-tuple-element.22), channel_id=1, source_target_pairs={{0,2},{2,4},{4,6},{6,8},{8,10},{10,12},{12,14},{14,0},{1,3},{3,5},... | collective-permute-start | bytes 589832 | tf_op jit(solution)/shard_map/ppermute | solution.py:316
  54.9 0.6 collective-permute-start.9
  55.4 3.6 %collective-permute-done.8.refs_4_ = bf16[128,768]{1,0:T(8,128)(2,1)S(1)} collective-permute-done((bf16[128,768]{1,0:T(8,128)(2,1)S(1)}, bf16[128,768]{1,0:T(8,128)(2,1)S(1)}, u32[]{:S(2)}, u32[]{:S(2)}) %collective-permute-start.8) | collective-permute-done | bytes 196640 | tf_op jit(solution)/shard_map/ppermute | solution.py:316
  59.1 1.5 %collective-permute-done.9.refs_5_ = bf16[128,768]{1,0:T(8,128)(2,1)S(1)} collective-permute-done((bf16[128,768]{1,0:T(8,128)(2,1)S(1)}, bf16[128,768]{1,0:T(8,128)(2,1)S(1)}, u32[]{:S(2)}, u32[]{:S(2)}) %collective-permute-start.9) | collective-permute-done | bytes 196640 | tf_op jit(solution)/shard_map/ppermute | solution.py:316
  60.5 0.9 pick_rows.3
  61.5 0.8 copy-done.5
  62.4 7.2 %all-to-all-start.2 = ((bf16[16,3,8,768]{3,2,1,0:T(8,128)(2,1)}), bf16[16,3,8,768]{3,2,1,0:T(8,128)(2,1)}, u32[]{:S(2)}, u32[]{:S(2)}) async-start(bf16[16,3,8,768]{3,2,1,0:T(8,128)(2,1)} %copy-done.5), calls=%async_computation.2 | async-start | bytes 1179648 | tf_op jit(solution)/shard_map/all_to_all | solution.py:354
  69.6 8.6 %all-to-all-done.2.refs_2_ = bf16[16,3,8,768]{3,2,1,0:T(8,128)(2,1)} async-done(((bf16[16,3,8,768]{3,2,1,0:T(8,128)(2,1)}), bf16[16,3,8,768]{3,2,1,0:T(8,128)(2,1)}, u32[]{:S(2)}, u32[]{:S(2)}) %all-to-all-start.2) | async-done | bytes 589856 | tf_op jit(solution)/shard_map/all_to_all | solution.py:354
  78.2 2.9 %shard_map.109.refs_1_ = f32[768,1024]{1,0:T(8,128)S(1)} custom-call(s32[2]{0:T(128)S(1)} %pad_add_fusion.refs_0_.at_ref, bf16[16,5,8,768]{3,2,1,0:T(8,128)(2,1)S(1)} %all-to-all-done.1.refs_1_, s32[8,128]{1,0:T(8,128)S(1)} %reshape.27.refs_2_.refs_3_, bf16[768,1024]{1,0:T(8,128)(2,1)S(1)} %copy-done.1), custom_call_target="tpu_custom_call" | custom-call | tf_op jit(solution)/shard_map/pallas_call | solution.py:141
  81.1 3.6 %shard_map.110.refs_1_ = f32[768,1024]{1,0:T(8,128)S(1)} custom-call(s32[2]{0:T(128)S(1)} %pad_add_fusion.refs_0_.at_ref, f32[768,1024]{1,0:T(8,128)S(1)} %shard_map.109.refs_1_, bf16[16,5,8,768]{3,2,1,0:T(8,128)(2,1)} %collective-permute-done.5.refs_2_, s32[8,128]{1,0:T(8,128)S(1)} %collective-permute-done.4.refs_3_, bf16[768,1024]{1,0:T(8,128)(2,1)S(1)} %copy-done.1), custom_call_target="tpu_custom_call" | custom-call | tf_op jit(solution)/shard_map/pallas_call | solution.py:141
  84.8 1.6 %copy-done.2 = f32[768,1024]{1,0:T(8,128)} copy-done((f32[768,1024]{1,0:T(8,128)}, f32[768,1024]{1,0:T(8,128)S(1)}, u32[]{:S(2)}) %copy-start.2) | copy-done | bytes 3145752
  86.4 3.9 %shard_map.111.refs_1_ = f32[768,1024]{1,0:T(8,128)S(1)} custom-call(s32[2]{0:T(128)S(1)} %pad_add_fusion.refs_0_.at_ref, f32[768,1024]{1,0:T(8,128)} %copy-done.2, bf16[16,3,8,768]{3,2,1,0:T(8,128)(2,1)} %all-to-all-done.2.refs_2_, s32[8,128]{1,0:T(8,128)S(1)} %reshape.27.refs_2_.refs_3_, bf16[768,1024]{1,0:T(8,128)(2,1)S(1)} %copy-done.1), custom_call_target="tpu_custom_call" | custom-call | tf_op jit(solution)/shard_map/pallas_call | solution.py:141
  90.4 2.6 %shard_map.112 = (f32[512,1024]{1,0:T(8,128)S(1)}, bf16[768,1024]{1,0:T(8,128)(2,1)S(1)}, bf16[256,1024]{1,0:T(8,128)(2,1)S(1)}) custom-call(s32[2]{0:T(128)S(1)} %pad_add_fusion.refs_0_.at_ref, f32[768,1024]{1,0:T(8,128)S(1)} %shard_map.111.refs_1_, bf16[16,3,8,768]{3,2,1,0:T(8,128)(2,1)S(1)} %collective-permute-done.10.refs_2_, ...), custom_call_target="tpu_custom_call" | custom-call | tf_op jit(solution)/shard_map/pallas_call | solution.py:141
  93.0 4.3 %collective-permute-start.11 = (bf16[256,1024]{1,0:T(8,128)(2,1)S(1)}, bf16[256,1024]{1,0:T(8,128)(2,1)S(1)}, u32[]{:S(2)}, u32[]{:S(2)}) collective-permute-start(bf16[256,1024]{1,0:T(8,128)(2,1)S(1)} %get-tuple-element.28), channel_id=1, source_target_pairs={{16,1},{32,17},{48,33},{64,49},{80,65},{96,81},{112,97},{128,113},... | collective-permute-start | bytes 1572872 | tf_op jit(solution)/shard_map/ppermute | solution.py:397
  97.3 5.1 %near_projections.1 = (bf16[512,1024]{1,0:T(8,128)(2,1)S(1)}, bf16[768,1024]{1,0:T(8,128)(2,1)S(1)}, bf16[1024,768]{1,0:T(8,128)(2,1)S(1)}) custom-call(s32[2]{0:T(128)S(1)} %pad_add_fusion.refs_0_.at_ref, bf16[768,1024]{1,0:T(8,128)(2,1)S(1)} %get-tuple-element.24.x_ref, bf16[1024,1024]{1,0:T(8,128)(2,1)S(1)} %copy-done.7, ...), custom_call_target="tpu_custom_call" | custom-call | tf_op jit(solution)/shard_map/near_projections/pallas_call | solution.py:172
  102.5 3.1 %collective-permute-done.11.far_ref = bf16[256,1024]{1,0:T(8,128)(2,1)S(1)} collective-permute-done((bf16[256,1024]{1,0:T(8,128)(2,1)S(1)}, bf16[256,1024]{1,0:T(8,128)(2,1)S(1)}, u32[]{:S(2)}, u32[]{:S(2)}) %collective-permute-start.11) | collective-permute-done | bytes 524320 | tf_op jit(solution)/shard_map/ppermute | solution.py:397
  105.6 12.4 %window_attention.1 = bf16[512,1024]{1,0:T(8,128)(2,1)} custom-call(bf16[512,1024]{1,0:T(8,128)(2,1)S(1)} %get-tuple-element.25.q_ref, bf16[768,1024]{1,0:T(8,128)(2,1)S(1)} %get-tuple-element.26.k_ref, bf16[1024,768]{1,0:T(8,128)(2,1)S(1)} %get-tuple-element.27.v_ref, bf16[256,1024]{1,0:T(8,128)(2,1)S(1)} %collective-permute-done.11.far_ref, ...), custom_call_target="tpu_custom_call" | custom-call | tf_op jit(solution)/shard_map/window_attention/pallas_call | solution.py:267
  (34 shorter events, 0.1 us)
Async XLA Ops:
  0.0 16.2 %copy-start = (bf16[256,64,16]{0,2,1:T(8,128)(2,1)S(1)}, bf16[256,64,16]{0,2,1:T(8,128)(2,1)}, u32[]{:S(2)}) copy-start(bf16[256,64,16]{0,2,1:T(8,128)(2,1)} %param.21) | copy-start | bytes 1572868
  0.0 30.0 %copy-start.8 = (bf16[256,768]{1,0:T(8,128)(2,1)S(1)}, bf16[256,768]{1,0:T(8,128)(2,1)}, u32[]{:S(2)}) copy-start(bf16[256,768]{1,0:T(8,128)(2,1)} %refs_2_.1) | copy-start | bytes 1179652
  0.0 16.7 %collective-permute-start = (bf16[256,768]{1,0:T(8,128)(2,1)}, bf16[256,768]{1,0:T(8,128)(2,1)S(1)}, u32[]{:S(2)}, u32[]{:S(2)}) collective-permute-start(bf16[256,768]{1,0:T(8,128)(2,1)} %refs_2_.1), channel_id=1, source_target_pairs={{0,2},{2,4},{4,6},{6,8},{8,10},{10,12},{12,14},{14,0},{1,3},{3,5},... | collective-permute-start | bytes 1179656 | tf_op jit(solution)/shard_map/ppermute | solution.py:316
  1.9 16.8 %collective-permute-start.1 = (bf16[256,768]{1,0:T(8,128)(2,1)}, bf16[256,768]{1,0:T(8,128)(2,1)S(1)}, u32[]{:S(2)}, u32[]{:S(2)}) collective-permute-start(bf16[256,768]{1,0:T(8,128)(2,1)} %refs_2_.1), channel_id=1, source_target_pairs={{2,0},{4,2},{6,4},{8,6},{10,8},{12,10},{14,12},{0,14},{3,1},{5,3},... | collective-permute-start | bytes 1179656 | tf_op jit(solution)/shard_map/ppermute | solution.py:316
  10.4 13.5 %all-to-all-start = ((s32[8,1,128]{2,1,0:T(1,128)}), s32[8,1,128]{2,1,0:T(1,128)S(1)}, u32[]{:S(2)}, u32[]{:S(2)}) async-start(s32[8,1,128]{2,1,0:T(1,128)} %bitcast.5), calls=%async_computation | async-start | bytes 8192 | tf_op jit(solution)/shard_map/all_to_all | solution.py:331
  16.2 15.8 %collective-permute-start.4 = (s32[8,128]{1,0:T(8,128)S(1)}, s32[8,128]{1,0:T(8,128)S(1)}, u32[]{:S(2)}, u32[]{:S(2)}) collective-permute-start(s32[8,128]{1,0:T(8,128)S(1)} %reshape.27.refs_2_.refs_3_), channel_id=1, source_target_pairs={{0,1},{1,0},{2,3},{3,2},{4,5},{5,4},{6,7},{7,6},{8,9},{9,8},{10,11... | collective-permute-start | bytes 12296 | tf_op jit(solution)/shard_map/ppermute | solution.py:330
  16.7 13.1 %collective-permute-start.2 = (bf16[256,768]{1,0:T(8,128)(2,1)S(1)}, bf16[256,768]{1,0:T(8,128)(2,1)S(1)}, u32[]{:S(2)}, u32[]{:S(2)}) collective-permute-start(bf16[256,768]{1,0:T(8,128)(2,1)S(1)} %collective-permute-done.refs_3_), channel_id=1, source_target_pairs={{0,2},{2,4},{4,6},{6,8},{8,10},{10,12},{12,14},{14,0},{1,3},{3,5},... | collective-permute-start | bytes 1179656 | tf_op jit(solution)/shard_map/ppermute | solution.py:316
  18.8 11.3 %collective-permute-start.3 = (bf16[256,768]{1,0:T(8,128)(2,1)S(1)}, bf16[256,768]{1,0:T(8,128)(2,1)S(1)}, u32[]{:S(2)}, u32[]{:S(2)}) collective-permute-start(bf16[256,768]{1,0:T(8,128)(2,1)S(1)} %collective-permute-done.1.refs_4_), channel_id=1, source_target_pairs={{2,0},{4,2},{6,4},{8,6},{10,8},{12,10},{14,12},{0,14},{3,1},{5,3},... | collective-permute-start | bytes 1179656 | tf_op jit(solution)/shard_map/ppermute | solution.py:316
  29.8 2.2 %copy-start.9 = (bf16[256,768]{1,0:T(8,128)(2,1)}, bf16[256,768]{1,0:T(8,128)(2,1)S(1)}, u32[]{:S(2)}) copy-start(bf16[256,768]{1,0:T(8,128)(2,1)S(1)} %collective-permute-done.2.refs_5_) | copy-start | bytes 1179652
  30.0 2.0 %copy-start.10 = (bf16[256,768]{1,0:T(8,128)(2,1)}, bf16[256,768]{1,0:T(8,128)(2,1)S(1)}, u32[]{:S(2)}) copy-start(bf16[256,768]{1,0:T(8,128)(2,1)S(1)} %collective-permute-done.3.refs_6_) | copy-start | bytes 1179652
  32.0 30.4 %all-to-all-start.1 = ((bf16[16,5,8,768]{3,2,1,0:T(8,128)(2,1)}), bf16[16,5,8,768]{3,2,1,0:T(8,128)(2,1)S(1)}, u32[]{:S(2)}, u32[]{:S(2)}) async-start(bf16[16,5,8,768]{3,2,1,0:T(8,128)(2,1)} %pick_rows.2), calls=%async_computation.1 | async-start | bytes 1966080 | tf_op jit(solution)/shard_map/all_to_all | solution.py:354
  39.4 38.8 %copy-start.1 = (bf16[768,1024]{1,0:T(8,128)(2,1)S(1)}, bf16[768,1024]{1,0:T(8,128)(2,1)}, u32[]{:S(2)}) copy-start(bf16[768,1024]{1,0:T(8,128)(2,1)} %refs_4_.5) | copy-start | bytes 4718596
  39.4 11.6 %collective-permute-start.6 = (bf16[256,768]{1,0:T(8,128)(2,1)}, bf16[256,768]{1,0:T(8,128)(2,1)S(1)}, u32[]{:S(2)}, u32[]{:S(2)}) collective-permute-start(bf16[256,768]{1,0:T(8,128)(2,1)} %copy-done.9), channel_id=1, source_target_pairs={{0,2},{2,4},{4,6},{6,8},{8,10},{10,12},{12,14},{14,0},{1,3},{3,5},... | collective-permute-start | bytes 1179656 | tf_op jit(solution)/shard_map/ppermute | solution.py:316
  40.9 10.7 %collective-permute-start.7 = (bf16[256,768]{1,0:T(8,128)(2,1)}, bf16[256,768]{1,0:T(8,128)(2,1)S(1)}, u32[]{:S(2)}, u32[]{:S(2)}) collective-permute-start(bf16[256,768]{1,0:T(8,128)(2,1)} %copy-done.10), channel_id=1, source_target_pairs={{2,0},{4,2},{6,4},{8,6},{10,8},{12,10},{14,12},{0,14},{3,1},{5,3},... | collective-permute-start | bytes 1179656 | tf_op jit(solution)/shard_map/ppermute | solution.py:316
  52.1 7.0 %collective-permute-start.8 = (bf16[128,768]{1,0:T(8,128)(2,1)S(1)}, bf16[128,768]{1,0:T(8,128)(2,1)S(1)}, u32[]{:S(2)}, u32[]{:S(2)}) collective-permute-start(bf16[128,768]{1,0:T(8,128)(2,1)S(1)} %get-tuple-element.22), channel_id=1, source_target_pairs={{0,2},{2,4},{4,6},{6,8},{8,10},{10,12},{12,14},{14,0},{1,3},{3,5},... | collective-permute-start | bytes 589832 | tf_op jit(solution)/shard_map/ppermute | solution.py:316
  54.9 5.7 %collective-permute-start.9 = (bf16[128,768]{1,0:T(8,128)(2,1)S(1)}, bf16[128,768]{1,0:T(8,128)(2,1)S(1)}, u32[]{:S(2)}, u32[]{:S(2)}) collective-permute-start(bf16[128,768]{1,0:T(8,128)(2,1)S(1)} %get-tuple-element.23), channel_id=1, source_target_pairs={{2,0},{4,2},{6,4},{8,6},{10,8},{12,10},{14,12},{0,14},{3,1},{5,3},... | collective-permute-start | bytes 589832 | tf_op jit(solution)/shard_map/ppermute | solution.py:316
  61.5 0.9 copy-start.5
  62.4 15.8 %all-to-all-start.2 = ((bf16[16,3,8,768]{3,2,1,0:T(8,128)(2,1)}), bf16[16,3,8,768]{3,2,1,0:T(8,128)(2,1)}, u32[]{:S(2)}, u32[]{:S(2)}) async-start(bf16[16,3,8,768]{3,2,1,0:T(8,128)(2,1)} %copy-done.5), calls=%async_computation.2 | async-start | bytes 1179648 | tf_op jit(solution)/shard_map/all_to_all | solution.py:354
  69.6 11.5 %collective-permute-start.5 = (bf16[16,5,8,768]{3,2,1,0:T(8,128)(2,1)S(1)}, bf16[16,5,8,768]{3,2,1,0:T(8,128)(2,1)}, u32[]{:S(2)}, u32[]{:S(2)}) collective-permute-start(bf16[16,5,8,768]{3,2,1,0:T(8,128)(2,1)S(1)} %all-to-all-done.1.refs_1_), channel_id=1, source_target_pairs={{0,1},{1,0},{2,3},{3,2},{4,5},{5,4},{6,7},{7,6},{8,9},{9,8},{10,11... | collective-permute-start | bytes 2949128 | tf_op jit(solution)/shard_map/ppermute | solution.py:355
  78.2 12.2 %collective-permute-start.10 = (bf16[16,3,8,768]{3,2,1,0:T(8,128)(2,1)}, bf16[16,3,8,768]{3,2,1,0:T(8,128)(2,1)S(1)}, u32[]{:S(2)}, u32[]{:S(2)}) collective-permute-start(bf16[16,3,8,768]{3,2,1,0:T(8,128)(2,1)} %all-to-all-done.2.refs_2_), channel_id=1, source_target_pairs={{0,1},{1,0},{2,3},{3,2},{4,5},{5,4},{6,7},{7,6},{8,9},{9,8},{10,11... | collective-permute-start | bytes 1769480 | tf_op jit(solution)/shard_map/ppermute | solution.py:355
  84.7 1.6 %copy-start.2 = (f32[768,1024]{1,0:T(8,128)}, f32[768,1024]{1,0:T(8,128)S(1)}, u32[]{:S(2)}) copy-start(f32[768,1024]{1,0:T(8,128)S(1)} %shard_map.110.refs_1_) | copy-start | bytes 9437188
  86.4 3.9 %copy-start.11 = (f32[1024]{0:T(1024)S(1)}, f32[1024]{0:T(1024)}, u32[]{:S(2)}) copy-start(f32[1024]{0:T(1024)} %param.16) | copy-start | bytes 12292
  86.4 10.9 %copy-start.7 = (bf16[1024,1024]{1,0:T(8,128)(2,1)S(1)}, bf16[1024,1024]{1,0:T(8,128)(2,1)}, u32[]{:S(2)}) copy-start(bf16[1024,1024]{1,0:T(8,128)(2,1)} %wq_ref.1) | copy-start | bytes 6291460
  90.3 7.0 %copy-start.3 = (bf16[1024,1024]{1,0:T(8,128)(2,1)S(1)}, bf16[1024,1024]{1,0:T(8,128)(2,1)}, u32[]{:S(2)}) copy-start(bf16[1024,1024]{1,0:T(8,128)(2,1)} %wk_ref.3) | copy-start | bytes 6291460
  90.3 7.0 %copy-start.4 = (bf16[1024,1024]{1,0:T(8,128)(2,1)S(1)}, bf16[1024,1024]{1,0:T(8,128)(2,1)}, u32[]{:S(2)}) copy-start(bf16[1024,1024]{1,0:T(8,128)(2,1)} %wv_ref.3) | copy-start | bytes 6291460
  93.0 12.6 %collective-permute-start.11 = (bf16[256,1024]{1,0:T(8,128)(2,1)S(1)}, bf16[256,1024]{1,0:T(8,128)(2,1)S(1)}, u32[]{:S(2)}, u32[]{:S(2)}) collective-permute-start(bf16[256,1024]{1,0:T(8,128)(2,1)S(1)} %get-tuple-element.28), channel_id=1, source_target_pairs={{16,1},{32,17},{48,33},{64,49},{80,65},{96,81},{112,97},{128,113},... | collective-permute-start | bytes 1572872 | tf_op jit(solution)/shard_map/ppermute | solution.py:397
  97.3 8.3 %copy-start.6 = (bf16[1024,1024]{1,0:T(8,128)(2,1)S(1)}, bf16[1024,1024]{1,0:T(8,128)(2,1)}, u32[]{:S(2)}) copy-start(bf16[1024,1024]{1,0:T(8,128)(2,1)} %wo_ref.1) | copy-start | bytes 6291460
